TPU v7x, 32 devices: a whole 2x2x4 slice. The times are simulated.
32 devices in a mesh: gx: 8 (over y, x, core), gy: 4 (over z).
Axes of the slice: x: 2, y: 2, z: 4, core: 2. Of those that a mesh axis runs over, the one named last changes fastest.
Arguments:
- east_flow: float32 [8, 1024, 2048], P(None, 'gx', 'gy'), may hold values from -36 to 36
- north_flow: float32 [8, 1024, 2048], P(None, 'gx', 'gy'), may hold values from -36 to 36
Outputs:
- stress: float32 [3, 8, 256, 512], P(None, None, 'gx', 'gy')
- library: float32 [48, 8, 256, 512], P(None, None, 'gx', 'gy')
All inputs are finite; a program needn't handle non-finite values.
Results may differ from a plain program's by a relative error of at most 0.0003.
Values sent between devices are 32-bit elements; how exact they have to be, the bound alone decides.
No kernel may reach another device: no remote copies, remote signals or barrier semaphores. Data moves between devices by JAX's collectives and lax.ppermute only.
A program may use at most 128 MiB of HBM per device.

v0:
```python
import jax
import jax.numpy as jnp
from jax import lax
from jax.sharding import PartitionSpec as P

spread_cells = 5.5


def with_halo(block, sides, width):
    for axis, dim in sides:
        count = lax.axis_size(axis)
        forward = [(i, i + 1) for i in range(count - 1)]
        forward.append((count - 1, 0))
        backward = [(target, source) for source, target in forward]
        low = lax.ppermute(
            lax.slice_in_dim(block, block.shape[dim] - width, None, axis=dim), axis, forward
        )
        high = lax.ppermute(lax.slice_in_dim(block, 0, width, axis=dim), axis, backward)
        block = jnp.concatenate([low, block, high], axis=dim)
    return block


def band_matrix(count_out, count_in):
    offsets = jnp.arange(33).astype(jnp.float32) - 16.0
    total = jnp.sum(jnp.exp(-0.5 * (offsets / spread_cells) ** 2))
    lag = jnp.arange(count_in)[None, :] - 4 * jnp.arange(count_out)[:, None]
    lagged = lag.astype(jnp.float32) - 16.0
    values = jnp.exp(-0.5 * (lagged / spread_cells) ** 2) / total
    return jnp.where((lag >= 0) & (lag <= 32), values, jnp.float32(0.0))


def first_form(plus_two, plus_one, minus_one, minus_two):
    return (8.0 * plus_one - plus_two - 8.0 * minus_one + minus_two) / 12.0


def second_form(plus_two, plus_one, centre, minus_one, minus_two):
    return (16.0 * plus_one - plus_two - 30.0 * centre + 16.0 * minus_one - minus_two) / 12.0


def moved(field, step, axis):
    count = field.shape[axis] - 4
    return lax.slice_in_dim(field, 2 + step, 2 + step + count, axis=axis)


def first_diff(field, axis):
    return first_form(
        moved(field, 2, axis), moved(field, 1, axis), moved(field, -1, axis), moved(field, -2, axis)
    )


def second_diff(field, axis):
    return second_form(
        moved(field, 2, axis),
        moved(field, 1, axis),
        moved(field, 0, axis),
        moved(field, -1, axis),
        moved(field, -2, axis),
    )


def build_library(
    east_mean,
    north_mean,
    grad_ux,
    grad_uy,
    grad_vx,
    grad_vy,
    curve_uxx,
    curve_uxy,
    curve_uyy,
    curve_vxx,
    curve_vxy,
    curve_vyy,
):
    vorticity = grad_vx - grad_uy
    features = [
        grad_ux,
        grad_uy,
        grad_vx,
        grad_vy,
        curve_uxx,
        curve_uxy,
        curve_uyy,
        curve_vxx,
        curve_vxy,
        curve_vyy,
        curve_vxx - curve_uxy,
        curve_vxy - curve_uyy,
    ]
    columns = []
    for feature in features:
        columns.append(feature)
        columns.append(east_mean * feature)
        columns.append(north_mean * feature)
        columns.append(vorticity * feature)
    return jnp.stack(columns, axis=0)


def with_products(pair):
    east, north = (pair[0], pair[1])
    return jnp.stack([east, north, east * east, east * north, north * north], axis=0)


def smooth_rows(fields, matrix):
    return jnp.einsum("cp,flpq->flcq", matrix, fields, precision=lax.Precision.HIGHEST)


def smooth_cols(fields, matrix):
    return jnp.einsum("flcq,dq->flcd", fields, matrix, precision=lax.Precision.HIGHEST)


def per_device(east_flow, north_flow):
    levels, count_x, count_y = east_flow.shape
    rows_matrix = band_matrix(count_x // 4, count_x + 32)
    cols_matrix = band_matrix(count_y // 4, count_y + 32)
    outgoing = jnp.stack([east_flow, north_flow], axis=0)
    arrived = with_halo(outgoing, (("gx", 2), ("gy", 3)), 16)
    widened = with_products(arrived)
    means = smooth_cols(smooth_rows(widened, rows_matrix), cols_matrix)
    east_mean, north_mean = (means[0], means[1])
    stress = jnp.stack(
        [
            means[2] - east_mean * east_mean,
            means[3] - east_mean * north_mean,
            means[4] - north_mean * north_mean,
        ],
        axis=0,
    )
    rim = with_halo(jnp.stack([east_mean, north_mean], axis=0), (("gx", 2), ("gy", 3)), 2)
    inner_x = lax.slice_in_dim(rim, 2, rim.shape[2] - 2, axis=2)
    along_x = first_diff(rim, 2)
    grad_x = lax.slice_in_dim(along_x, 2, along_x.shape[3] - 2, axis=3)
    grad_y = first_diff(inner_x, 3)
    curve_xx_full = second_diff(rim, 2)
    curve_xx = lax.slice_in_dim(curve_xx_full, 2, curve_xx_full.shape[3] - 2, axis=3)
    curve_yy = second_diff(inner_x, 3)
    curve_xy = first_diff(along_x, 3)
    library = build_library(
        east_mean,
        north_mean,
        grad_x[0],
        grad_y[0],
        grad_x[1],
        grad_y[1],
        curve_xx[0],
        curve_xy[0],
        curve_yy[0],
        curve_xx[1],
        curve_xy[1],
        curve_yy[1],
    )
    return (stress, library)


def solution(mesh):
    return jax.shard_map(
        per_device,
        mesh=mesh,
        in_specs=(P(None, "gx", "gy"), P(None, "gx", "gy")),
        out_specs=(P(None, None, "gx", "gy"), P(None, None, "gx", "gy")),
        check_vma=False,
    )
```

profile of v0, /device:TPU:0, one launch (start us, length us, event | category | flops | bytes accessed | tf_op | source)
XLA Modules:
  0.0 95.2 jit_solution(11491516774628069424)
XLA Ops:
  0.7 1.4 %pad_maximum_fusion.7 = (f32[2,8,16,512]{3,2,1,0:T(8,128)S(1)}, f32[2,8,16,512]{3,2,1,0:T(8,128)S(1)}) fusion(f32[1,8,128,512]{3,2,1,0:T(8,128)} %bitcast.15, f32[1,8,128,512]{3,2,1,0:T(8,128)} %bitcast.19), kind=kLoop, calls=%fused_computation.35 | loop fusion | flops 262144 | bytes 5242880 | tf_op jit(solution)/shard_map/slice | solution.py:16
  2.1 0.5 collective-permute-start
  2.6 2.9 %collective-permute-start.1 = (f32[2,8,16,512]{3,2,1,0:T(8,128)S(1)}, f32[2,8,16,512]{3,2,1,0:T(8,128)S(1)}, u32[]{:S(2)}, u32[]{:S(2)}) collective-permute-start(f32[2,8,16,512]{3,2,1,0:T(8,128)S(1)} %get-tuple-element.14), channel_id=1, source_target_pairs={{4,0},{8,4},{12,8},{16,12},{20,16},{24,20},{28,24},{0,28},{5,1},{9... | collective-permute-start | bytes 1572872 | tf_op jit(solution)/shard_map/ppermute | solution.py:18
  5.6 9.8 %collective-permute-done = f32[2,8,16,512]{3,2,1,0:T(8,128)S(1)} collective-permute-done((f32[2,8,16,512]{3,2,1,0:T(8,128)S(1)}, f32[2,8,16,512]{3,2,1,0:T(8,128)S(1)}, u32[]{:S(2)}, u32[]{:S(2)}) %collective-permute-start) | collective-permute-done | bytes 524320 | tf_op jit(solution)/shard_map/ppermute | solution.py:15
  15.4 1.5 %collective-permute-done.1 = f32[2,8,16,512]{3,2,1,0:T(8,128)S(1)} collective-permute-done((f32[2,8,16,512]{3,2,1,0:T(8,128)S(1)}, f32[2,8,16,512]{3,2,1,0:T(8,128)S(1)}, u32[]{:S(2)}, u32[]{:S(2)}) %collective-permute-start.1) | collective-permute-done | bytes 524320 | tf_op jit(solution)/shard_map/ppermute | solution.py:18
  16.9 1.5 %pad_maximum_fusion.4 = (f32[2,8,160,16]{3,2,1,0:T(8,128)}, f32[2,8,160,16]{3,2,1,0:T(8,128)S(1)}) fusion(f32[2,8,16,512]{3,2,1,0:T(8,128)S(1)} %collective-permute-done.1, f32[2,8,16,512]{3,2,1,0:T(8,128)S(1)} %collective-permute-done, f32[1,8,128,512]{3,2,1,0:T(8,128)S(1)} %bitcast.16, f32[1,8,128,512]{3,2,1,0:T(8,128)S(1)} %bitcast.21), kind=kLoop, calls=%fused_computation.27 | loop fusion | flops 245760 | bytes 5570560 | tf_op jit(solution)/shard_map/slice | solution.py:16
  18.4 2.6 %copy.6 = f32[2,8,160,16]{2,3,1,0:T(8,128)} copy(f32[2,8,160,16]{3,2,1,0:T(8,128)} %get-tuple-element.11) | data formatting | bytes 327680 | tf_op jit(solution)/shard_map/slice | solution.py:16
  21.0 1.6 %collective-permute-start.2 = (f32[2,8,160,16]{2,3,1,0:T(8,128)}, f32[2,8,160,16]{2,3,1,0:T(8,128)}, u32[]{:S(2)}, u32[]{:S(2)}) collective-permute-start(f32[2,8,160,16]{2,3,1,0:T(8,128)} %copy.6), channel_id=1, source_target_pairs={{0,1},{1,2},{2,3},{3,0},{4,5},{5,6},{6,7},{7,4},{8,9},{9,10},{10,1... | collective-permute-start | bytes 491528 | tf_op jit(solution)/shard_map/ppermute | solution.py:15
  22.6 1.3 %copy.7 = f32[2,8,160,16]{2,3,1,0:T(8,128)} copy(f32[2,8,160,16]{3,2,1,0:T(8,128)S(1)} %get-tuple-element.12) | data formatting | bytes 327680 | tf_op jit(solution)/shard_map/slice | solution.py:18
  23.9 2.2 %collective-permute-start.3 = (f32[2,8,160,16]{2,3,1,0:T(8,128)}, f32[2,8,160,16]{2,3,1,0:T(8,128)}, u32[]{:S(2)}, u32[]{:S(2)}) collective-permute-start(f32[2,8,160,16]{2,3,1,0:T(8,128)} %copy.7), channel_id=1, source_target_pairs={{1,0},{2,1},{3,2},{0,3},{5,4},{6,5},{7,6},{4,7},{9,8},{10,9},{11,1... | collective-permute-start | bytes 491528 | tf_op jit(solution)/shard_map/ppermute | solution.py:18
  26.1 0.7 exponential_reduce_fusion
  26.8 4.7 %collective-permute-done.2 = f32[2,8,160,16]{2,3,1,0:T(8,128)} collective-permute-done((f32[2,8,160,16]{2,3,1,0:T(8,128)}, f32[2,8,160,16]{2,3,1,0:T(8,128)}, u32[]{:S(2)}, u32[]{:S(2)}) %collective-permute-start.2) | collective-permute-done | bytes 163872 | tf_op jit(solution)/shard_map/ppermute | solution.py:15
  31.5 1.4 %copy.8 = f32[2,8,160,16]{3,2,1,0:T(8,128)S(1)} copy(f32[2,8,160,16]{2,3,1,0:T(8,128)} %collective-permute-done.2) | data formatting | bytes 327680 | tf_op jit(solution)/shard_map/ppermute | solution.py:15
  32.9 4.9 %collective-permute-done.3 = f32[2,8,160,16]{2,3,1,0:T(8,128)} collective-permute-done((f32[2,8,160,16]{2,3,1,0:T(8,128)}, f32[2,8,160,16]{2,3,1,0:T(8,128)}, u32[]{:S(2)}, u32[]{:S(2)}) %collective-permute-start.3) | collective-permute-done | bytes 163872 | tf_op jit(solution)/shard_map/ppermute | solution.py:18
  37.9 2.5 %copy.9 = f32[2,8,160,16]{3,2,1,0:T(8,128)} copy(f32[2,8,160,16]{2,3,1,0:T(8,128)} %collective-permute-done.3) | data formatting | bytes 327680 | tf_op jit(solution)/shard_map/ppermute | solution.py:18
  40.3 5.7 %pad_maximum_fusion = f32[2,8,160,544]{3,2,1,0:T(8,128)S(1)} fusion(f32[2,8,160,16]{3,2,1,0:T(8,128)} %copy.9, f32[2,8,16,512]{3,2,1,0:T(8,128)} %copy-done.6, f32[1,8,128,512]{3,2,1,0:T(8,128)S(1)} %bitcast.17, f32[1,8,128,512]{3,2,1,0:T(8,128)} %bitcast.20, f32[2,8,16,512]{3,2,1,0:T(8,128)} %copy-done.4, f32[2,8,160,16]{3,2,1,0:T(8,128)S(1)} %copy.8), kind=kLoop, calls=%fused_computation.18 | loop fusion | flops 6963200 | bytes 11141120 | tf_op jit(solution)/shard_map/concatenate | solution.py:19
  46.0 1.0 %slice_multiply_fusion.2 = (f32[1,8,160,544]{3,2,1,0:T(8,128)S(1)}, f32[1,8,160,544]{3,2,1,0:T(8,128)S(1)}, f32[1,8,160,544]{3,2,1,0:T(8,128)S(1)}) fusion(f32[2,8,160,544]{3,2,1,0:T(8,128)S(1)} %pad_maximum_fusion), kind=kLoop, calls=%fused_computation.23 | loop fusion | flops 2088960 | bytes 13926400 | tf_op jit(solution)/shard_map/mul | solution.py:101
  47.1 0.5 copy-done.2
  48.0 13.8 %fusion = f32[5,8,544,32]{2,3,1,0:T(8,128)S(1)} fusion(f32[1,8,160,544]{3,2,1,0:T(8,128)S(1)} %get-tuple-element.9, f32[1,8,160,544]{3,2,1,0:T(8,128)S(1)} %get-tuple-element.10, f32[1,8,160,544]{3,2,1,0:T(8,128)S(1)} %get-tuple-element.8, f32[2,8,160,16]{3,2,1,0:T(8,128)S(1)} %copy-done.3, f32[2,8,16,512]{3,2,1,0:T(8,128)} %copy-done.6, ...), kind=kOutput, calls=%fused_computation | convolution fusion | flops 1364843520 | bytes 16711812 | tf_op jit(solution)/shard_map/cp,flpq->flcq/dot_general | solution.py:105
  61.9 3.5 %fusion.18 = f32[5,8,32,128]{3,2,1,0:T(8,128)S(1)} fusion(f32[5,8,544,32]{2,3,1,0:T(8,128)S(1)} %fusion, f32[]{:T(128)} %exponential_reduce_fusion, s32[128]{0:T(128)S(1)} %iota_multiply_fusion), kind=kOutput, calls=%fused_computation.19 | convolution fusion | flops 1070313472 | bytes 3441156 | tf_op jit(solution)/shard_map/flcq,dq->flcd/dot_general | solution.py:109
  65.6 2.5 %collective-permute-start.5 = (f32[2,8,2,128]{3,2,1,0:T(2,128)S(1)}, f32[2,8,2,128]{3,2,1,0:T(2,128)S(1)}, u32[]{:S(2)}, u32[]{:S(2)}) collective-permute-start(f32[2,8,2,128]{3,2,1,0:T(2,128)S(1)} %get-tuple-element.22), channel_id=1, source_target_pairs={{4,0},{8,4},{12,8},{16,12},{20,16},{24,20},{28,24},{0,28},{5,1},{9... | collective-permute-start | bytes 49160 | tf_op jit(solution)/shard_map/ppermute | solution.py:18
  68.1 1.4 %collective-permute-done.4 = f32[2,8,2,128]{3,2,1,0:T(2,128)S(1)} collective-permute-done((f32[2,8,2,128]{3,2,1,0:T(2,128)S(1)}, f32[2,8,2,128]{3,2,1,0:T(2,128)S(1)}, u32[]{:S(2)}, u32[]{:S(2)}) %collective-permute-start.4) | collective-permute-done | bytes 16416 | tf_op jit(solution)/shard_map/ppermute | solution.py:15
  69.8 0.6 collective-permute-start.6
  70.4 3.3 %collective-permute-start.7 = (f32[2,8,36,2]{3,2,1,0:T(8,128)S(1)}, f32[2,8,36,2]{3,2,1,0:T(8,128)S(1)}, u32[]{:S(2)}, u32[]{:S(2)}) collective-permute-start(f32[2,8,36,2]{3,2,1,0:T(8,128)S(1)} %get-tuple-element.24), channel_id=1, source_target_pairs={{1,0},{2,1},{3,2},{0,3},{5,4},{6,5},{7,6},{4,7},{9,8},{10,9},{11,1... | collective-permute-start | bytes 13832 | tf_op jit(solution)/shard_map/ppermute | solution.py:18
  73.6 8.6 %collective-permute-done.6 = f32[2,8,36,2]{3,2,1,0:T(8,128)S(1)} collective-permute-done((f32[2,8,36,2]{3,2,1,0:T(8,128)S(1)}, f32[2,8,36,2]{3,2,1,0:T(8,128)S(1)}, u32[]{:S(2)}, u32[]{:S(2)}) %collective-permute-start.6) | collective-permute-done | bytes 4640 | tf_op jit(solution)/shard_map/ppermute | solution.py:15
  82.2 5.2 %collective-permute-done.7 = f32[2,8,36,2]{3,2,1,0:T(8,128)S(1)} collective-permute-done((f32[2,8,36,2]{3,2,1,0:T(8,128)S(1)}, f32[2,8,36,2]{3,2,1,0:T(8,128)S(1)}, u32[]{:S(2)}, u32[]{:S(2)}) %collective-permute-start.7) | collective-permute-done | bytes 4640 | tf_op jit(solution)/shard_map/ppermute | solution.py:18
  87.4 0.4 pad_maximum_fusion.5
  87.8 0.4 fusion.23
  88.8 0.6 add_multiply_fusion.1
  90.7 0.6 subtract_multiply_fusion
  92.4 0.8 pad_maximum_fusion.8
  93.2 2.0 %copy-done.7 = f32[48,8,32,128]{3,2,1,0:T(8,128)} copy-done((f32[48,8,32,128]{3,2,1,0:T(8,128)}, f32[48,8,32,128]{3,2,1,0:T(8,128)S(1)}, u32[]{:S(2)}) %copy-start.7) | copy-done | bytes 6291480
  (71 shorter events, 3.6 us)
Async XLA Ops:
  0.6 16.2 %copy-start.1 = (f32[8,128,512]{2,1,0:T(8,128)S(1)}, f32[8,128,512]{2,1,0:T(8,128)}, u32[]{:S(2)}) copy-start(f32[8,128,512]{2,1,0:T(8,128)} %param.2) | copy-start | bytes 6291460
  0.6 16.2 %copy-start = (f32[8,128,512]{2,1,0:T(8,128)S(1)}, f32[8,128,512]{2,1,0:T(8,128)}, u32[]{:S(2)}) copy-start(f32[8,128,512]{2,1,0:T(8,128)} %param.3) | copy-start | bytes 6291460
  2.1 13.3 %collective-permute-start = (f32[2,8,16,512]{3,2,1,0:T(8,128)S(1)}, f32[2,8,16,512]{3,2,1,0:T(8,128)S(1)}, u32[]{:S(2)}, u32[]{:S(2)}) collective-permute-start(f32[2,8,16,512]{3,2,1,0:T(8,128)S(1)} %get-tuple-element.13), channel_id=1, source_target_pairs={{0,4},{4,8},{8,12},{12,16},{16,20},{20,24},{24,28},{28,0},{1,5},{5... | collective-permute-start | bytes 1572872 | tf_op jit(solution)/shard_map/ppermute | solution.py:15
  2.6 14.2 %collective-permute-start.1 = (f32[2,8,16,512]{3,2,1,0:T(8,128)S(1)}, f32[2,8,16,512]{3,2,1,0:T(8,128)S(1)}, u32[]{:S(2)}, u32[]{:S(2)}) collective-permute-start(f32[2,8,16,512]{3,2,1,0:T(8,128)S(1)} %get-tuple-element.14), channel_id=1, source_target_pairs={{4,0},{8,4},{12,8},{16,12},{20,16},{24,20},{28,24},{0,28},{5,1},{9... | collective-permute-start | bytes 1572872 | tf_op jit(solution)/shard_map/ppermute | solution.py:18
  15.4 3.0 %copy-start.4 = (f32[2,8,16,512]{3,2,1,0:T(8,128)}, f32[2,8,16,512]{3,2,1,0:T(8,128)S(1)}, u32[]{:S(2)}) copy-start(f32[2,8,16,512]{3,2,1,0:T(8,128)S(1)} %collective-permute-done) | copy-start | bytes 1572868
  16.9 1.5 %copy-start.6 = (f32[2,8,16,512]{3,2,1,0:T(8,128)}, f32[2,8,16,512]{3,2,1,0:T(8,128)S(1)}, u32[]{:S(2)}) copy-start(f32[2,8,16,512]{3,2,1,0:T(8,128)S(1)} %collective-permute-done.1) | copy-start | bytes 1572868
  21.0 10.5 %collective-permute-start.2 = (f32[2,8,160,16]{2,3,1,0:T(8,128)}, f32[2,8,160,16]{2,3,1,0:T(8,128)}, u32[]{:S(2)}, u32[]{:S(2)}) collective-permute-start(f32[2,8,160,16]{2,3,1,0:T(8,128)} %copy.6), channel_id=1, source_target_pairs={{0,1},{1,2},{2,3},{3,0},{4,5},{5,6},{6,7},{7,4},{8,9},{9,10},{10,1... | collective-permute-start | bytes 491528 | tf_op jit(solution)/shard_map/ppermute | solution.py:15
  23.9 13.9 %collective-permute-start.3 = (f32[2,8,160,16]{2,3,1,0:T(8,128)}, f32[2,8,160,16]{2,3,1,0:T(8,128)}, u32[]{:S(2)}, u32[]{:S(2)}) collective-permute-start(f32[2,8,160,16]{2,3,1,0:T(8,128)} %copy.7), channel_id=1, source_target_pairs={{1,0},{2,1},{3,2},{0,3},{5,4},{6,5},{7,6},{4,7},{9,8},{10,9},{11,1... | collective-permute-start | bytes 491528 | tf_op jit(solution)/shard_map/ppermute | solution.py:18
  46.0 1.6 %copy-start.2 = (f32[8,128,512]{2,1,0:T(8,128)S(1)}, f32[8,128,512]{2,1,0:T(8,128)}, u32[]{:S(2)}) copy-start(f32[8,128,512]{2,1,0:T(8,128)} %param.2) | copy-start | bytes 6291460
  46.0 1.9 %copy-start.3 = (f32[2,8,160,16]{3,2,1,0:T(8,128)S(1)}, f32[2,8,160,16]{3,2,1,0:T(8,128)}, u32[]{:S(2)}) copy-start(f32[2,8,160,16]{3,2,1,0:T(8,128)} %copy.9) | copy-start | bytes 491524
  46.0 2.0 %copy-start.5 = (f32[2,8,16,512]{3,2,1,0:T(8,128)S(1)}, f32[2,8,16,512]{3,2,1,0:T(8,128)}, u32[]{:S(2)}) copy-start(f32[2,8,16,512]{3,2,1,0:T(8,128)} %copy-done.4) | copy-start | bytes 1572868
  65.4 4.1 %collective-permute-start.4 = (f32[2,8,2,128]{3,2,1,0:T(2,128)S(1)}, f32[2,8,2,128]{3,2,1,0:T(2,128)S(1)}, u32[]{:S(2)}, u32[]{:S(2)}) collective-permute-start(f32[2,8,2,128]{3,2,1,0:T(2,128)S(1)} %get-tuple-element.21), channel_id=1, source_target_pairs={{0,4},{4,8},{8,12},{12,16},{16,20},{20,24},{24,28},{28,0},{1,5},{5... | collective-permute-start | bytes 49160 | tf_op jit(solution)/shard_map/ppermute | solution.py:15
  65.6 4.0 %collective-permute-start.5 = (f32[2,8,2,128]{3,2,1,0:T(2,128)S(1)}, f32[2,8,2,128]{3,2,1,0:T(2,128)S(1)}, u32[]{:S(2)}, u32[]{:S(2)}) collective-permute-start(f32[2,8,2,128]{3,2,1,0:T(2,128)S(1)} %get-tuple-element.22), channel_id=1, source_target_pairs={{4,0},{8,4},{12,8},{16,12},{20,16},{24,20},{28,24},{0,28},{5,1},{9... | collective-permute-start | bytes 49160 | tf_op jit(solution)/shard_map/ppermute | solution.py:18
  69.8 12.5 %collective-permute-start.6 = (f32[2,8,36,2]{3,2,1,0:T(8,128)S(1)}, f32[2,8,36,2]{3,2,1,0:T(8,128)S(1)}, u32[]{:S(2)}, u32[]{:S(2)}) collective-permute-start(f32[2,8,36,2]{3,2,1,0:T(8,128)S(1)} %get-tuple-element.23), channel_id=1, source_target_pairs={{0,1},{1,2},{2,3},{3,0},{4,5},{5,6},{6,7},{7,4},{8,9},{9,10},{10,1... | collective-permute-start | bytes 13832 | tf_op jit(solution)/shard_map/ppermute | solution.py:15
  70.4 17.0 %collective-permute-start.7 = (f32[2,8,36,2]{3,2,1,0:T(8,128)S(1)}, f32[2,8,36,2]{3,2,1,0:T(8,128)S(1)}, u32[]{:S(2)}, u32[]{:S(2)}) collective-permute-start(f32[2,8,36,2]{3,2,1,0:T(8,128)S(1)} %get-tuple-element.24), channel_id=1, source_target_pairs={{1,0},{2,1},{3,2},{0,3},{5,4},{6,5},{7,6},{4,7},{9,8},{10,9},{11,1... | collective-permute-start | bytes 13832 | tf_op jit(solution)/shard_map/ppermute | solution.py:18
  92.4 2.8 %copy-start.7 = (f32[48,8,32,128]{3,2,1,0:T(8,128)}, f32[48,8,32,128]{3,2,1,0:T(8,128)S(1)}, u32[]{:S(2)}) copy-start(f32[48,8,32,128]{3,2,1,0:T(8,128)S(1)} %multiply_dynamic-update-slice_fusion) | copy-start | bytes 18874372
where the time goes:
time: 95.5 us; the launch traced here: 95.2 us
  waiting for transfers between devices  36.2 us (38%)
  matrix products  17.3 us (18%)
  other arithmetic  15.4 us (16%)
  starting transfers between devices  13.9 us (15%)
  local copies, waits for them, and re-layouts  11.3 us (12%)
  between operations  1.1 us (1%)
    ppermute x4, waiting for transfers between devices, with_halo(): lax.ppermute(lax.slice_in_dim(block, block.shape[dim] - width, None, axis...  24.6 us
    dot_general x1, matrix products, smooth_rows(): jnp.einsum('cp,flpq->flcq', matrix, fields, precision=lax.Precision.HIGHEST)  13.8 us
    ppermute x4, waiting for transfers between devices, with_halo(): lax.ppermute(lax.slice_in_dim(block, 0, width, axis=dim), axis, backward)  11.6 us
    ppermute x4, starting transfers between devices, with_halo(): lax.ppermute(lax.slice_in_dim(block, 0, width, axis=dim), axis, backward)  10.9 us
    concatenate x3, other arithmetic, with_halo(): block = jnp.concatenate([low, block, high], axis=dim)  6.09 us
    dot_general x1, matrix products, smooth_cols(): jnp.einsum('flcq,dq->flcd', fields, matrix, precision=lax.Precision.HIGHEST)  3.54 us
    unnamed x26, local copies, waits for them, and re-layouts  3.43 us
    slice x2, other arithmetic, with_halo(): lax.slice_in_dim(block, block.shape[dim] - width, None, axis=dim)  2.98 us
  transfers between devices with their start and end apart: 8, of which 7 were waited for; matrix products, arithmetic and copies ran while one was open for 4% of the time, Pallas kernels for 0%

commit v1 on v0

v1 whole, which is shorter than its diff:
```python
import functools

import jax
import jax.numpy as jnp
import numpy as np
from jax import lax
from jax.experimental import pallas as pl
from jax.experimental.pallas import tpu as pltpu
from jax.sharding import PartitionSpec as P

spread_cells = 5.5
REACH = 16
STEP = 4
EXT = REACH // STEP
RIM = 2
WIDE = EXT + RIM
EDGE = 32
HALF = 64
MSG = 24
F32, BF16 = jnp.float32, jnp.bfloat16


def taps(cells, count_in):
    offsets = np.arange(2 * REACH + 1) - REACH
    bumps = np.exp(-0.5 * (offsets / spread_cells) ** 2)
    lag = np.arange(count_in)[None, :] - STEP * np.asarray(cells)[:, None]
    inside = np.abs(lag) <= REACH
    return np.where(inside, np.exp(-0.5 * (lag / spread_cells) ** 2), 0.0) / bumps.sum()


def pieces(values):
    high = values.astype(BF16)
    low = (values - high.astype(np.float64)).astype(BF16)
    return high, low


def left_operand(rows):
    high, low = pieces(rows)
    return np.concatenate(
        [np.concatenate([high, high], 1), np.concatenate([low, np.zeros_like(low)], 1)], 0
    )


def message_rows(count_x):
    coarse = count_x // STEP
    low_wide = list(range(-EXT, RIM))
    high_wide = list(range(coarse - RIM, coarse + EXT))
    low_short = list(range(-EXT, 0))
    high_short = list(range(coarse, coarse + EXT))

    def rows(cells):
        full = taps(cells, count_x)
        return np.concatenate([full[:, :EDGE], full[:, count_x - EDGE :]], 1)

    sides = {"low": (rows(low_wide), rows(low_short)), "high": (rows(high_wide), rows(high_short))}

    def placed(at, part):
        block = np.zeros((8, 2 * EDGE))
        block[at : at + part.shape[0]] = part
        return block

    both = {"wide": [], "uu": [], "uv": [], "vv": []}
    for first, second in (("high", "low"), ("low", "high")):
        wide = np.concatenate([placed(0, sides[s][0]) for s in (first, second)], 0)
        uu = np.concatenate([placed(0, sides[s][1]) for s in (first, second)], 0)
        uv = np.concatenate([placed(4, sides[s][1]) for s in (first, second)], 0)
        vv = np.concatenate(
            [placed(6, sides[s][1][:2]) for s in (first, second)]
            + [placed(6, sides[s][1][2:]) for s in (first, second)],
            0,
        )
        for name, value in (("wide", wide), ("uu", uu), ("uv", uv), ("vv", vv)):
            both[name].append(left_operand(value))
    return tuple(np.stack(both[name]) for name in ("wide", "uu", "uv", "vv"))


def column_weights(count_y):
    coarse = count_y // STEP
    own = taps(range(coarse), count_y).T
    strips = np.zeros((count_y, 2 * HALF))
    strips[:, :WIDE] = taps(range(-EXT, RIM), count_y).T
    strips[:, HALF : HALF + WIDE] = taps(range(coarse - RIM, coarse + EXT), count_y).T
    return pieces(np.concatenate([own, strips], 1))


def split(values):
    high = values.astype(BF16)
    return high, (values - high.astype(F32)).astype(BF16)


def row_sums(left, field):
    high, low = split(field)
    both = jnp.dot(left, jnp.concatenate([high, low], 0), preferred_element_type=F32)
    half = both.shape[0] // 2
    return both[:half] + both[half:]


def column_sums(rows, w_high, w_low):
    high, low = split(rows)
    total = jnp.dot(high, w_high, preferred_element_type=F32)
    total = total + jnp.dot(high, w_low, preferred_element_type=F32)
    return total + jnp.dot(low, w_high, preferred_element_type=F32)


def products(u, v):
    return u, v, u * u, u * v, v * v


def edge_kernel(block, ut, ub, vt, vb, wide, cuu, cuv, cvv, w_high, w_low, e_ref, o_ref):
    odd = lax.rem(lax.axis_index("gx"), 2)
    step = pl.program_id(0)
    levels = e_ref.shape[0] - 1

    @pl.when(step == 0)
    def _():
        e_ref[levels] = jnp.zeros(e_ref.shape[1:], F32)
        o_ref[levels] = jnp.zeros(o_ref.shape[1:], F32)

    gathered = []
    for q in range(block):
        u = jnp.concatenate([ut[q], ub[q]], 0)
        v = jnp.concatenate([vt[q], vb[q]], 0)
        _, _, uu, uv, vv = products(u, v)
        last = row_sums(cvv[odd], vv)
        gathered.append(row_sums(wide[odd], u) + last[:16])
        gathered.append(row_sums(wide[odd], v) + last[16:])
        gathered.append(row_sums(cuu[odd], uu) + row_sums(cuv[odd], uv))
    sums = column_sums(jnp.concatenate(gathered, 0), w_high[...], w_low[...])
    lanes = e_ref.shape[2]
    for q in range(block):
        level = step * block + q
        for place, ref in ((0, e_ref), (8, o_ref)):
            part = jnp.concatenate(
                [sums[48 * q + 16 * t + place : 48 * q + 16 * t + place + 8] for t in range(3)], 0
            )
            ref[level] = part[:, :lanes]
            ref[levels] += pltpu.roll(part[:, lanes:], WIDE * level, 1)


def own_kernel(block, u_ref, v_ref, c_ref, w_high, w_low, p_ref, s_ref):
    step = pl.program_id(0)

    @pl.when(step == 0)
    def _():
        s_ref[...] = jnp.zeros(s_ref.shape, F32)

    coarse, lanes = p_ref.shape[2:]
    for q in range(block):
        fields = products(u_ref[q], v_ref[q])
        rows = jnp.concatenate([row_sums(c_ref[...], f) for f in fields], 0)
        sums = column_sums(rows, w_high[...], w_low[...])
        for k in range(5):
            p_ref[q, k] = sums[coarse * k : coarse * (k + 1), :lanes]
        s_ref[...] += pltpu.roll(sums[:, lanes:], WIDE * (step * block + q), 1)


def low_and_high(odd, e, o):
    return jnp.where(odd == 0, o, e), jnp.where(odd == 0, e, o)


def add_rows(wide_refs, short_refs, own_low, own_high, got_low, got_high):
    for k, ref in enumerate(wide_refs):
        count = ref.shape[0]
        at = 8 * k
        ref[0:RIM] = own_low[at + EXT - RIM : at + EXT]
        ref[count - RIM : count] = own_high[at + RIM : at + 2 * RIM]
        ref[0:WIDE] = ref[0:WIDE] + got_low[at : at + WIDE]
        ref[count - WIDE : count] = ref[count - WIDE : count] + got_high[at : at + WIDE]
    for k, ref in enumerate(short_refs):
        count = ref.shape[0]
        if k < 2:
            at = 16 + EXT * k
            ref[0:EXT] = ref[0:EXT] + got_low[at : at + EXT]
            ref[count - EXT : count] = ref[count - EXT : count] + got_high[at : at + EXT]
        else:
            for h in range(2):
                at = 8 * h + WIDE
                ref[2 * h : 2 * h + 2] = ref[2 * h : 2 * h + 2] + got_low[at : at + 2]
                back = count - EXT + 2 * h
                ref[back : back + 2] = ref[back : back + 2] + got_high[at : at + 2]


def strip_kernel(s_ref, own_e, own_o, got_e, got_o, e_ref, o_ref, us, vs, uus, uvs, vvs):
    odd_x = lax.rem(lax.axis_index("gx"), 2)
    odd_y = lax.rem(lax.axis_index("gy"), 2)
    coarse = uus.shape[0]
    us[RIM : RIM + coarse] = s_ref[0:coarse]
    vs[RIM : RIM + coarse] = s_ref[coarse : 2 * coarse]
    uus[...] = s_ref[2 * coarse : 3 * coarse]
    uvs[...] = s_ref[3 * coarse : 4 * coarse]
    vvs[...] = s_ref[4 * coarse : 5 * coarse]
    own_low, own_high = low_and_high(odd_x, own_e[0], own_o[0])
    got_low, got_high = low_and_high(odd_x, got_e[0], got_o[0])
    add_rows((us, vs), (uus, uvs, vvs), own_low, own_high, got_low, got_high)
    rim_rows = us.shape[0]
    start = -(-rim_rows // 8) * 8
    pairs = (
        (0, us[...], vs[...]),
        (start, uus[...], uvs[...]),
        (start + coarse, vvs[0 : coarse // 2], vvs[coarse // 2 : coarse]),
    )
    for at, a, b in pairs:
        lane = lax.broadcasted_iota(jnp.int32, a.shape, 1)
        low = jnp.where(lane < HALF, a, pltpu.roll(b, HALF, 1))
        high = jnp.where(lane < HALF, pltpu.roll(a, HALF, 1), b)
        e_ref[at : at + a.shape[0]] = jnp.where(odd_y == 0, high, low)
        o_ref[at : at + a.shape[0]] = jnp.where(odd_y == 0, low, high)


def first_form(plus_two, plus_one, minus_one, minus_two):
    return (8.0 * plus_one - plus_two - 8.0 * minus_one + minus_two) * (1.0 / 12.0)


def second_form(plus_two, plus_one, centre, minus_one, minus_two):
    return (16.0 * plus_one - plus_two - 30.0 * centre + 16.0 * minus_one - minus_two) * (1.0 / 12.0)


def final_kernel(
    p_ref, xe_own, xo_own, xe_got, xo_got, ye_own, yo_own, ye_got, yo_got, st_ref, lib_ref,
    us, vs, uus, uvs, vvs, low_side, high_side, slopes,
):
    odd_x = lax.rem(lax.axis_index("gx"), 2)
    odd_y = lax.rem(lax.axis_index("gy"), 2)
    level = pl.program_id(0)
    coarse, lanes = p_ref.shape[2:]
    rim_rows = us.shape[0]

    @pl.when(level == 0)
    def _():
        own_low, own_high = low_and_high(odd_y, ye_own[...], yo_own[...])
        got_low, got_high = low_and_high(odd_y, ye_got[...], yo_got[...])
        place = lax.rem(lax.rem(lax.broadcasted_iota(jnp.int32, own_low.shape, 1), HALF), WIDE)
        back = pltpu.roll(own_low, lanes - RIM, 1)
        ahead = pltpu.roll(own_high, RIM, 1)
        low_side[...] = got_low + jnp.where(place < RIM, back, 0.0)
        high_side[...] = got_high + jnp.where(place >= EXT, ahead, 0.0)

    us[RIM : RIM + coarse] = p_ref[0, 0]
    vs[RIM : RIM + coarse] = p_ref[0, 1]
    for k, ref in enumerate((uus, uvs, vvs)):
        ref[...] = p_ref[0, 2 + k]
    own_low, own_high = low_and_high(odd_x, xe_own[0], xo_own[0])
    got_low, got_high = low_and_high(odd_x, xe_got[0], xo_got[0])
    add_rows((us, vs), (uus, uvs, vvs), own_low, own_high, got_low, got_high)

    shift = WIDE * level

    def sides(at, count, second):
        base = HALF if second else 0
        low = pltpu.roll(low_side[at : at + count], lanes - RIM - base - shift, 1)
        high = pltpu.roll(high_side[at : at + count], lanes - EXT - base - shift, 1)
        return low, high

    def joined(field, low, high):
        lane = lax.broadcasted_iota(jnp.int32, field.shape, 1)
        return field + jnp.where(lane < EXT, low, 0.0) + jnp.where(lane >= lanes - EXT, high, 0.0)

    means = []
    found = []
    for k, ref in enumerate((us, vs)):
        low, high = sides(0, rim_rows, k == 1)
        f = joined(ref[...], low, high)
        ref[...] = f
        lane = lax.broadcasted_iota(jnp.int32, f.shape, 1)
        plus_one = pltpu.roll(jnp.where(lane < 1, high, f), lanes - 1, 1)
        plus_two = pltpu.roll(jnp.where(lane < 2, high, f), lanes - 2, 1)
        minus_one = pltpu.roll(jnp.where(lane >= lanes - 1, low, f), 1, 1)
        minus_two = pltpu.roll(jnp.where(lane >= lanes - 2, low, f), 2, 1)
        slopes[...] = first_form(plus_two, plus_one, minus_one, minus_two)

        def row(source, by):
            return source[RIM + by : RIM + by + coarse]

        curve_y = second_form(plus_two, plus_one, f, minus_one, minus_two)[RIM : RIM + coarse]
        centre = row(ref, 0)
        shifted = [row(ref, by) for by in (2, 1, -1, -2)]
        grad_x = first_form(*shifted)
        curve_x = second_form(shifted[0], shifted[1], centre, shifted[2], shifted[3])
        grad_y = row(slopes, 0)
        cross = first_form(*[row(slopes, by) for by in (2, 1, -1, -2)])
        means.append(centre)
        found.append((grad_x, grad_y, curve_x, cross, curve_y))

    u, v = means
    start = -(-rim_rows // 8) * 8
    low, high = sides(start, coarse, False)
    st_ref[0, 0] = joined(uus[...], low, high) - u * u
    low, high = sides(start, coarse, True)
    st_ref[1, 0] = joined(uvs[...], low, high) - u * v
    for h in range(2):
        part = slice(coarse // 2 * h, coarse // 2 * (h + 1))
        low, high = sides(start + coarse, coarse // 2, h == 1)
        st_ref[2, 0, part] = joined(vvs[part], low, high) - v[part] * v[part]

    (ux, uy, uxx, uxy, uyy), (vx, vy, vxx, vxy, vyy) = found
    vorticity = vx - uy
    features = (ux, uy, vx, vy, uxx, uxy, uyy, vxx, vxy, vyy, vxx - uxy, vxy - uyy)
    for k, feature in enumerate(features):
        lib_ref[4 * k, 0] = feature
        lib_ref[4 * k + 1, 0] = u * feature
        lib_ref[4 * k + 2, 0] = v * feature
        lib_ref[4 * k + 3, 0] = vorticity * feature


def swapped(axis, even, odd):
    count = lax.axis_size(axis)
    assert count % 2 == 0
    pairs = [(i, i ^ 1) for i in range(count)]
    others = [(i, (i + 1) % count if i % 2 else (i - 1) % count) for i in range(count)]
    return lax.ppermute(even, axis, pairs), lax.ppermute(odd, axis, others)


def whole(shape):
    return pl.BlockSpec(shape, lambda *_: (0,) * len(shape))


def per_device(east_flow, north_flow):
    levels, count_x, count_y = east_flow.shape
    coarse, lanes = count_x // STEP, count_y // STEP
    assert lanes == 2 * HALF and WIDE * levels <= HALF and coarse % 16 == 0
    w_high, w_low = (jnp.asarray(w) for w in column_weights(count_y))
    edge_rows = tuple(jnp.asarray(c) for c in message_rows(count_x))
    own_rows = jnp.asarray(left_operand(taps(range(coarse), count_x)))
    shape = functools.partial(jax.ShapeDtypeStruct, dtype=F32)

    block = 2
    top = pl.BlockSpec((block, EDGE, count_y), lambda i: (i, 0, 0))
    bottom = pl.BlockSpec((block, EDGE, count_y), lambda i: (i, count_x // EDGE - 1, 0))
    message = (levels + 1, MSG, lanes)
    xe, xo = pl.pallas_call(
        functools.partial(edge_kernel, block),
        grid=(levels // block,),
        in_specs=[top, bottom, top, bottom]
        + [whole(c.shape) for c in edge_rows]
        + [whole(w_high.shape), whole(w_low.shape)],
        out_specs=[whole(message)] * 2,
        out_shape=[shape(message)] * 2,
        name="edge",
    )(east_flow, east_flow, north_flow, north_flow, *edge_rows, w_high, w_low)
    xe_got, xo_got = swapped("gx", xe, xo)

    block = 1
    fine = pl.BlockSpec((block, count_x, count_y), lambda i: (i, 0, 0))
    strip = (5 * coarse, lanes)
    partial_sums, strips = pl.pallas_call(
        functools.partial(own_kernel, block),
        grid=(levels // block,),
        in_specs=[fine, fine, whole(own_rows.shape), whole(w_high.shape), whole(w_low.shape)],
        out_specs=[pl.BlockSpec((block, 5, coarse, lanes), lambda i: (i, 0, 0, 0)), whole(strip)],
        out_shape=[shape((levels, 5, coarse, lanes)), shape(strip)],
        name="own",
    )(east_flow, north_flow, own_rows, w_high, w_low)

    rim_rows = coarse + 2 * RIM
    start = -(-rim_rows // 8) * 8
    side = (start + coarse + coarse // 2, lanes)
    rows = [pltpu.VMEM((rim_rows, lanes), F32)] * 2 + [pltpu.VMEM((coarse, lanes), F32)] * 3
    slab = pl.BlockSpec((1, MSG, lanes), lambda i: (levels, 0, 0))
    ye, yo = pl.pallas_call(
        strip_kernel,
        grid=(1,),
        in_specs=[whole(strip)] + [slab] * 4,
        out_specs=[whole(side)] * 2,
        out_shape=[shape(side)] * 2,
        scratch_shapes=rows,
        name="strips",
    )(strips, xe, xo, xe_got, xo_got)
    ye_got, yo_got = swapped("gy", ye, yo)

    one = pl.BlockSpec((1, MSG, lanes), lambda i: (i, 0, 0))
    stress, library = pl.pallas_call(
        final_kernel,
        grid=(levels,),
        in_specs=[pl.BlockSpec((1, 5, coarse, lanes), lambda i: (i, 0, 0, 0))] + [one] * 4 + [whole(side)] * 4,
        out_specs=[
            pl.BlockSpec((3, 1, coarse, lanes), lambda i: (0, i, 0, 0)),
            pl.BlockSpec((48, 1, coarse, lanes), lambda i: (0, i, 0, 0)),
        ],
        out_shape=[shape((3, levels, coarse, lanes)), shape((48, levels, coarse, lanes))],
        scratch_shapes=rows
        + [pltpu.VMEM(side, F32)] * 2
        + [pltpu.VMEM((rim_rows, lanes), F32)],
        name="final",
    )(partial_sums, xe, xo, xe_got, xo_got, ye, yo, ye_got, yo_got)
    return stress, library


def solution(mesh):
    return jax.shard_map(
        per_device,
        mesh=mesh,
        in_specs=(P(None, "gx", "gy"), P(None, "gx", "gy")),
        out_specs=(P(None, None, "gx", "gy"), P(None, None, "gx", "gy")),
        check_vma=False,
    )
```

time: 95.5 us -> 36.8 us (0.39)
  waiting for transfers between devices: 36.2 us -> 3.58 us
  Pallas kernels: 0 us -> 22.5 us
  matrix products: 17.3 us -> 0 us
  other arithmetic: 15.4 us -> 0 us
  local copies, waits for them, and re-layouts: 11.3 us -> 1.29 us
  starting transfers between devices: 13.9 us -> 8.09 us
    ppermute x8 -> x4, waiting for transfers between devices: 36.2 us -> 3.58 us  [swapped(): return (lax.ppermute(even, axis, pairs), lax.ppermute(odd, axis, others))]
    pallas_call x0 -> x4, Pallas kernels: none -> 22.5 us  [the longest x1 8.58 us: per_device(): pl.pallas_call(functools.partial(own_kernel, block), grid=(levels // bloc...]
    dot_general x2 -> x0, matrix products: 17.3 us -> none  [the longest x1 13.8 us: smooth_rows(): jnp.einsum('cp,flpq->flcq', matrix, fields, precision=lax.Precision.HIGHEST)]
    concatenate x3 -> x0, other arithmetic: 6.09 us -> none  [with_halo(): block = jnp.concatenate([low, block, high], axis=dim)]
    ppermute x8 -> x4, starting transfers between devices: 13.9 us -> 8.09 us  [swapped(): return (lax.ppermute(even, axis, pairs), lax.ppermute(odd, axis, others))]
    slice x4 -> x0, local copies, waits for them, and re-layouts: 4.03 us -> none  [the longest x3 2.75 us: with_halo(): lax.slice_in_dim(block, block.shape[dim] - width, None, axis=dim)]
    ppermute x2 -> x0, local copies, waits for them, and re-layouts: 3.85 us -> none  [the longest x1 2.46 us: with_halo(): lax.ppermute(lax.slice_in_dim(block, 0, width, axis=dim), axis, backward)]
    slice x2 -> x0, other arithmetic: 2.98 us -> none  [with_halo(): lax.slice_in_dim(block, block.shape[dim] - width, None, axis=dim)]
  transfers between devices with their start and end apart: 8 -> 4, of which waited for: 7 -> 2; matrix products, arithmetic and copies ran while one was open for 4% -> 0% of each run, Pallas kernels for 0% -> 24%
where the time goes in v1:
time: 36.8 us; the launch traced here: 36.1 us
  Pallas kernels  22.5 us (61%)
  starting transfers between devices  8.09 us (22%)
  waiting for transfers between devices  3.58 us (10%)
  local copies, waits for them, and re-layouts  1.29 us (4%)
  between operations  0.66 us (2%)
    pallas_call x1, Pallas kernels, per_device(): pl.pallas_call(functools.partial(own_kernel, block), grid=(levels // bloc...  8.58 us
    ppermute x4, starting transfers between devices, swapped(): return (lax.ppermute(even, axis, pairs), lax.ppermute(odd, axis, others))  8.09 us
    pallas_call x1, Pallas kernels, per_device(): pl.pallas_call(final_kernel, grid=(levels,), in_specs=[pl.BlockSpec((1, 5...  7.2 us
    pallas_call x1, Pallas kernels, per_device(): pl.pallas_call(functools.partial(edge_kernel, block), grid=(levels // blo...  5.05 us
    ppermute x4, waiting for transfers between devices, swapped(): return (lax.ppermute(even, axis, pairs), lax.ppermute(odd, axis, others))  3.58 us
    pallas_call x1, Pallas kernels, per_device(): pl.pallas_call(strip_kernel, grid=(1,), in_specs=[whole(strip)] + [slab]...  1.66 us
    unnamed x8, local copies, waits for them, and re-layouts  1.29 us
  transfers between devices with their start and end apart: 4, of which 2 were waited for; matrix products, arithmetic and copies ran while one was open for 0% of the time, Pallas kernels for 24%

profile of v1, /device:TPU:0, one launch (start us, length us, event | category | flops | bytes accessed | tf_op | source)
XLA Modules:
  0.0 36.1 jit_solution(542899285446652553)
XLA Ops:
  0.6 5.1 %edge.1 = (f32[9,24,128]{2,1,0:T(8,128)}, f32[9,24,128]{2,1,0:T(8,128)}) custom-call(f32[8,128,512]{2,1,0:T(8,128)} %ub.1, f32[8,128,512]{2,1,0:T(8,128)} %ub.1, f32[8,128,512]{2,1,0:T(8,128)} %vb.1, f32[8,128,512]{2,1,0:T(8,128)} %vb.1, bf16[2,32,128]{2,1,0:T(8,128)(2,1)} %constant.16.clone.wide, bf16[2,32,128]{2,1,0:T(8,128)(2,1)} %constant.17.clone.cuu, ...), custom_call_target="tpu_custom_call" | custom-call | tf_op jit(solution)/shard_map/edge/pallas_call | solution.py:330
  5.7 0.5 %collective-permute-start = (f32[9,24,128]{2,1,0:T(8,128)}, f32[9,24,128]{2,1,0:T(8,128)S(1)}, u32[]{:S(2)}, u32[]{:S(2)}) collective-permute-start(f32[9,24,128]{2,1,0:T(8,128)} %get-tuple-element.9.own_e.xe_own), channel_id=1, source_target_pairs={{0,4},{4,0},{8,12},{12,8},{16,20},{20,16},{24,28},{28,24},{1,5},{5... | collective-permute-start | bytes 331784 | tf_op jit(solution)/shard_map/ppermute | solution.py:310
  6.2 3.5 %collective-permute-start.1 = (f32[9,24,128]{2,1,0:T(8,128)}, f32[9,24,128]{2,1,0:T(8,128)S(1)}, u32[]{:S(2)}, u32[]{:S(2)}) collective-permute-start(f32[9,24,128]{2,1,0:T(8,128)} %get-tuple-element.10.own_o.xo_own), channel_id=1, source_target_pairs={{0,28},{4,8},{8,4},{12,16},{16,12},{20,24},{24,20},{28,0},{1,29},{... | collective-permute-start | bytes 331784 | tf_op jit(solution)/shard_map/ppermute | solution.py:310
  9.7 8.6 %own.1 = (f32[8,5,32,128]{3,2,1,0:T(8,128)}, f32[160,128]{1,0:T(8,128)}) custom-call(f32[8,128,512]{2,1,0:T(8,128)} %ub.1, f32[8,128,512]{2,1,0:T(8,128)} %vb.1, bf16[64,256]{1,0:T(8,128)(2,1)} %constant.20.clone.c_ref, bf16[512,256]{1,0:T(8,128)(2,1)} %constant.14.clone.w_high, bf16[512,256]{1,0:T(8,128)(2,1)} %constant.15.clone.w_low), custom_call_target="tpu_custom_call" | custom-call | tf_op jit(solution)/shard_map/own/pallas_call | solution.py:345
  18.3 0.0 collective-permute-done.got_e.xe_got
  18.3 0.0 copy-start
  18.3 0.0 collective-permute-done.1.got_o.xo_got
  18.3 0.0 copy-start.1
  18.3 0.6 %copy-done = f32[9,24,128]{2,1,0:T(8,128)} copy-done((f32[9,24,128]{2,1,0:T(8,128)}, f32[9,24,128]{2,1,0:T(8,128)S(1)}, u32[]{:S(2)}) %copy-start) | copy-done | bytes 110616
  18.9 0.1 copy-done.1
  19.0 1.7 %strips.1 = (f32[88,128]{1,0:T(8,128)}, f32[88,128]{1,0:T(8,128)}) custom-call(f32[160,128]{1,0:T(8,128)} %get-tuple-element.11.s_ref, f32[9,24,128]{2,1,0:T(8,128)} %get-tuple-element.9.own_e.xe_own, f32[9,24,128]{2,1,0:T(8,128)} %get-tuple-element.10.own_o.xo_own, f32[9,24,128]{2,1,0:T(8,128)} %copy-done, f32[9,24,128]{2,1,0:T(8,128)} %copy-done.1), custom_call_target="tpu_custom_call" | custom-call | tf_op jit(solution)/shard_map/strips/pallas_call | solution.py:359
  20.7 1.6 %collective-permute-start.2 = (f32[88,128]{1,0:T(8,128)}, f32[88,128]{1,0:T(8,128)S(1)}, u32[]{:S(2)}, u32[]{:S(2)}) collective-permute-start(f32[88,128]{1,0:T(8,128)} %get-tuple-element.12.ye_own), channel_id=1, source_target_pairs={{0,1},{1,0},{2,3},{3,2},{4,5},{5,4},{6,7},{7,6},{8,9},{9,8},{10,11... | collective-permute-start | bytes 135176 | tf_op jit(solution)/shard_map/ppermute | solution.py:310
  22.2 2.5 %collective-permute-start.3 = (f32[88,128]{1,0:T(8,128)}, f32[88,128]{1,0:T(8,128)S(1)}, u32[]{:S(2)}, u32[]{:S(2)}) collective-permute-start(f32[88,128]{1,0:T(8,128)} %get-tuple-element.13.yo_own), channel_id=1, source_target_pairs={{0,3},{1,2},{2,1},{3,0},{4,7},{5,6},{6,5},{7,4},{8,11},{9,10},{10,... | collective-permute-start | bytes 135176 | tf_op jit(solution)/shard_map/ppermute | solution.py:310
  24.7 0.2 collective-permute-done.2.ye_got
  24.9 0.0 copy-start.2
  24.9 3.4 %collective-permute-done.3.yo_got = f32[88,128]{1,0:T(8,128)S(1)} collective-permute-done((f32[88,128]{1,0:T(8,128)}, f32[88,128]{1,0:T(8,128)S(1)}, u32[]{:S(2)}, u32[]{:S(2)}) %collective-permute-start.3) | collective-permute-done | bytes 45088 | tf_op jit(solution)/shard_map/ppermute | solution.py:310
  28.3 0.0 copy-start.3
  28.3 0.0 copy-done.2
  28.3 0.6 %copy-done.3 = f32[88,128]{1,0:T(8,128)} copy-done((f32[88,128]{1,0:T(8,128)}, f32[88,128]{1,0:T(8,128)S(1)}, u32[]{:S(2)}) %copy-start.3) | copy-done | bytes 45080
  28.9 7.2 %final.1 = (f32[3,8,32,128]{3,2,1,0:T(8,128)}, f32[48,8,32,128]{3,2,1,0:T(8,128)}) custom-call(f32[8,5,32,128]{3,2,1,0:T(8,128)} %get-tuple-element.8.p_ref, f32[9,24,128]{2,1,0:T(8,128)} %get-tuple-element.9.own_e.xe_own, f32[9,24,128]{2,1,0:T(8,128)} %get-tuple-element.10.own_o.xo_own, f32[9,24,128]{2,1,0:T(8,128)} %copy-done, f32[9,24,128]{2,1,0:T(8,128)} %copy-done.1, ...), custom_call_target="tpu_custom_call" | custom-call | tf_op jit(solution)/shard_map/final/pallas_call | solution.py:371
Async XLA Ops:
  5.7 12.6 %collective-permute-start = (f32[9,24,128]{2,1,0:T(8,128)}, f32[9,24,128]{2,1,0:T(8,128)S(1)}, u32[]{:S(2)}, u32[]{:S(2)}) collective-permute-start(f32[9,24,128]{2,1,0:T(8,128)} %get-tuple-element.9.own_e.xe_own), channel_id=1, source_target_pairs={{0,4},{4,0},{8,12},{12,8},{16,20},{20,16},{24,28},{28,24},{1,5},{5... | collective-permute-start | bytes 331784 | tf_op jit(solution)/shard_map/ppermute | solution.py:310
  6.2 12.1 %collective-permute-start.1 = (f32[9,24,128]{2,1,0:T(8,128)}, f32[9,24,128]{2,1,0:T(8,128)S(1)}, u32[]{:S(2)}, u32[]{:S(2)}) collective-permute-start(f32[9,24,128]{2,1,0:T(8,128)} %get-tuple-element.10.own_o.xo_own), channel_id=1, source_target_pairs={{0,28},{4,8},{8,4},{12,16},{16,12},{20,24},{24,20},{28,0},{1,29},{... | collective-permute-start | bytes 331784 | tf_op jit(solution)/shard_map/ppermute | solution.py:310
  18.3 0.6 %copy-start = (f32[9,24,128]{2,1,0:T(8,128)}, f32[9,24,128]{2,1,0:T(8,128)S(1)}, u32[]{:S(2)}) copy-start(f32[9,24,128]{2,1,0:T(8,128)S(1)} %collective-permute-done.got_e.xe_got) | copy-start | bytes 331780
  18.3 0.7 %copy-start.1 = (f32[9,24,128]{2,1,0:T(8,128)}, f32[9,24,128]{2,1,0:T(8,128)S(1)}, u32[]{:S(2)}) copy-start(f32[9,24,128]{2,1,0:T(8,128)S(1)} %collective-permute-done.1.got_o.xo_got) | copy-start | bytes 331780
  20.7 4.3 %collective-permute-start.2 = (f32[88,128]{1,0:T(8,128)}, f32[88,128]{1,0:T(8,128)S(1)}, u32[]{:S(2)}, u32[]{:S(2)}) collective-permute-start(f32[88,128]{1,0:T(8,128)} %get-tuple-element.12.ye_own), channel_id=1, source_target_pairs={{0,1},{1,0},{2,3},{3,2},{4,5},{5,4},{6,7},{7,6},{8,9},{9,8},{10,11... | collective-permute-start | bytes 135176 | tf_op jit(solution)/shard_map/ppermute | solution.py:310
  22.2 6.1 %collective-permute-start.3 = (f32[88,128]{1,0:T(8,128)}, f32[88,128]{1,0:T(8,128)S(1)}, u32[]{:S(2)}, u32[]{:S(2)}) collective-permute-start(f32[88,128]{1,0:T(8,128)} %get-tuple-element.13.yo_own), channel_id=1, source_target_pairs={{0,3},{1,2},{2,1},{3,0},{4,7},{5,6},{6,5},{7,4},{8,11},{9,10},{10,... | collective-permute-start | bytes 135176 | tf_op jit(solution)/shard_map/ppermute | solution.py:310
  24.9 3.4 %copy-start.2 = (f32[88,128]{1,0:T(8,128)}, f32[88,128]{1,0:T(8,128)S(1)}, u32[]{:S(2)}) copy-start(f32[88,128]{1,0:T(8,128)S(1)} %collective-permute-done.2.ye_got) | copy-start | bytes 135172
  28.3 0.6 %copy-start.3 = (f32[88,128]{1,0:T(8,128)}, f32[88,128]{1,0:T(8,128)S(1)}, u32[]{:S(2)}) copy-start(f32[88,128]{1,0:T(8,128)S(1)} %collective-permute-done.3.yo_got) | copy-start | bytes 135172

commit v2 on v1

v2 whole, which is shorter than its diff:
```python
import functools

import jax
import jax.numpy as jnp
import numpy as np
from jax import lax
from jax.experimental import pallas as pl
from jax.experimental.pallas import tpu as pltpu
from jax.sharding import PartitionSpec as P

spread_cells = 5.5
REACH = 16
STEP = 4
EXT = REACH // STEP
RIM = 2
WIDE = EXT + RIM
EDGE = 32
HALF = 64
MSG = 24
F32, BF16 = jnp.float32, jnp.bfloat16
VMEM_BYTES = 24 << 20
EDGE_UNROLL, OWN_UNROLL, OWN_CHUNK, FINAL_UNROLL = 2, 2, 2, 1


def taps(cells, count_in):
    offsets = np.arange(2 * REACH + 1) - REACH
    bumps = np.exp(-0.5 * (offsets / spread_cells) ** 2)
    lag = np.arange(count_in)[None, :] - STEP * np.asarray(cells)[:, None]
    inside = np.abs(lag) <= REACH
    return np.where(inside, np.exp(-0.5 * (lag / spread_cells) ** 2), 0.0) / bumps.sum()


def pieces(values):
    high = values.astype(BF16)
    low = (values - high.astype(np.float64)).astype(BF16)
    return high, low


def left_operand(rows):
    high, low = pieces(rows)
    return np.concatenate(
        [np.concatenate([high, high], 1), np.concatenate([low, np.zeros_like(low)], 1)], 0
    )


def message_rows(count_x):
    coarse = count_x // STEP
    low_wide = list(range(-EXT, RIM))
    high_wide = list(range(coarse - RIM, coarse + EXT))
    low_short = list(range(-EXT, 0))
    high_short = list(range(coarse, coarse + EXT))

    def rows(cells):
        full = taps(cells, count_x)
        return np.concatenate([full[:, :EDGE], full[:, count_x - EDGE :]], 1)

    sides = {"low": (rows(low_wide), rows(low_short)), "high": (rows(high_wide), rows(high_short))}

    def placed(at, part):
        block = np.zeros((8, 2 * EDGE))
        block[at : at + part.shape[0]] = part
        return block

    both = {"wide": [], "uu": [], "uv": [], "vv": []}
    for first, second in (("high", "low"), ("low", "high")):
        wide = np.concatenate([placed(0, sides[s][0]) for s in (first, second)], 0)
        uu = np.concatenate([placed(0, sides[s][1]) for s in (first, second)], 0)
        uv = np.concatenate([placed(4, sides[s][1]) for s in (first, second)], 0)
        vv = np.concatenate(
            [placed(6, sides[s][1][:2]) for s in (first, second)]
            + [placed(6, sides[s][1][2:]) for s in (first, second)],
            0,
        )
        for name, value in (("wide", wide), ("uu", uu), ("uv", uv), ("vv", vv)):
            both[name].append(left_operand(value))
    return tuple(np.stack(both[name]) for name in ("wide", "uu", "uv", "vv"))


def column_weights(count_y):
    coarse = count_y // STEP
    own = taps(range(coarse), count_y).T
    strips = np.zeros((count_y, 2 * HALF))
    strips[:, :WIDE] = taps(range(-EXT, RIM), count_y).T
    strips[:, HALF : HALF + WIDE] = taps(range(coarse - RIM, coarse + EXT), count_y).T
    return pieces(np.concatenate([own, strips], 1))


def split(values):
    high = values.astype(BF16)
    return high, (values - high.astype(F32)).astype(BF16)


def row_sums(left, field):
    high, low = split(field)
    both = jnp.dot(left, jnp.concatenate([high, low], 0), preferred_element_type=F32)
    half = both.shape[0] // 2
    return both[:half] + both[half:]


def column_sums(high, low, w_high, w_low):
    total = jnp.dot(high, w_high, preferred_element_type=F32)
    total = total + jnp.dot(high, w_low, preferred_element_type=F32)
    return total + jnp.dot(low, w_high, preferred_element_type=F32)


def products(u, v):
    return u, v, u * u, u * v, v * v


def each(count, unroll, body):
    lax.fori_loop(0, count, lambda i, _: (body(i), None)[1], None, unroll=unroll)


def edge_kernel(
    u_hbm, v_hbm, *refs,
):
    consts, (e_ref, o_ref, u_ref, v_ref), kept = refs[:7], refs[7:11], refs[11:14]
    wide, cuu, cuv, cvv, x_high, x_low, sem, const_sem = refs[14:]
    w_high, w_low = kept[0], kept[1]
    odd = lax.rem(lax.axis_index("gx"), 2)
    levels, count_x = u_ref.shape[:2]

    def fine(level, part):
        source, held = ((u_hbm, u_ref), (v_hbm, v_ref))[part % 2]
        rows = (pl.ds(0, EDGE), pl.ds(count_x - EDGE, EDGE), pl.ds(EDGE, count_x - 2 * EDGE))[part // 2]
        return pltpu.make_async_copy(source.at[level, rows], held.at[level, rows], sem.at[part, level])

    copies = [
        pltpu.make_async_copy(source, held, const_sem.at[k])
        for k, (source, held) in enumerate(zip(consts, (wide, cuu, cuv, cvv) + kept))
    ]
    for part in range(4):
        fine(0, part).start()
    for copy in copies[:4]:
        copy.start()
    for level in range(1, levels):
        for part in range(4):
            fine(level, part).start()
    for copy in copies[4:]:
        copy.start()
    for level in range(levels):
        for part in range(4, 6):
            fine(level, part).start()
    for copy in copies[:4]:
        copy.wait()

    def rows_of(level):
        for part in range(4):
            fine(level, part).wait()
        u, v = (jnp.concatenate([r[level, :EDGE], r[level, count_x - EDGE :]], 0) for r in (u_ref, v_ref))
        _, _, uu, uv, vv = products(u, v)
        last = row_sums(cvv[odd], vv)
        sums = jnp.concatenate(
            [
                row_sums(wide[odd], u) + last[:16],
                row_sums(wide[odd], v) + last[16:],
                row_sums(cuu[odd], uu) + row_sums(cuv[odd], uv),
            ],
            0,
        )
        at = pl.ds(pl.multiple_of(level * 48, 16), 48)
        x_high[at], x_low[at] = split(sums)

    each(levels, EDGE_UNROLL, rows_of)
    for copy in copies[4:6]:
        copy.wait()
    sums = column_sums(x_high[...], x_low[...], w_high[...], w_low[...])
    lanes = e_ref.shape[2]
    for place, ref in ((0, e_ref), (8, o_ref)):
        strips = jnp.zeros((MSG, lanes), F32)
        for level in range(levels):
            part = jnp.concatenate(
                [sums[48 * level + 16 * t + place : 48 * level + 16 * t + place + 8] for t in range(3)], 0
            )
            ref[level] = part[:, :lanes]
            strips = strips + pltpu.roll(part[:, lanes:], WIDE * level, 1)
        ref[levels] = strips
    copies[6].wait()
    for level in range(levels):
        for part in range(4, 6):
            fine(level, part).wait()


def own_kernel(u_ref, v_ref, w_high, w_low, c_ref, p_ref, s_ref, x_high, x_low):
    levels = u_ref.shape[0]
    rows, lanes = s_ref.shape

    def rows_of(level):
        fields = products(u_ref[level], v_ref[level])
        sums = jnp.concatenate([row_sums(c_ref[...], f) for f in fields], 0)
        at = pl.ds(pl.multiple_of(level * rows, 16), rows)
        x_high[at], x_low[at] = split(sums)

    each(levels, OWN_UNROLL, rows_of)
    strips = jnp.zeros((rows, lanes), F32)
    for first in range(0, levels, OWN_CHUNK):
        at = slice(first * rows, (first + OWN_CHUNK) * rows)
        sums = column_sums(x_high[at], x_low[at], w_high[...], w_low[...])
        p_ref[at] = sums[:, :lanes]
        for level in range(first, first + OWN_CHUNK):
            part = sums[(level - first) * rows : (level - first + 1) * rows, lanes:]
            strips = strips + pltpu.roll(part, WIDE * level, 1)
    s_ref[...] = strips


def low_and_high(odd, e, o):
    return jnp.where(odd == 0, o, e), jnp.where(odd == 0, e, o)


def add_rows(wide_refs, short_refs, own_low, own_high, got_low, got_high):
    for k, ref in enumerate(wide_refs):
        count = ref.shape[0]
        at = 8 * k
        ref[0:RIM] = own_low[at + EXT - RIM : at + EXT]
        ref[count - RIM : count] = own_high[at + RIM : at + 2 * RIM]
        ref[0:WIDE] = ref[0:WIDE] + got_low[at : at + WIDE]
        ref[count - WIDE : count] = ref[count - WIDE : count] + got_high[at : at + WIDE]
    for k, ref in enumerate(short_refs):
        count = ref.shape[0]
        if k < 2:
            at = 16 + EXT * k
            ref[0:EXT] = ref[0:EXT] + got_low[at : at + EXT]
            ref[count - EXT : count] = ref[count - EXT : count] + got_high[at : at + EXT]
        else:
            for h in range(2):
                at = 8 * h + WIDE
                ref[2 * h : 2 * h + 2] = ref[2 * h : 2 * h + 2] + got_low[at : at + 2]
                back = count - EXT + 2 * h
                ref[back : back + 2] = ref[back : back + 2] + got_high[at : at + 2]


def strip_kernel(s_ref, own_e, own_o, got_e, got_o, e_ref, o_ref, us, vs, uus, uvs, vvs):
    odd_x = lax.rem(lax.axis_index("gx"), 2)
    odd_y = lax.rem(lax.axis_index("gy"), 2)
    coarse = uus.shape[0]
    us[RIM : RIM + coarse] = s_ref[0:coarse]
    vs[RIM : RIM + coarse] = s_ref[coarse : 2 * coarse]
    uus[...] = s_ref[2 * coarse : 3 * coarse]
    uvs[...] = s_ref[3 * coarse : 4 * coarse]
    vvs[...] = s_ref[4 * coarse : 5 * coarse]
    own_low, own_high = low_and_high(odd_x, own_e[own_e.shape[0] - 1], own_o[own_o.shape[0] - 1])
    got_low, got_high = low_and_high(odd_x, got_e[got_e.shape[0] - 1], got_o[got_o.shape[0] - 1])
    add_rows((us, vs), (uus, uvs, vvs), own_low, own_high, got_low, got_high)
    rim_rows = us.shape[0]
    start = -(-rim_rows // 8) * 8
    pairs = (
        (0, us[...], vs[...]),
        (start, uus[...], uvs[...]),
        (start + coarse, vvs[0 : coarse // 2], vvs[coarse // 2 : coarse]),
    )
    for at, a, b in pairs:
        lane = lax.broadcasted_iota(jnp.int32, a.shape, 1)
        low = jnp.where(lane < HALF, a, pltpu.roll(b, HALF, 1))
        high = jnp.where(lane < HALF, pltpu.roll(a, HALF, 1), b)
        e_ref[at : at + a.shape[0]] = jnp.where(odd_y == 0, high, low)
        o_ref[at : at + a.shape[0]] = jnp.where(odd_y == 0, low, high)


def first_form(plus_two, plus_one, minus_one, minus_two):
    return (8.0 * plus_one - plus_two - 8.0 * minus_one + minus_two) * (1.0 / 12.0)


def second_form(plus_two, plus_one, centre, minus_one, minus_two):
    return (16.0 * plus_one - plus_two - 30.0 * centre + 16.0 * minus_one - minus_two) * (1.0 / 12.0)


def final_kernel(
    p_ref, xe_own, xo_own, xe_got, xo_got, ye_own, yo_own, ye_got, yo_got, st_hbm, lib_hbm,
    us, vs, uus, uvs, vvs, low_side, high_side, slopes, st_ref, lib_ref, sem,
):
    odd_x = lax.rem(lax.axis_index("gx"), 2)
    odd_y = lax.rem(lax.axis_index("gy"), 2)
    levels, coarse, lanes = st_ref.shape[1:]
    rim_rows = us.shape[0]
    own_low, own_high = low_and_high(odd_y, ye_own[...], yo_own[...])
    got_low, got_high = low_and_high(odd_y, ye_got[...], yo_got[...])
    place = lax.rem(lax.rem(lax.broadcasted_iota(jnp.int32, own_low.shape, 1), HALF), WIDE)
    back = pltpu.roll(own_low, lanes - RIM, 1)
    ahead = pltpu.roll(own_high, RIM, 1)
    low_side[...] = got_low + jnp.where(place < RIM, back, 0.0)
    high_side[...] = got_high + jnp.where(place >= EXT, ahead, 0.0)

    def out(level):
        return (
            pltpu.make_async_copy(st_ref.at[:, level], st_hbm.at[:, level], sem.at[0, level]),
            pltpu.make_async_copy(lib_ref.at[:, level], lib_hbm.at[:, level], sem.at[1, level]),
        )

    def finish(level):
        def part_of(k):
            return p_ref[pl.ds(pl.multiple_of((5 * level + k) * coarse, 8), coarse)]

        us[RIM : RIM + coarse] = part_of(0)
        vs[RIM : RIM + coarse] = part_of(1)
        for k, ref in enumerate((uus, uvs, vvs)):
            ref[...] = part_of(2 + k)
        own_low, own_high = low_and_high(odd_x, xe_own[level], xo_own[level])
        got_low, got_high = low_and_high(odd_x, xe_got[level], xo_got[level])
        add_rows((us, vs), (uus, uvs, vvs), own_low, own_high, got_low, got_high)

        shift = WIDE * level

        def sides(at, count, second):
            base = HALF if second else 0
            low = pltpu.roll(low_side[at : at + count], lanes - RIM - base - shift, 1)
            high = pltpu.roll(high_side[at : at + count], lanes - EXT - base - shift, 1)
            return low, high

        def joined(field, low, high):
            lane = lax.broadcasted_iota(jnp.int32, field.shape, 1)
            return field + jnp.where(lane < EXT, low, 0.0) + jnp.where(lane >= lanes - EXT, high, 0.0)

        means = []
        found = []
        for k, ref in enumerate((us, vs)):
            low, high = sides(0, rim_rows, k == 1)
            f = joined(ref[...], low, high)
            ref[...] = f
            lane = lax.broadcasted_iota(jnp.int32, f.shape, 1)
            plus_one = pltpu.roll(jnp.where(lane < 1, high, f), lanes - 1, 1)
            plus_two = pltpu.roll(jnp.where(lane < 2, high, f), lanes - 2, 1)
            minus_one = pltpu.roll(jnp.where(lane >= lanes - 1, low, f), 1, 1)
            minus_two = pltpu.roll(jnp.where(lane >= lanes - 2, low, f), 2, 1)
            slopes[...] = first_form(plus_two, plus_one, minus_one, minus_two)

            def row(source, by):
                return source[RIM + by : RIM + by + coarse]

            curve_y = second_form(plus_two, plus_one, f, minus_one, minus_two)[RIM : RIM + coarse]
            centre = row(ref, 0)
            shifted = [row(ref, by) for by in (2, 1, -1, -2)]
            grad_x = first_form(*shifted)
            curve_x = second_form(shifted[0], shifted[1], centre, shifted[2], shifted[3])
            grad_y = row(slopes, 0)
            cross = first_form(*[row(slopes, by) for by in (2, 1, -1, -2)])
            means.append(centre)
            found.append((grad_x, grad_y, curve_x, cross, curve_y))

        u, v = means
        start = -(-rim_rows // 8) * 8
        low, high = sides(start, coarse, False)
        st_ref[0, level] = joined(uus[...], low, high) - u * u
        low, high = sides(start, coarse, True)
        st_ref[1, level] = joined(uvs[...], low, high) - u * v
        for h in range(2):
            part = slice(coarse // 2 * h, coarse // 2 * (h + 1))
            low, high = sides(start + coarse, coarse // 2, h == 1)
            st_ref[2, level, part] = joined(vvs[part], low, high) - v[part] * v[part]

        (ux, uy, uxx, uxy, uyy), (vx, vy, vxx, vxy, vyy) = found
        vorticity = vx - uy
        features = (ux, uy, vx, vy, uxx, uxy, uyy, vxx, vxy, vyy, vxx - uxy, vxy - uyy)
        for k, feature in enumerate(features):
            lib_ref[4 * k, level] = feature
            lib_ref[4 * k + 1, level] = u * feature
            lib_ref[4 * k + 2, level] = v * feature
            lib_ref[4 * k + 3, level] = vorticity * feature
        for copy in out(level):
            copy.start()

    each(levels, FINAL_UNROLL, finish)
    for level in range(levels):
        for copy in out(level):
            copy.wait()


def swapped(axis, even, odd):
    count = lax.axis_size(axis)
    assert count % 2 == 0
    pairs = [(i, i ^ 1) for i in range(count)]
    others = [(i, (i + 1) % count if i % 2 else (i - 1) % count) for i in range(count)]
    return lax.ppermute(even, axis, pairs), lax.ppermute(odd, axis, others)


def local_call(body, outs, scratch, name, *operands):
    in_vmem, in_hbm = pl.BlockSpec(memory_space=pltpu.VMEM), pl.BlockSpec(memory_space=pltpu.HBM)
    specs, arrays = [], []
    for operand, here in operands:
        specs.append(in_vmem if here else in_hbm)
        arrays.append(pltpu.with_memory_space_constraint(operand, pltpu.VMEM) if here else pltpu.with_memory_space_constraint(operand, pltpu.HBM))
    return pl.pallas_call(
        body,
        in_specs=specs,
        out_specs=[in_hbm if isinstance(o, jax.ShapeDtypeStruct) else in_vmem for o in outs],
        out_shape=outs,
        scratch_shapes=scratch,
        compiler_params=pltpu.CompilerParams(vmem_limit_bytes=VMEM_BYTES),
        name=name,
    )(*arrays)


def per_device(east_flow, north_flow):
    levels, count_x, count_y = east_flow.shape
    coarse, lanes = count_x // STEP, count_y // STEP
    assert lanes == 2 * HALF and WIDE * levels <= HALF and coarse % 16 == 0
    consts = message_rows(count_x) + column_weights(count_y) + (left_operand(taps(range(coarse), count_x)),)
    consts = [jnp.asarray(c) for c in consts]
    rim_rows = coarse + 2 * RIM
    start = -(-rim_rows // 8) * 8
    side = (start + coarse + coarse // 2, lanes)
    message = (levels + 1, MSG, lanes)
    held = [pltpu.VMEM(c.shape, BF16) for c in consts]
    f32 = functools.partial(pltpu.VMEM, dtype=F32)

    xe, xo, u, v, *kept = local_call(
        edge_kernel,
        [f32(message), f32(message), f32(east_flow.shape), f32(north_flow.shape)] + held[4:],
        held[:4]
        + [pltpu.VMEM((48 * levels, count_y), BF16)] * 2
        + [pltpu.SemaphoreType.DMA((6, levels)), pltpu.SemaphoreType.DMA((7,))],
        "edge",
        (east_flow, False),
        (north_flow, False),
        *[(c, False) for c in consts],
    )
    xe_got, xo_got = swapped("gx", xe, xo)
    partial_sums, strips = local_call(
        own_kernel,
        [f32((levels * 5 * coarse, lanes)), f32((5 * coarse, lanes))],
        [pltpu.VMEM((levels * 5 * coarse, count_y), BF16)] * 2,
        "own",
        *[(a, True) for a in (u, v, *kept)],
    )
    rows = [f32((rim_rows, lanes))] * 2 + [f32((coarse, lanes))] * 3
    along_x = [(a, True) for a in (xe, xo, xe_got, xo_got)]
    ye, yo = local_call(strip_kernel, [f32(side)] * 2, rows, "strips", (strips, True), *along_x)
    ye_got, yo_got = swapped("gy", ye, yo)
    outs = [jax.ShapeDtypeStruct((n, levels, coarse, lanes), F32) for n in (3, 48)]
    return local_call(
        final_kernel,
        outs,
        rows
        + [f32(side)] * 2
        + [f32((rim_rows, lanes))]
        + [f32(o.shape) for o in outs]
        + [pltpu.SemaphoreType.DMA((2, levels))],
        "final",
        (partial_sums, True),
        *along_x,
        *[(a, True) for a in (ye, yo, ye_got, yo_got)],
    )


def solution(mesh):
    return jax.shard_map(
        per_device,
        mesh=mesh,
        in_specs=(P(None, "gx", "gy"), P(None, "gx", "gy")),
        out_specs=(P(None, None, "gx", "gy"), P(None, None, "gx", "gy")),
        check_vma=False,
    )
```

time: 36.8 us -> 25 us (0.68); the launches traced: 36.1 us -> 24.8 us
  Pallas kernels: 22.5 us -> 12.6 us
  local copies, waits for them, and re-layouts: 1.29 us -> 0 us
    pallas_call x4, Pallas kernels: 22.5 us -> 12.6 us  [local_call(): pl.pallas_call(body, in_specs=specs, out_specs=[in_hbm if isinstance(o, j...]
    unnamed x8 -> x0, local copies, waits for them, and re-layouts: 1.29 us -> none
  transfers between devices with their start and end apart: 4 -> 4, of which waited for: 2 -> 1; matrix products, arithmetic and copies ran while one was open for 0% -> 0% of each run, Pallas kernels for 24% -> 17%
where the time goes in v2:
time: 25 us; the launch traced here: 24.8 us
  Pallas kernels  12.6 us (50%)
  starting transfers between devices  8.22 us (33%)
  waiting for transfers between devices  3.38 us (14%)
  between operations  0.67 us (3%)
    pallas_call x4, Pallas kernels, local_call(): pl.pallas_call(body, in_specs=specs, out_specs=[in_hbm if isinstance(o, j...  12.6 us
    ppermute x4, starting transfers between devices, swapped(): return (lax.ppermute(even, axis, pairs), lax.ppermute(odd, axis, others))  8.22 us
    ppermute x4, waiting for transfers between devices, swapped(): return (lax.ppermute(even, axis, pairs), lax.ppermute(odd, axis, others))  3.38 us
  transfers between devices with their start and end apart: 4, of which 1 were waited for; matrix products, arithmetic and copies ran while one was open for 0% of the time, Pallas kernels for 17%

profile of v2, /device:TPU:0, one launch (start us, length us, event | category | flops | bytes accessed | tf_op | source)
XLA Modules:
  0.0 24.8 jit_solution(13933709781935439796)
XLA Ops:
  0.6 5.0 %edge.1 = (f32[9,24,128]{2,1,0:T(8,128)S(1)}, f32[9,24,128]{2,1,0:T(8,128)S(1)}, f32[8,128,512]{2,1,0:T(8,128)S(1)}, f32[8,128,512]{2,1,0:T(8,128)S(1)}, bf16[51...) custom-call(f32[8,128,512]{2,1,0:T(8,128)} %u_hbm.1, f32[8,128,512]{2,1,0:T(8,128)} %v_hbm.1, ...), custom_call_target="tpu_custom_call" | custom-call | tf_op jit(solution)/shard_map/edge/pallas_call | solution.py:381
  5.6 0.6 %collective-permute-start = (f32[9,24,128]{2,1,0:T(8,128)S(1)}, f32[9,24,128]{2,1,0:T(8,128)S(1)}, u32[]{:S(2)}, u32[]{:S(2)}) collective-permute-start(f32[9,24,128]{2,1,0:T(8,128)S(1)} %get-tuple-element.19.own_e.xe_own), channel_id=1, source_target_pairs={{0,4},{4,0},{8,12},{12,8},{16,20},{20,16},{24,28},{28,24},{1,5},{5... | collective-permute-start | bytes 331784 | tf_op jit(solution)/shard_map/ppermute | solution.py:372
  6.2 3.5 %collective-permute-start.1 = (f32[9,24,128]{2,1,0:T(8,128)S(1)}, f32[9,24,128]{2,1,0:T(8,128)S(1)}, u32[]{:S(2)}, u32[]{:S(2)}) collective-permute-start(f32[9,24,128]{2,1,0:T(8,128)S(1)} %get-tuple-element.20.own_o.xo_own), channel_id=1, source_target_pairs={{0,28},{4,8},{8,4},{12,16},{16,12},{20,24},{24,20},{28,0},{1,29},{... | collective-permute-start | bytes 331784 | tf_op jit(solution)/shard_map/ppermute | solution.py:372
  9.7 4.2 %own.1 = (f32[1280,128]{1,0:T(8,128)S(1)}, f32[160,128]{1,0:T(8,128)S(1)}) custom-call(f32[8,128,512]{2,1,0:T(8,128)S(1)} %get-tuple-element.13.u_ref, f32[8,128,512]{2,1,0:T(8,128)S(1)} %get-tuple-element.14.v_ref, bf16[512,256]{1,0:T(8,128)(2,1)S(1)} %get-tuple-element.15.w_high, bf16[512,256]{1,0:T(8,128)(2,1)S(1)} %get-tuple-element.16.w_low, ...), custom_call_target="tpu_custom_call" | custom-call | tf_op jit(solution)/shard_map/own/pallas_call | solution.py:381
  14.0 0.0 collective-permute-done.got_e.xe_got
  14.0 0.0 collective-permute-done.1.got_o.xo_got
  14.0 0.1 strips.1
  14.1 1.6 %collective-permute-start.2 = (f32[88,128]{1,0:T(8,128)S(1)}, f32[88,128]{1,0:T(8,128)S(1)}, u32[]{:S(2)}, u32[]{:S(2)}) collective-permute-start(f32[88,128]{1,0:T(8,128)S(1)} %get-tuple-element.22.ye_own), channel_id=1, source_target_pairs={{0,1},{1,0},{2,3},{3,2},{4,5},{5,4},{6,7},{7,6},{8,9},{9,8},{10,11... | collective-permute-start | bytes 135176 | tf_op jit(solution)/shard_map/ppermute | solution.py:372
  15.7 2.5 %collective-permute-start.3 = (f32[88,128]{1,0:T(8,128)S(1)}, f32[88,128]{1,0:T(8,128)S(1)}, u32[]{:S(2)}, u32[]{:S(2)}) collective-permute-start(f32[88,128]{1,0:T(8,128)S(1)} %get-tuple-element.23.yo_own), channel_id=1, source_target_pairs={{0,3},{1,2},{2,1},{3,0},{4,7},{5,6},{6,5},{7,4},{8,11},{9,10},{10,... | collective-permute-start | bytes 135176 | tf_op jit(solution)/shard_map/ppermute | solution.py:372
  18.2 0.0 collective-permute-done.2.ye_got
  18.2 3.4 %collective-permute-done.3.yo_got = f32[88,128]{1,0:T(8,128)S(1)} collective-permute-done((f32[88,128]{1,0:T(8,128)S(1)}, f32[88,128]{1,0:T(8,128)S(1)}, u32[]{:S(2)}, u32[]{:S(2)}) %collective-permute-start.3) | collective-permute-done | bytes 45088 | tf_op jit(solution)/shard_map/ppermute | solution.py:372
  21.6 3.2 %final.1 = (f32[3,8,32,128]{3,2,1,0:T(8,128)}, f32[48,8,32,128]{3,2,1,0:T(8,128)}) custom-call(f32[1280,128]{1,0:T(8,128)S(1)} %get-tuple-element.18.p_ref, f32[9,24,128]{2,1,0:T(8,128)S(1)} %get-tuple-element.19.own_e.xe_own, f32[9,24,128]{2,1,0:T(8,128)S(1)} %get-tuple-element.20.own_o.xo_own, f32[9,24,128]{2,1,0:T(8,128)S(1)} %collective-permute-done.got_e.xe_got, ...), custom_call_target="tpu_custom_call" | custom-call | tf_op jit(solution)/shard_map/final/pallas_call | solution.py:381
Async XLA Ops:
  5.6 8.3 %collective-permute-start = (f32[9,24,128]{2,1,0:T(8,128)S(1)}, f32[9,24,128]{2,1,0:T(8,128)S(1)}, u32[]{:S(2)}, u32[]{:S(2)}) collective-permute-start(f32[9,24,128]{2,1,0:T(8,128)S(1)} %get-tuple-element.19.own_e.xe_own), channel_id=1, source_target_pairs={{0,4},{4,0},{8,12},{12,8},{16,20},{20,16},{24,28},{28,24},{1,5},{5... | collective-permute-start | bytes 331784 | tf_op jit(solution)/shard_map/ppermute | solution.py:372
  6.2 7.8 %collective-permute-start.1 = (f32[9,24,128]{2,1,0:T(8,128)S(1)}, f32[9,24,128]{2,1,0:T(8,128)S(1)}, u32[]{:S(2)}, u32[]{:S(2)}) collective-permute-start(f32[9,24,128]{2,1,0:T(8,128)S(1)} %get-tuple-element.20.own_o.xo_own), channel_id=1, source_target_pairs={{0,28},{4,8},{8,4},{12,16},{16,12},{20,24},{24,20},{28,0},{1,29},{... | collective-permute-start | bytes 331784 | tf_op jit(solution)/shard_map/ppermute | solution.py:372
  14.1 4.1 %collective-permute-start.2 = (f32[88,128]{1,0:T(8,128)S(1)}, f32[88,128]{1,0:T(8,128)S(1)}, u32[]{:S(2)}, u32[]{:S(2)}) collective-permute-start(f32[88,128]{1,0:T(8,128)S(1)} %get-tuple-element.22.ye_own), channel_id=1, source_target_pairs={{0,1},{1,0},{2,3},{3,2},{4,5},{5,4},{6,7},{7,6},{8,9},{9,8},{10,11... | collective-permute-start | bytes 135176 | tf_op jit(solution)/shard_map/ppermute | solution.py:372
  15.7 5.8 %collective-permute-start.3 = (f32[88,128]{1,0:T(8,128)S(1)}, f32[88,128]{1,0:T(8,128)S(1)}, u32[]{:S(2)}, u32[]{:S(2)}) collective-permute-start(f32[88,128]{1,0:T(8,128)S(1)} %get-tuple-element.23.yo_own), channel_id=1, source_target_pairs={{0,3},{1,2},{2,1},{3,0},{4,7},{5,6},{6,5},{7,4},{8,11},{9,10},{10,... | collective-permute-start | bytes 135176 | tf_op jit(solution)/shard_map/ppermute | solution.py:372

commit v3 on v2

--- a/solution.py
+++ b/solution.py
@@ -14,12 +14,14 @@
 EXT = REACH // STEP
 RIM = 2
 WIDE = EXT + RIM
-EDGE = 32
+EDGE = 24
+SHORT = 16
+SIDE = 128
 HALF = 64
 MSG = 24
 F32, BF16 = jnp.float32, jnp.bfloat16
 VMEM_BYTES = 24 << 20
-EDGE_UNROLL, OWN_UNROLL, OWN_CHUNK, FINAL_UNROLL = 2, 2, 2, 1
+SLAB_UNROLL, MAIN_UNROLL, OWN_UNROLL, FINAL_UNROLL = 2, 2, 4, 1
 
 
 def taps(cells, count_in):
@@ -36,44 +38,41 @@
     return high, low
 
 
-def left_operand(rows):
-    high, low = pieces(rows)
-    return np.concatenate(
-        [np.concatenate([high, high], 1), np.concatenate([low, np.zeros_like(low)], 1)], 0
-    )
+def left_operand(*sources):
+    tops, bottoms = [], []
+    for rows in sources:
+        high, low = pieces(rows)
+        tops += [high, high]
+        bottoms += [low, np.zeros_like(low)]
+    return np.concatenate([np.concatenate(tops, 1), np.concatenate(bottoms, 1)], 0)
 
 
 def message_rows(count_x):
     coarse = count_x // STEP
-    low_wide = list(range(-EXT, RIM))
-    high_wide = list(range(coarse - RIM, coarse + EXT))
-    low_short = list(range(-EXT, 0))
-    high_short = list(range(coarse, coarse + EXT))
-
-    def rows(cells):
+
+    def rows(cells, ends):
         full = taps(cells, count_x)
-        return np.concatenate([full[:, :EDGE], full[:, count_x - EDGE :]], 1)
-
-    sides = {"low": (rows(low_wide), rows(low_short)), "high": (rows(high_wide), rows(high_short))}
-
-    def placed(at, part):
-        block = np.zeros((8, 2 * EDGE))
-        block[at : at + part.shape[0]] = part
-        return block
-
-    both = {"wide": [], "uu": [], "uv": [], "vv": []}
-    for first, second in (("high", "low"), ("low", "high")):
-        wide = np.concatenate([placed(0, sides[s][0]) for s in (first, second)], 0)
-        uu = np.concatenate([placed(0, sides[s][1]) for s in (first, second)], 0)
-        uv = np.concatenate([placed(4, sides[s][1]) for s in (first, second)], 0)
-        vv = np.concatenate(
-            [placed(6, sides[s][1][:2]) for s in (first, second)]
-            + [placed(6, sides[s][1][2:]) for s in (first, second)],
-            0,
-        )
-        for name, value in (("wide", wide), ("uu", uu), ("uv", uv), ("vv", vv)):
-            both[name].append(left_operand(value))
-    return tuple(np.stack(both[name]) for name in ("wide", "uu", "uv", "vv"))
+        return np.concatenate([full[:, :ends], full[:, count_x - ends :]], 1)
+
+    wide = {"low": rows(range(-EXT, RIM), EDGE), "high": rows(range(coarse - RIM, coarse + EXT), EDGE)}
+    short = {"low": rows(range(-EXT, 0), SHORT), "high": rows(range(coarse, coarse + EXT), SHORT)}
+
+    def placed(at, parts):
+        blocks = []
+        for part in parts:
+            block = np.zeros((8, part.shape[1]))
+            block[at : at + part.shape[0]] = part
+            blocks.append(block)
+        return np.concatenate(blocks, 0)
+
+    three, two = [], []
+    for sides in (("high", "low"), ("low", "high")):
+        w = placed(0, [wide[s] for s in sides])
+        none = np.zeros_like(w)
+        vv = [placed(WIDE, [short[s][2 * h : 2 * h + 2] for s in sides]) for h in range(2)]
+        three.append(left_operand(np.concatenate([w, none]), np.concatenate([none, w]), np.concatenate(vv)))
+        two.append(left_operand(*[placed(EXT * h, [short[s] for s in sides]) for h in range(2)]))
+    return np.stack(three), np.stack(two)
 
 
 def column_weights(count_y):
@@ -82,7 +81,11 @@
     strips = np.zeros((count_y, 2 * HALF))
     strips[:, :WIDE] = taps(range(-EXT, RIM), count_y).T
     strips[:, HALF : HALF + WIDE] = taps(range(coarse - RIM, coarse + EXT), count_y).T
-    return pieces(np.concatenate([own, strips], 1))
+
+    def ends(w):
+        return np.concatenate([w[:SIDE], w[count_y - SIDE :]], 0)
+
+    return tuple(np.concatenate(pieces(w), 1) for w in (ends(strips), ends(own), own[SIDE : count_y - SIDE]))
 
 
 def split(values):
@@ -97,10 +100,10 @@
     return both[:half] + both[half:]
 
 
-def column_sums(high, low, w_high, w_low):
-    total = jnp.dot(high, w_high, preferred_element_type=F32)
-    total = total + jnp.dot(high, w_low, preferred_element_type=F32)
-    return total + jnp.dot(low, w_high, preferred_element_type=F32)
+def column_sums(high, low, weights):
+    count = weights.shape[1] // 2
+    both = jnp.dot(high, weights[...], preferred_element_type=F32)
+    return both[:, :count] + both[:, count:] + jnp.dot(low, weights[:, :count], preferred_element_type=F32)
 
 
 def products(u, v):
@@ -111,96 +114,149 @@
     lax.fori_loop(0, count, lambda i, _: (body(i), None)[1], None, unroll=unroll)
 
 
-def edge_kernel(
-    u_hbm, v_hbm, *refs,
+def message_sums(three, two, u, v):
+    us, vs = (jnp.concatenate([f[:SHORT], f[2 * EDGE - SHORT :]], 0) for f in (u, v))
+    first = jnp.concatenate([*split(u), *split(v), *split(vs * vs)], 0)
+    second = jnp.concatenate([*split(us * us), *split(us * vs)], 0)
+    first = jnp.dot(three, first, preferred_element_type=F32)
+    second = jnp.dot(two, second, preferred_element_type=F32)
+    return jnp.concatenate([first[:32] + first[32:], second[:16] + second[16:]], 0)
+
+
+def slab_kernel(
+    u_hbm, v_hbm, three_hbm, two_hbm, w_hbm, w_ends_hbm, w_rest_hbm, left_hbm,
+    e_ref, o_ref, x_high, x_low, three, two, weights, w_ends, w_rest, left,
+    u_ref, v_ref, sem, const_sem,
 ):
-    consts, (e_ref, o_ref, u_ref, v_ref), kept = refs[:7], refs[7:11], refs[11:14]
-    wide, cuu, cuv, cvv, x_high, x_low, sem, const_sem = refs[14:]
-    w_high, w_low = kept[0], kept[1]
+    odd = lax.rem(lax.axis_index("gx"), 2)
+    levels = u_ref.shape[0]
+    _, count_x, count_y = u_hbm.shape
+    parts = sem.shape[0]
+    batch = levels // parts
+
+    def loads(part):
+        some = pl.ds(part * batch, batch)
+        copies = []
+        for f, (source, held) in enumerate(((u_hbm, u_ref), (v_hbm, v_ref))):
+            for r in range(2):
+                for c in range(2):
+                    copies.append(
+                        pltpu.make_async_copy(
+                            source.at[
+                                some, pl.ds(r * (count_x - EDGE), EDGE), pl.ds(c * (count_y - SIDE), SIDE)
+                            ],
+                            held.at[some, pl.ds(r * EDGE, EDGE), pl.ds(c * SIDE, SIDE)],
+                            sem.at[part, 4 * f + 2 * r + c],
+                        )
+                    )
+        return copies
+
+    consts = [
+        pltpu.make_async_copy(source, held, const_sem.at[k])
+        for k, (source, held) in enumerate(
+            (
+                (three_hbm, three),
+                (two_hbm, two),
+                (w_hbm, weights),
+                (left_hbm, left),
+                (w_ends_hbm, w_ends),
+                (w_rest_hbm, w_rest),
+            )
+        )
+    ]
+    for copy in loads(0) + consts[:2]:
+        copy.start()
+    for part in range(1, parts):
+        for copy in loads(part):
+            copy.start()
+    for copy in consts[2:]:
+        copy.start()
+    for copy in consts[:2]:
+        copy.wait()
+    for part in range(parts):
+        for copy in loads(part):
+            copy.wait()
+
+        def rows_of(i, part=part):
+            level = part * batch + i
+            at = pl.ds(pl.multiple_of(level * 48, 16), 48)
+            x_high[at], x_low[at] = split(message_sums(three[odd], two[odd], u_ref[level], v_ref[level]))
+
+        each(batch, SLAB_UNROLL, rows_of)
+    consts[2].wait()
+    sums = column_sums(x_high[...], x_low[...], weights)
+    for place, ref in ((0, e_ref), (8, o_ref)):
+        strips = jnp.zeros(ref.shape, F32)
+        for level in range(levels):
+            strips = strips + pltpu.roll(message_of(sums, level, place), WIDE * level, 1)
+        ref[...] = strips
+    for copy in consts[3:]:
+        copy.wait()
+
+
+def message_of(sums, level, place):
+    return jnp.concatenate([sums[48 * level + 16 * t + place : 48 * level + 16 * t + place + 8] for t in range(3)], 0)
+
+
+def middle(ref):
+    count_y = ref.shape[-1]
+    return pl.ds(SIDE, count_y - 2 * SIDE)
+
+
+def main_kernel(u_ref, v_ref, three, two, ends_high, ends_low, w_ends, w_rest, e_ref, o_ref, x_high, x_low):
     odd = lax.rem(lax.axis_index("gx"), 2)
     levels, count_x = u_ref.shape[:2]
 
-    def fine(level, part):
-        source, held = ((u_hbm, u_ref), (v_hbm, v_ref))[part % 2]
-        rows = (pl.ds(0, EDGE), pl.ds(count_x - EDGE, EDGE), pl.ds(EDGE, count_x - 2 * EDGE))[part // 2]
-        return pltpu.make_async_copy(source.at[level, rows], held.at[level, rows], sem.at[part, level])
-
-    copies = [
-        pltpu.make_async_copy(source, held, const_sem.at[k])
-        for k, (source, held) in enumerate(zip(consts, (wide, cuu, cuv, cvv) + kept))
-    ]
-    for part in range(4):
-        fine(0, part).start()
-    for copy in copies[:4]:
-        copy.start()
-    for level in range(1, levels):
-        for part in range(4):
-            fine(level, part).start()
-    for copy in copies[4:]:
-        copy.start()
-    for level in range(levels):
-        for part in range(4, 6):
-            fine(level, part).start()
-    for copy in copies[:4]:
-        copy.wait()
-
     def rows_of(level):
-        for part in range(4):
-            fine(level, part).wait()
-        u, v = (jnp.concatenate([r[level, :EDGE], r[level, count_x - EDGE :]], 0) for r in (u_ref, v_ref))
-        _, _, uu, uv, vv = products(u, v)
-        last = row_sums(cvv[odd], vv)
-        sums = jnp.concatenate(
-            [
-                row_sums(wide[odd], u) + last[:16],
-                row_sums(wide[odd], v) + last[16:],
-                row_sums(cuu[odd], uu) + row_sums(cuv[odd], uv),
-            ],
-            0,
+        u, v = (
+            jnp.concatenate([r[level, :EDGE, middle(r)], r[level, count_x - EDGE :, middle(r)]], 0)
+            for r in (u_ref, v_ref)
         )
         at = pl.ds(pl.multiple_of(level * 48, 16), 48)
-        x_high[at], x_low[at] = split(sums)
-
-    each(levels, EDGE_UNROLL, rows_of)
-    for copy in copies[4:6]:
-        copy.wait()
-    sums = column_sums(x_high[...], x_low[...], w_high[...], w_low[...])
-    lanes = e_ref.shape[2]
+        x_high[at], x_low[at] = split(message_sums(three[odd], two[odd], u, v))
+
+    each(levels, MAIN_UNROLL, rows_of)
+    sums = column_sums(ends_high[...], ends_low[...], w_ends) + column_sums(x_high[...], x_low[...], w_rest)
     for place, ref in ((0, e_ref), (8, o_ref)):
-        strips = jnp.zeros((MSG, lanes), F32)
         for level in range(levels):
-            part = jnp.concatenate(
-                [sums[48 * level + 16 * t + place : 48 * level + 16 * t + place + 8] for t in range(3)], 0
-            )
-            ref[level] = part[:, :lanes]
-            strips = strips + pltpu.roll(part[:, lanes:], WIDE * level, 1)
-        ref[levels] = strips
-    copies[6].wait()
-    for level in range(levels):
-        for part in range(4, 6):
-            fine(level, part).wait()
-
-
-def own_kernel(u_ref, v_ref, w_high, w_low, c_ref, p_ref, s_ref, x_high, x_low):
-    levels = u_ref.shape[0]
+            ref[level] = message_of(sums, level, place)
+
+
+def own_rows_of(left, u, v):
+    return split(jnp.concatenate([row_sums(left, f) for f in products(u, v)], 0))
+
+
+def ends_kernel(u_ref, v_ref, left, weights, s_ref, x_high, x_low):
+    levels, _, count_y = u_ref.shape
     rows, lanes = s_ref.shape
 
     def rows_of(level):
-        fields = products(u_ref[level], v_ref[level])
-        sums = jnp.concatenate([row_sums(c_ref[...], f) for f in fields], 0)
+        u, v = (
+            jnp.concatenate([r[level, :, :SIDE], r[level, :, count_y - SIDE :]], 1) for r in (u_ref, v_ref)
+        )
         at = pl.ds(pl.multiple_of(level * rows, 16), rows)
-        x_high[at], x_low[at] = split(sums)
+        x_high[at], x_low[at] = own_rows_of(left[...], u, v)
 
     each(levels, OWN_UNROLL, rows_of)
     strips = jnp.zeros((rows, lanes), F32)
-    for first in range(0, levels, OWN_CHUNK):
-        at = slice(first * rows, (first + OWN_CHUNK) * rows)
-        sums = column_sums(x_high[at], x_low[at], w_high[...], w_low[...])
-        p_ref[at] = sums[:, :lanes]
-        for level in range(first, first + OWN_CHUNK):
-            part = sums[(level - first) * rows : (level - first + 1) * rows, lanes:]
-            strips = strips + pltpu.roll(part, WIDE * level, 1)
+    for level in range(levels):
+        at = slice(level * rows, (level + 1) * rows)
+        strips = strips + pltpu.roll(column_sums(x_high[at], x_low[at], weights), WIDE * level, 1)
     s_ref[...] = strips
+
+
+def own_kernel(u_ref, v_ref, left, ends_high, ends_low, w_ends, w_rest, p_ref, x_high, x_low):
+    levels = u_ref.shape[0]
+    rows = p_ref.shape[0] // levels
+
+    def rows_of(level):
+        at = pl.ds(pl.multiple_of(level * rows, 16), rows)
+        x_high[at], x_low[at] = own_rows_of(left[...], u_ref[level, :, middle(u_ref)], v_ref[level, :, middle(v_ref)])
+
+    each(levels, OWN_UNROLL, rows_of)
+    for level in range(0, levels, 2):
+        at = slice(level * rows, (level + 2) * rows)
+        p_ref[at] = column_sums(ends_high[at], ends_low[at], w_ends) + column_sums(x_high[at], x_low[at], w_rest)
 
 
 def low_and_high(odd, e, o):
@@ -238,8 +294,8 @@
     uus[...] = s_ref[2 * coarse : 3 * coarse]
     uvs[...] = s_ref[3 * coarse : 4 * coarse]
     vvs[...] = s_ref[4 * coarse : 5 * coarse]
-    own_low, own_high = low_and_high(odd_x, own_e[own_e.shape[0] - 1], own_o[own_o.shape[0] - 1])
-    got_low, got_high = low_and_high(odd_x, got_e[got_e.shape[0] - 1], got_o[got_o.shape[0] - 1])
+    own_low, own_high = low_and_high(odd_x, own_e[...], own_o[...])
+    got_low, got_high = low_and_high(odd_x, got_e[...], got_o[...])
     add_rows((us, vs), (uus, uvs, vvs), own_low, own_high, got_low, got_high)
     rim_rows = us.shape[0]
     start = -(-rim_rows // 8) * 8
@@ -372,7 +428,7 @@
     return lax.ppermute(even, axis, pairs), lax.ppermute(odd, axis, others)
 
 
-def local_call(body, outs, scratch, name, *operands):
+def local_call(body, outs, scratch, *operands):
     in_vmem, in_hbm = pl.BlockSpec(memory_space=pltpu.VMEM), pl.BlockSpec(memory_space=pltpu.HBM)
     specs, arrays = [], []
     for operand, here in operands:
@@ -385,46 +441,64 @@
         out_shape=outs,
         scratch_shapes=scratch,
         compiler_params=pltpu.CompilerParams(vmem_limit_bytes=VMEM_BYTES),
-        name=name,
     )(*arrays)
 
 
-def per_device(east_flow, north_flow):
+def in_order(east_flow, north_flow):
     levels, count_x, count_y = east_flow.shape
     coarse, lanes = count_x // STEP, count_y // STEP
     assert lanes == 2 * HALF and WIDE * levels <= HALF and coarse % 16 == 0
-    consts = message_rows(count_x) + column_weights(count_y) + (left_operand(taps(range(coarse), count_x)),)
-    consts = [jnp.asarray(c) for c in consts]
+    assert count_x >= 2 * EDGE and count_y > 2 * SIDE
+    three, two = (jnp.asarray(c) for c in message_rows(count_x))
+    w_strips, w_ends, w_rest = (jnp.asarray(c) for c in column_weights(count_y))
+    left = jnp.asarray(left_operand(taps(range(coarse), count_x)))
     rim_rows = coarse + 2 * RIM
     start = -(-rim_rows // 8) * 8
     side = (start + coarse + coarse // 2, lanes)
-    message = (levels + 1, MSG, lanes)
-    held = [pltpu.VMEM(c.shape, BF16) for c in consts]
-    f32 = functools.partial(pltpu.VMEM, dtype=F32)
-
-    xe, xo, u, v, *kept = local_call(
-        edge_kernel,
-        [f32(message), f32(message), f32(east_flow.shape), f32(north_flow.shape)] + held[4:],
-        held[:4]
-        + [pltpu.VMEM((48 * levels, count_y), BF16)] * 2
-        + [pltpu.SemaphoreType.DMA((6, levels)), pltpu.SemaphoreType.DMA((7,))],
-        "edge",
-        (east_flow, False),
-        (north_flow, False),
-        *[(c, False) for c in consts],
+    own_count = 5 * coarse
+    f32, bf16 = functools.partial(pltpu.VMEM, dtype=F32), functools.partial(pltpu.VMEM, dtype=BF16)
+
+    def held(*arrays):
+        return [(a, True) for a in arrays]
+
+    parts = 2
+    consts = (three, two, w_strips, w_ends, w_rest, left)
+    se, so, ends_high, ends_low, *kept = local_call(
+        slab_kernel,
+        [f32((MSG, lanes))] * 2 + [bf16((48 * levels, 2 * SIDE))] * 2 + [bf16(c.shape) for c in consts],
+        [f32((levels, 2 * EDGE, 2 * SIDE))] * 2
+        + [pltpu.SemaphoreType.DMA((parts, 8)), pltpu.SemaphoreType.DMA((len(consts),))],
+        *[(a, False) for a in (east_flow, north_flow) + consts],
+    )
+    message_ends = (ends_high, ends_low)
+    three, two, w_strips, w_ends, w_rest, left = kept
+    se_got, so_got = swapped("gx", se, so)
+    fine = held(east_flow, north_flow)
+    xe, xo = local_call(
+        main_kernel,
+        [f32((levels, MSG, lanes))] * 2,
+        [bf16((48 * levels, count_y - 2 * SIDE))] * 2,
+        *fine,
+        *held(three, two, *message_ends, w_ends, w_rest),
     )
     xe_got, xo_got = swapped("gx", xe, xo)
-    partial_sums, strips = local_call(
+    strips, *own_ends = local_call(
+        ends_kernel,
+        [f32((own_count, lanes))] + [bf16((own_count * levels, 2 * SIDE))] * 2,
+        [],
+        *fine,
+        *held(left, w_strips),
+    )
+    rows = [f32((rim_rows, lanes))] * 2 + [f32((coarse, lanes))] * 3
+    ye, yo = local_call(strip_kernel, [f32(side)] * 2, rows, *held(strips, se, so, se_got, so_got))
+    ye_got, yo_got = swapped("gy", ye, yo)
+    (partial_sums,) = local_call(
         own_kernel,
-        [f32((levels * 5 * coarse, lanes)), f32((5 * coarse, lanes))],
-        [pltpu.VMEM((levels * 5 * coarse, count_y), BF16)] * 2,
-        "own",
-        *[(a, True) for a in (u, v, *kept)],
-    )
-    rows = [f32((rim_rows, lanes))] * 2 + [f32((coarse, lanes))] * 3
-    along_x = [(a, True) for a in (xe, xo, xe_got, xo_got)]
-    ye, yo = local_call(strip_kernel, [f32(side)] * 2, rows, "strips", (strips, True), *along_x)
-    ye_got, yo_got = swapped("gy", ye, yo)
+        [f32((own_count * levels, lanes))],
+        [bf16((own_count * levels, count_y - 2 * SIDE))] * 2,
+        *fine,
+        *held(left, *own_ends, w_ends, w_rest),
+    )
     outs = [jax.ShapeDtypeStruct((n, levels, coarse, lanes), F32) for n in (3, 48)]
     return local_call(
         final_kernel,
@@ -434,16 +508,13 @@
         + [f32((rim_rows, lanes))]
         + [f32(o.shape) for o in outs]
         + [pltpu.SemaphoreType.DMA((2, levels))],
-        "final",
-        (partial_sums, True),
-        *along_x,
-        *[(a, True) for a in (ye, yo, ye_got, yo_got)],
+        *held(partial_sums, xe, xo, xe_got, xo_got, ye, yo, ye_got, yo_got),
     )
 
 
 def solution(mesh):
     return jax.shard_map(
-        per_device,
+        in_order,
         mesh=mesh,
         in_specs=(P(None, "gx", "gy"), P(None, "gx", "gy")),
         out_specs=(P(None, None, "gx", "gy"), P(None, None, "gx", "gy")),

time: 25 us -> 23.6 us (0.944)
  Pallas kernels: 12.6 us -> 11.1 us
  waiting for transfers between devices: 3.38 us -> 2.64 us
  starting transfers between devices: 8.22 us -> 8.87 us
    pallas_call x4 -> x6, Pallas kernels: 12.6 us -> 11.1 us  [local_call(): pl.pallas_call(body, in_specs=specs, out_specs=[in_hbm if isinstance(o, j...]
    ppermute x4 -> x6, waiting for transfers between devices: 3.38 us -> 2.64 us  [swapped(): return (lax.ppermute(even, axis, pairs), lax.ppermute(odd, axis, others))]
    ppermute x4 -> x6, starting transfers between devices: 8.22 us -> 8.87 us  [swapped(): return (lax.ppermute(even, axis, pairs), lax.ppermute(odd, axis, others))]
  transfers between devices with their start and end apart: 4 -> 6, of which waited for: 1 -> 2; matrix products, arithmetic and copies ran while one was open for 0% -> 0% of each run, Pallas kernels for 17% -> 18%
where the time goes in v3:
time: 23.6 us; the launch traced here: 23.4 us
  Pallas kernels  11.1 us (47%)
  starting transfers between devices  8.87 us (38%)
  waiting for transfers between devices  2.64 us (11%)
  between operations  0.71 us (3%)
    pallas_call x6, Pallas kernels, local_call(): pl.pallas_call(body, in_specs=specs, out_specs=[in_hbm if isinstance(o, j...  11.1 us
    ppermute x6, starting transfers between devices, swapped(): return (lax.ppermute(even, axis, pairs), lax.ppermute(odd, axis, others))  8.87 us
    ppermute x6, waiting for transfers between devices, swapped(): return (lax.ppermute(even, axis, pairs), lax.ppermute(odd, axis, others))  2.64 us
  transfers between devices with their start and end apart: 6, of which 2 were waited for; matrix products, arithmetic and copies ran while one was open for 0% of the time, Pallas kernels for 18%

profile of v3, /device:TPU:0, one launch (start us, length us, event | category | flops | bytes accessed | tf_op | source)
XLA Modules:
  0.0 23.4 jit_solution(9437382385506345113)
XLA Ops:
  0.6 0.0 copy-start.1
  0.6 0.0 copy-start
  0.6 2.5 %shard_map.95 = (f32[24,128]{1,0:T(8,128)S(1)}, f32[24,128]{1,0:T(8,128)S(1)}, bf16[384,256]{1,0:T(8,128)(2,1)S(1)}, bf16[384,256]{1,0:T(8,128)(2,1)S(1)}, bf16[...) custom-call(f32[8,128,512]{2,1,0:T(8,128)} %u_ref.5, ...), custom_call_target="tpu_custom_call" | custom-call | tf_op jit(solution)/shard_map/pallas_call | solution.py:437
  3.2 0.0 copy-done.1
  3.2 0.2 copy-done
  3.3 1.1 %shard_map.98 = (f32[8,24,128]{2,1,0:T(8,128)S(1)}, f32[8,24,128]{2,1,0:T(8,128)S(1)}) custom-call(f32[8,128,512]{2,1,0:T(8,128)S(1)} %copy-done, f32[8,128,512]{2,1,0:T(8,128)S(1)} %copy-done.1, bf16[2,64,256]{2,1,0:T(8,128)(2,1)S(1)} %get-tuple-element.25.three, bf16[2,32,128]{2,1,0:T(8,128)(2,1)S(1)} %get-tuple-element.26.two, ...), custom_call_target="tpu_custom_call" | custom-call | tf_op jit(solution)/shard_map/pallas_call | solution.py:437
  4.5 0.6 %collective-permute-start = (f32[8,24,128]{2,1,0:T(8,128)S(1)}, f32[8,24,128]{2,1,0:T(8,128)S(1)}, u32[]{:S(2)}, u32[]{:S(2)}) collective-permute-start(f32[8,24,128]{2,1,0:T(8,128)S(1)} %get-tuple-element.29.xe_own), channel_id=1, source_target_pairs={{0,4},{4,0},{8,12},{12,8},{16,20},{20,16},{24,28},{28,24},{1,5},{5... | collective-permute-start | bytes 294920 | tf_op jit(solution)/shard_map/ppermute | solution.py:428
  5.0 3.5 %collective-permute-start.1 = (f32[8,24,128]{2,1,0:T(8,128)S(1)}, f32[8,24,128]{2,1,0:T(8,128)S(1)}, u32[]{:S(2)}, u32[]{:S(2)}) collective-permute-start(f32[8,24,128]{2,1,0:T(8,128)S(1)} %get-tuple-element.30.xo_own), channel_id=1, source_target_pairs={{0,28},{4,8},{8,4},{12,16},{16,12},{20,24},{24,20},{28,0},{1,29},{... | collective-permute-start | bytes 294920 | tf_op jit(solution)/shard_map/ppermute | solution.py:428
  8.6 0.0 collective-permute-start.2
  8.6 0.6 %collective-permute-start.3 = (f32[24,128]{1,0:T(8,128)S(1)}, f32[24,128]{1,0:T(8,128)S(1)}, u32[]{:S(2)}, u32[]{:S(2)}) collective-permute-start(f32[24,128]{1,0:T(8,128)S(1)} %get-tuple-element.33.own_o), channel_id=1, source_target_pairs={{0,28},{4,8},{8,4},{12,16},{16,12},{20,24},{24,20},{28,0},{1,29},{... | collective-permute-start | bytes 36872 | tf_op jit(solution)/shard_map/ppermute | solution.py:428
  9.2 1.9 %shard_map.96 = (f32[160,128]{1,0:T(8,128)S(1)}, bf16[1280,256]{1,0:T(8,128)(2,1)S(1)}, bf16[1280,256]{1,0:T(8,128)(2,1)S(1)}) custom-call(f32[8,128,512]{2,1,0:T(8,128)S(1)} %copy-done, f32[8,128,512]{2,1,0:T(8,128)S(1)} %copy-done.1, bf16[64,256]{1,0:T(8,128)(2,1)S(1)} %get-tuple-element.19.left, bf16[256,256]{1,0:T(8,128)(2,1)S(1)} %get-tuple-element.20.weights), custom_call_target="tpu_custom_call" | custom-call | tf_op jit(solution)/shard_map/pallas_call | solution.py:437
  11.1 0.0 collective-permute-done.2.got_e
  11.1 1.5 %collective-permute-done.3.got_o = f32[24,128]{1,0:T(8,128)S(1)} collective-permute-done((f32[24,128]{1,0:T(8,128)S(1)}, f32[24,128]{1,0:T(8,128)S(1)}, u32[]{:S(2)}, u32[]{:S(2)}) %collective-permute-start.3) | collective-permute-done | bytes 12320 | tf_op jit(solution)/shard_map/ppermute | solution.py:428
  12.6 0.1 shard_map.99
  12.7 1.6 %collective-permute-start.4 = (f32[88,128]{1,0:T(8,128)S(1)}, f32[88,128]{1,0:T(8,128)S(1)}, u32[]{:S(2)}, u32[]{:S(2)}) collective-permute-start(f32[88,128]{1,0:T(8,128)S(1)} %get-tuple-element.34.ye_own), channel_id=1, source_target_pairs={{0,1},{1,0},{2,3},{3,2},{4,5},{5,4},{6,7},{7,6},{8,9},{9,8},{10,11... | collective-permute-start | bytes 135176 | tf_op jit(solution)/shard_map/ppermute | solution.py:428
  14.3 2.5 %collective-permute-start.5 = (f32[88,128]{1,0:T(8,128)S(1)}, f32[88,128]{1,0:T(8,128)S(1)}, u32[]{:S(2)}, u32[]{:S(2)}) collective-permute-start(f32[88,128]{1,0:T(8,128)S(1)} %get-tuple-element.35.yo_own), channel_id=1, source_target_pairs={{0,3},{1,2},{2,1},{3,0},{4,7},{5,6},{6,5},{7,4},{8,11},{9,10},{10,... | collective-permute-start | bytes 135176 | tf_op jit(solution)/shard_map/ppermute | solution.py:428
  16.8 2.2 %shard_map.97.p_ref = f32[1280,128]{1,0:T(8,128)S(1)} custom-call(f32[8,128,512]{2,1,0:T(8,128)S(1)} %copy-done, f32[8,128,512]{2,1,0:T(8,128)S(1)} %copy-done.1, bf16[64,256]{1,0:T(8,128)(2,1)S(1)} %get-tuple-element.19.left, bf16[1280,256]{1,0:T(8,128)(2,1)S(1)} %get-tuple-element.21.ends_high, bf16[1280,256]{1,0:T(8,128)(2,1)S(1)} %get-tuple-element.22.ends_low, ...), custom_call_target="tpu_custom_call" | custom-call | tf_op jit(solution)/shard_map/pallas_call | solution.py:437
  19.0 0.0 collective-permute-done.4.ye_got
  19.0 1.2 %collective-permute-done.5.yo_got = f32[88,128]{1,0:T(8,128)S(1)} collective-permute-done((f32[88,128]{1,0:T(8,128)S(1)}, f32[88,128]{1,0:T(8,128)S(1)}, u32[]{:S(2)}, u32[]{:S(2)}) %collective-permute-start.5) | collective-permute-done | bytes 45088 | tf_op jit(solution)/shard_map/ppermute | solution.py:428
  20.2 0.0 collective-permute-done.xe_got
  20.2 0.0 collective-permute-done.1.xo_got
  20.2 3.2 %shard_map.100 = (f32[3,8,32,128]{3,2,1,0:T(8,128)}, f32[48,8,32,128]{3,2,1,0:T(8,128)}) custom-call(f32[1280,128]{1,0:T(8,128)S(1)} %shard_map.97.p_ref, f32[8,24,128]{2,1,0:T(8,128)S(1)} %get-tuple-element.29.xe_own, f32[8,24,128]{2,1,0:T(8,128)S(1)} %get-tuple-element.30.xo_own, f32[8,24,128]{2,1,0:T(8,128)S(1)} %collective-permute-done.xe_got, ...), custom_call_target="tpu_custom_call" | custom-call | tf_op jit(solution)/shard_map/pallas_call | solution.py:437
Async XLA Ops:
  0.6 2.5 %copy-start.1 = (f32[8,128,512]{2,1,0:T(8,128)S(1)}, f32[8,128,512]{2,1,0:T(8,128)}, u32[]{:S(2)}) copy-start(f32[8,128,512]{2,1,0:T(8,128)} %v_ref.5) | copy-start | bytes 6291460
  0.6 2.7 %copy-start = (f32[8,128,512]{2,1,0:T(8,128)S(1)}, f32[8,128,512]{2,1,0:T(8,128)}, u32[]{:S(2)}) copy-start(f32[8,128,512]{2,1,0:T(8,128)} %u_ref.5) | copy-start | bytes 6291460
  4.5 15.7 %collective-permute-start = (f32[8,24,128]{2,1,0:T(8,128)S(1)}, f32[8,24,128]{2,1,0:T(8,128)S(1)}, u32[]{:S(2)}, u32[]{:S(2)}) collective-permute-start(f32[8,24,128]{2,1,0:T(8,128)S(1)} %get-tuple-element.29.xe_own), channel_id=1, source_target_pairs={{0,4},{4,0},{8,12},{12,8},{16,20},{20,16},{24,28},{28,24},{1,5},{5... | collective-permute-start | bytes 294920 | tf_op jit(solution)/shard_map/ppermute | solution.py:428
  5.0 15.2 %collective-permute-start.1 = (f32[8,24,128]{2,1,0:T(8,128)S(1)}, f32[8,24,128]{2,1,0:T(8,128)S(1)}, u32[]{:S(2)}, u32[]{:S(2)}) collective-permute-start(f32[8,24,128]{2,1,0:T(8,128)S(1)} %get-tuple-element.30.xo_own), channel_id=1, source_target_pairs={{0,28},{4,8},{8,4},{12,16},{16,12},{20,24},{24,20},{28,0},{1,29},{... | collective-permute-start | bytes 294920 | tf_op jit(solution)/shard_map/ppermute | solution.py:428
  8.6 2.6 %collective-permute-start.2 = (f32[24,128]{1,0:T(8,128)S(1)}, f32[24,128]{1,0:T(8,128)S(1)}, u32[]{:S(2)}, u32[]{:S(2)}) collective-permute-start(f32[24,128]{1,0:T(8,128)S(1)} %get-tuple-element.32.own_e), channel_id=1, source_target_pairs={{0,4},{4,0},{8,12},{12,8},{16,20},{20,16},{24,28},{28,24},{1,5},{5... | collective-permute-start | bytes 36872 | tf_op jit(solution)/shard_map/ppermute | solution.py:428
  8.6 4.0 %collective-permute-start.3 = (f32[24,128]{1,0:T(8,128)S(1)}, f32[24,128]{1,0:T(8,128)S(1)}, u32[]{:S(2)}, u32[]{:S(2)}) collective-permute-start(f32[24,128]{1,0:T(8,128)S(1)} %get-tuple-element.33.own_o), channel_id=1, source_target_pairs={{0,28},{4,8},{8,4},{12,16},{16,12},{20,24},{24,20},{28,0},{1,29},{... | collective-permute-start | bytes 36872 | tf_op jit(solution)/shard_map/ppermute | solution.py:428
  12.7 6.3 %collective-permute-start.4 = (f32[88,128]{1,0:T(8,128)S(1)}, f32[88,128]{1,0:T(8,128)S(1)}, u32[]{:S(2)}, u32[]{:S(2)}) collective-permute-start(f32[88,128]{1,0:T(8,128)S(1)} %get-tuple-element.34.ye_own), channel_id=1, source_target_pairs={{0,1},{1,0},{2,3},{3,2},{4,5},{5,4},{6,7},{7,6},{8,9},{9,8},{10,11... | collective-permute-start | bytes 135176 | tf_op jit(solution)/shard_map/ppermute | solution.py:428
  14.3 5.8 %collective-permute-start.5 = (f32[88,128]{1,0:T(8,128)S(1)}, f32[88,128]{1,0:T(8,128)S(1)}, u32[]{:S(2)}, u32[]{:S(2)}) collective-permute-start(f32[88,128]{1,0:T(8,128)S(1)} %get-tuple-element.35.yo_own), channel_id=1, source_target_pairs={{0,3},{1,2},{2,1},{3,0},{4,7},{5,6},{6,5},{7,4},{8,11},{9,10},{10,... | collective-permute-start | bytes 135176 | tf_op jit(solution)/shard_map/ppermute | solution.py:428

commit v4 on v3

--- a/solution.py
+++ b/solution.py
@@ -21,7 +21,7 @@
 MSG = 24
 F32, BF16 = jnp.float32, jnp.bfloat16
 VMEM_BYTES = 24 << 20
-SLAB_UNROLL, MAIN_UNROLL, OWN_UNROLL, FINAL_UNROLL = 2, 2, 4, 1
+MAIN_UNROLL, OWN_UNROLL, FINAL_UNROLL = 8, 8, 1
 
 
 def taps(cells, count_in):
@@ -164,34 +164,34 @@
             )
         )
     ]
-    for copy in loads(0) + consts[:2]:
+    for copy in loads(0) + consts[:3]:
         copy.start()
     for part in range(1, parts):
         for copy in loads(part):
             copy.start()
-    for copy in consts[2:]:
+    for copy in consts[3:]:
         copy.start()
-    for copy in consts[:2]:
+    for copy in consts[:3]:
         copy.wait()
     for part in range(parts):
         for copy in loads(part):
             copy.wait()
 
-        def rows_of(i, part=part):
-            level = part * batch + i
-            at = pl.ds(pl.multiple_of(level * 48, 16), 48)
+        for level in range(part * batch, (part + 1) * batch):
+            at = slice(level * 48, (level + 1) * 48)
             x_high[at], x_low[at] = split(message_sums(three[odd], two[odd], u_ref[level], v_ref[level]))
-
-        each(batch, SLAB_UNROLL, rows_of)
-    consts[2].wait()
     sums = column_sums(x_high[...], x_low[...], weights)
     for place, ref in ((0, e_ref), (8, o_ref)):
-        strips = jnp.zeros(ref.shape, F32)
-        for level in range(levels):
-            strips = strips + pltpu.roll(message_of(sums, level, place), WIDE * level, 1)
-        ref[...] = strips
+        strips = [pltpu.roll(message_of(sums, level, place), WIDE * level, 1) for level in range(levels)]
+        ref[...] = added(strips)
     for copy in consts[3:]:
         copy.wait()
+
+
+def added(terms):
+    while len(terms) > 1:
+        terms = [a + b for a, b in zip(terms[::2], terms[1::2])] + terms[len(terms) & ~1 :]
+    return terms[0]
 
 
 def message_of(sums, level, place):
@@ -203,7 +203,9 @@
     return pl.ds(SIDE, count_y - 2 * SIDE)
 
 
-def main_kernel(u_ref, v_ref, three, two, ends_high, ends_low, w_ends, w_rest, e_ref, o_ref, x_high, x_low):
+def main_kernel(
+    u_ref, v_ref, three, two, ends_high, ends_low, w_ends, w_rest, slab_ref, e_ref, o_ref, x_high, x_low
+):
     odd = lax.rem(lax.axis_index("gx"), 2)
     levels, count_x = u_ref.shape[:2]
 
@@ -220,6 +222,7 @@
     for place, ref in ((0, e_ref), (8, o_ref)):
         for level in range(levels):
             ref[level] = message_of(sums, level, place)
+    e_ref[levels] = slab_ref[...]
 
 
 def own_rows_of(left, u, v):
@@ -230,14 +233,12 @@
     levels, _, count_y = u_ref.shape
     rows, lanes = s_ref.shape
 
-    def rows_of(level):
+    for level in range(levels):
         u, v = (
             jnp.concatenate([r[level, :, :SIDE], r[level, :, count_y - SIDE :]], 1) for r in (u_ref, v_ref)
         )
-        at = pl.ds(pl.multiple_of(level * rows, 16), rows)
+        at = slice(level * rows, (level + 1) * rows)
         x_high[at], x_low[at] = own_rows_of(left[...], u, v)
-
-    each(levels, OWN_UNROLL, rows_of)
     strips = jnp.zeros((rows, lanes), F32)
     for level in range(levels):
         at = slice(level * rows, (level + 1) * rows)
@@ -295,7 +296,7 @@
     uvs[...] = s_ref[3 * coarse : 4 * coarse]
     vvs[...] = s_ref[4 * coarse : 5 * coarse]
     own_low, own_high = low_and_high(odd_x, own_e[...], own_o[...])
-    got_low, got_high = low_and_high(odd_x, got_e[...], got_o[...])
+    got_low, got_high = low_and_high(odd_x, got_e[got_e.shape[0] - 1], got_o[...])
     add_rows((us, vs), (uus, uvs, vvs), own_low, own_high, got_low, got_high)
     rim_rows = us.shape[0]
     start = -(-rim_rows // 8) * 8
@@ -420,12 +421,12 @@
             copy.wait()
 
 
-def swapped(axis, even, odd):
+def pairs_of(axis):
     count = lax.axis_size(axis)
     assert count % 2 == 0
-    pairs = [(i, i ^ 1) for i in range(count)]
-    others = [(i, (i + 1) % count if i % 2 else (i - 1) % count) for i in range(count)]
-    return lax.ppermute(even, axis, pairs), lax.ppermute(odd, axis, others)
+    even = [(i, i ^ 1) for i in range(count)]
+    odd = [(i, (i + 1) % count if i % 2 else (i - 1) % count) for i in range(count)]
+    return even, odd
 
 
 def local_call(body, outs, scratch, *operands):
@@ -461,7 +462,8 @@
     def held(*arrays):
         return [(a, True) for a in arrays]
 
-    parts = 2
+    (even_x, odd_x), (even_y, odd_y) = pairs_of("gx"), pairs_of("gy")
+    parts = 1
     consts = (three, two, w_strips, w_ends, w_rest, left)
     se, so, ends_high, ends_low, *kept = local_call(
         slab_kernel,
@@ -472,16 +474,16 @@
     )
     message_ends = (ends_high, ends_low)
     three, two, w_strips, w_ends, w_rest, left = kept
-    se_got, so_got = swapped("gx", se, so)
+    so_got = lax.ppermute(so, "gx", odd_x)
     fine = held(east_flow, north_flow)
     xe, xo = local_call(
         main_kernel,
-        [f32((levels, MSG, lanes))] * 2,
+        [f32((levels + 1, MSG, lanes)), f32((levels, MSG, lanes))],
         [bf16((48 * levels, count_y - 2 * SIDE))] * 2,
         *fine,
-        *held(three, two, *message_ends, w_ends, w_rest),
-    )
-    xe_got, xo_got = swapped("gx", xe, xo)
+        *held(three, two, *message_ends, w_ends, w_rest, se),
+    )
+    xe_got, xo_got = lax.ppermute(xe, "gx", even_x), lax.ppermute(xo, "gx", odd_x)
     strips, *own_ends = local_call(
         ends_kernel,
         [f32((own_count, lanes))] + [bf16((own_count * levels, 2 * SIDE))] * 2,
@@ -490,8 +492,8 @@
         *held(left, w_strips),
     )
     rows = [f32((rim_rows, lanes))] * 2 + [f32((coarse, lanes))] * 3
-    ye, yo = local_call(strip_kernel, [f32(side)] * 2, rows, *held(strips, se, so, se_got, so_got))
-    ye_got, yo_got = swapped("gy", ye, yo)
+    ye, yo = local_call(strip_kernel, [f32(side)] * 2, rows, *held(strips, se, so, xe_got, so_got))
+    ye_got, yo_got = lax.ppermute(ye, "gy", even_y), lax.ppermute(yo, "gy", odd_y)
     (partial_sums,) = local_call(
         own_kernel,
         [f32((own_count * levels, lanes))],

time: 23.6 us -> 23.1 us (0.979)
  Pallas kernels: 11.1 us -> 9.77 us
  waiting for transfers between devices: 2.64 us -> 3.65 us
  starting transfers between devices: 8.87 us -> 8.26 us
  local copies, waits for them, and re-layouts: 0.16 us -> 0.54 us
    pallas_call x6, Pallas kernels: 11.1 us -> 9.77 us  [local_call(): pl.pallas_call(body, in_specs=specs, out_specs=[in_hbm if isinstance(o, j...]
    ppermute x6 -> x5, waiting for transfers between devices: 2.64 us -> 3.65 us  [the longest x1 2.35 us: in_order(): so_got = lax.ppermute(so, 'gx', odd_x)]
    ppermute x6 -> x5, starting transfers between devices: 8.87 us -> 8.26 us  [the longest x1 3.54 us: in_order(): lax.ppermute(xo, 'gx', odd_x)]
    unnamed x4, local copies, waits for them, and re-layouts: 0.16 us -> 0.54 us
  transfers between devices with their start and end apart: 6 -> 5, of which waited for: 2 -> 2; matrix products, arithmetic and copies ran while one was open for 0% -> 0% of each run, Pallas kernels for 18% -> 17%
where the time goes in v4:
time: 23.1 us; the launch traced here: 22.9 us
  Pallas kernels  9.77 us (42%)
  starting transfers between devices  8.26 us (36%)
  waiting for transfers between devices  3.65 us (16%)
  between operations  0.71 us (3%)
  local copies, waits for them, and re-layouts  0.54 us (2%)
    pallas_call x6, Pallas kernels, local_call(): pl.pallas_call(body, in_specs=specs, out_specs=[in_hbm if isinstance(o, j...  9.77 us
    ppermute x1, starting transfers between devices, in_order(): lax.ppermute(xo, 'gx', odd_x)  3.54 us
    ppermute x1, starting transfers between devices, in_order(): lax.ppermute(yo, 'gy', odd_y)  2.47 us
    ppermute x1, waiting for transfers between devices, in_order(): so_got = lax.ppermute(so, 'gx', odd_x)  2.35 us
    ppermute x1, starting transfers between devices, in_order(): lax.ppermute(ye, 'gy', even_y)  1.64 us
    ppermute x1, waiting for transfers between devices, in_order(): lax.ppermute(yo, 'gy', odd_y)  1.29 us
    ppermute x1, starting transfers between devices, in_order(): lax.ppermute(xe, 'gx', even_x)  0.56 us
    unnamed x4, local copies, waits for them, and re-layouts  0.54 us
  transfers between devices with their start and end apart: 5, of which 2 were waited for; matrix products, arithmetic and copies ran while one was open for 0% of the time, Pallas kernels for 17%

profile of v4, /device:TPU:0, one launch (start us, length us, event | category | flops | bytes accessed | tf_op | source)
XLA Modules:
  0.0 22.9 jit_solution(2439807798575357881)
XLA Ops:
  0.6 0.0 copy-start.1
  0.6 0.0 copy-start
  0.6 2.2 %shard_map.95 = (f32[24,128]{1,0:T(8,128)S(1)}, f32[24,128]{1,0:T(8,128)S(1)}, bf16[384,256]{1,0:T(8,128)(2,1)S(1)}, bf16[384,256]{1,0:T(8,128)(2,1)S(1)}, bf16[...) custom-call(f32[8,128,512]{2,1,0:T(8,128)} %u_ref.5, ...), custom_call_target="tpu_custom_call" | custom-call | tf_op jit(solution)/shard_map/pallas_call | solution.py:438
  2.8 0.0 copy-done.1
  2.8 0.5 %copy-done = f32[8,128,512]{2,1,0:T(8,128)S(1)} copy-done((f32[8,128,512]{2,1,0:T(8,128)S(1)}, f32[8,128,512]{2,1,0:T(8,128)}, u32[]{:S(2)}) %copy-start) | copy-done | bytes 2097176
  3.4 0.6 %shard_map.98 = (f32[9,24,128]{2,1,0:T(8,128)S(1)}, f32[8,24,128]{2,1,0:T(8,128)S(1)}) custom-call(f32[8,128,512]{2,1,0:T(8,128)S(1)} %copy-done, f32[8,128,512]{2,1,0:T(8,128)S(1)} %copy-done.1, bf16[2,64,256]{2,1,0:T(8,128)(2,1)S(1)} %get-tuple-element.25.three, bf16[2,32,128]{2,1,0:T(8,128)(2,1)S(1)} %get-tuple-element.26.two, ...), custom_call_target="tpu_custom_call" | custom-call | tf_op jit(solution)/shard_map/pallas_call | solution.py:438
  4.0 0.6 %collective-permute-start = (f32[9,24,128]{2,1,0:T(8,128)S(1)}, f32[9,24,128]{2,1,0:T(8,128)S(1)}, u32[]{:S(2)}, u32[]{:S(2)}) collective-permute-start(f32[9,24,128]{2,1,0:T(8,128)S(1)} %get-tuple-element.30.xe_own), channel_id=1, source_target_pairs={{0,4},{4,0},{8,12},{12,8},{16,20},{20,16},{24,28},{28,24},{1,5},{5... | collective-permute-start | bytes 331784 | tf_op jit(solution)/shard_map/ppermute | solution.py:486
  4.5 3.5 %collective-permute-start.1 = (f32[8,24,128]{2,1,0:T(8,128)S(1)}, f32[8,24,128]{2,1,0:T(8,128)S(1)}, u32[]{:S(2)}, u32[]{:S(2)}) collective-permute-start(f32[8,24,128]{2,1,0:T(8,128)S(1)} %get-tuple-element.31.xo_own), channel_id=1, source_target_pairs={{0,28},{4,8},{8,4},{12,16},{16,12},{20,24},{24,20},{28,0},{1,29},{... | collective-permute-start | bytes 294920 | tf_op jit(solution)/shard_map/ppermute | solution.py:486
  8.1 0.0 collective-permute-start.2
  8.1 1.6 %shard_map.96 = (f32[160,128]{1,0:T(8,128)S(1)}, bf16[1280,256]{1,0:T(8,128)(2,1)S(1)}, bf16[1280,256]{1,0:T(8,128)(2,1)S(1)}) custom-call(f32[8,128,512]{2,1,0:T(8,128)S(1)} %copy-done, f32[8,128,512]{2,1,0:T(8,128)S(1)} %copy-done.1, bf16[64,256]{1,0:T(8,128)(2,1)S(1)} %get-tuple-element.19.left, bf16[256,256]{1,0:T(8,128)(2,1)S(1)} %get-tuple-element.20.weights), custom_call_target="tpu_custom_call" | custom-call | tf_op jit(solution)/shard_map/pallas_call | solution.py:438
  9.7 2.4 %collective-permute-done.2.got_o = f32[24,128]{1,0:T(8,128)S(1)} collective-permute-done((f32[24,128]{1,0:T(8,128)S(1)}, f32[24,128]{1,0:T(8,128)S(1)}, u32[]{:S(2)}, u32[]{:S(2)}) %collective-permute-start.2) | collective-permute-done | bytes 12320 | tf_op jit(solution)/shard_map/ppermute | solution.py:477
  12.1 0.0 collective-permute-done.got_e.xe_got
  12.1 0.1 shard_map.99
  12.2 1.6 %collective-permute-start.3 = (f32[88,128]{1,0:T(8,128)S(1)}, f32[88,128]{1,0:T(8,128)S(1)}, u32[]{:S(2)}, u32[]{:S(2)}) collective-permute-start(f32[88,128]{1,0:T(8,128)S(1)} %get-tuple-element.34.ye_own), channel_id=1, source_target_pairs={{0,1},{1,0},{2,3},{3,2},{4,5},{5,4},{6,7},{7,6},{8,9},{9,8},{10,11... | collective-permute-start | bytes 135176 | tf_op jit(solution)/shard_map/ppermute | solution.py:496
  13.8 2.5 %collective-permute-start.4 = (f32[88,128]{1,0:T(8,128)S(1)}, f32[88,128]{1,0:T(8,128)S(1)}, u32[]{:S(2)}, u32[]{:S(2)}) collective-permute-start(f32[88,128]{1,0:T(8,128)S(1)} %get-tuple-element.35.yo_own), channel_id=1, source_target_pairs={{0,3},{1,2},{2,1},{3,0},{4,7},{5,6},{6,5},{7,4},{8,11},{9,10},{10,... | collective-permute-start | bytes 135176 | tf_op jit(solution)/shard_map/ppermute | solution.py:496
  16.3 2.1 %shard_map.97.p_ref = f32[1280,128]{1,0:T(8,128)S(1)} custom-call(f32[8,128,512]{2,1,0:T(8,128)S(1)} %copy-done, f32[8,128,512]{2,1,0:T(8,128)S(1)} %copy-done.1, bf16[64,256]{1,0:T(8,128)(2,1)S(1)} %get-tuple-element.19.left, bf16[1280,256]{1,0:T(8,128)(2,1)S(1)} %get-tuple-element.21.ends_high, bf16[1280,256]{1,0:T(8,128)(2,1)S(1)} %get-tuple-element.22.ends_low, ...), custom_call_target="tpu_custom_call" | custom-call | tf_op jit(solution)/shard_map/pallas_call | solution.py:438
  18.4 0.0 collective-permute-done.1.xo_got
  18.4 0.0 collective-permute-done.3.ye_got
  18.4 1.3 %collective-permute-done.4.yo_got = f32[88,128]{1,0:T(8,128)S(1)} collective-permute-done((f32[88,128]{1,0:T(8,128)S(1)}, f32[88,128]{1,0:T(8,128)S(1)}, u32[]{:S(2)}, u32[]{:S(2)}) %collective-permute-start.4) | collective-permute-done | bytes 45088 | tf_op jit(solution)/shard_map/ppermute | solution.py:496
  19.7 3.2 %shard_map.100 = (f32[3,8,32,128]{3,2,1,0:T(8,128)}, f32[48,8,32,128]{3,2,1,0:T(8,128)}) custom-call(f32[1280,128]{1,0:T(8,128)S(1)} %shard_map.97.p_ref, f32[9,24,128]{2,1,0:T(8,128)S(1)} %get-tuple-element.30.xe_own, f32[8,24,128]{2,1,0:T(8,128)S(1)} %get-tuple-element.31.xo_own, f32[9,24,128]{2,1,0:T(8,128)S(1)} %collective-permute-done.got_e.xe_got, ...), custom_call_target="tpu_custom_call" | custom-call | tf_op jit(solution)/shard_map/pallas_call | solution.py:438
Async XLA Ops:
  0.6 2.2 %copy-start.1 = (f32[8,128,512]{2,1,0:T(8,128)S(1)}, f32[8,128,512]{2,1,0:T(8,128)}, u32[]{:S(2)}) copy-start(f32[8,128,512]{2,1,0:T(8,128)} %v_ref.5) | copy-start | bytes 6291460
  0.6 2.7 %copy-start = (f32[8,128,512]{2,1,0:T(8,128)S(1)}, f32[8,128,512]{2,1,0:T(8,128)}, u32[]{:S(2)}) copy-start(f32[8,128,512]{2,1,0:T(8,128)} %u_ref.5) | copy-start | bytes 6291460
  4.0 8.1 %collective-permute-start = (f32[9,24,128]{2,1,0:T(8,128)S(1)}, f32[9,24,128]{2,1,0:T(8,128)S(1)}, u32[]{:S(2)}, u32[]{:S(2)}) collective-permute-start(f32[9,24,128]{2,1,0:T(8,128)S(1)} %get-tuple-element.30.xe_own), channel_id=1, source_target_pairs={{0,4},{4,0},{8,12},{12,8},{16,20},{20,16},{24,28},{28,24},{1,5},{5... | collective-permute-start | bytes 331784 | tf_op jit(solution)/shard_map/ppermute | solution.py:486
  4.5 13.9 %collective-permute-start.1 = (f32[8,24,128]{2,1,0:T(8,128)S(1)}, f32[8,24,128]{2,1,0:T(8,128)S(1)}, u32[]{:S(2)}, u32[]{:S(2)}) collective-permute-start(f32[8,24,128]{2,1,0:T(8,128)S(1)} %get-tuple-element.31.xo_own), channel_id=1, source_target_pairs={{0,28},{4,8},{8,4},{12,16},{16,12},{20,24},{24,20},{28,0},{1,29},{... | collective-permute-start | bytes 294920 | tf_op jit(solution)/shard_map/ppermute | solution.py:486
  8.1 4.0 %collective-permute-start.2 = (f32[24,128]{1,0:T(8,128)S(1)}, f32[24,128]{1,0:T(8,128)S(1)}, u32[]{:S(2)}, u32[]{:S(2)}) collective-permute-start(f32[24,128]{1,0:T(8,128)S(1)} %get-tuple-element.33.own_o), channel_id=1, source_target_pairs={{0,28},{4,8},{8,4},{12,16},{16,12},{20,24},{24,20},{28,0},{1,29},{... | collective-permute-start | bytes 36872 | tf_op jit(solution)/shard_map/ppermute | solution.py:477
  12.2 6.2 %collective-permute-start.3 = (f32[88,128]{1,0:T(8,128)S(1)}, f32[88,128]{1,0:T(8,128)S(1)}, u32[]{:S(2)}, u32[]{:S(2)}) collective-permute-start(f32[88,128]{1,0:T(8,128)S(1)} %get-tuple-element.34.ye_own), channel_id=1, source_target_pairs={{0,1},{1,0},{2,3},{3,2},{4,5},{5,4},{6,7},{7,6},{8,9},{9,8},{10,11... | collective-permute-start | bytes 135176 | tf_op jit(solution)/shard_map/ppermute | solution.py:496
  13.8 5.8 %collective-permute-start.4 = (f32[88,128]{1,0:T(8,128)S(1)}, f32[88,128]{1,0:T(8,128)S(1)}, u32[]{:S(2)}, u32[]{:S(2)}) collective-permute-start(f32[88,128]{1,0:T(8,128)S(1)} %get-tuple-element.35.yo_own), channel_id=1, source_target_pairs={{0,3},{1,2},{2,1},{3,0},{4,7},{5,6},{6,5},{7,4},{8,11},{9,10},{10,... | collective-permute-start | bytes 135176 | tf_op jit(solution)/shard_map/ppermute | solution.py:496

commit v5 on v4

--- a/solution.py
+++ b/solution.py
@@ -80,7 +80,8 @@
     own = taps(range(coarse), count_y).T
     strips = np.zeros((count_y, 2 * HALF))
     strips[:, :WIDE] = taps(range(-EXT, RIM), count_y).T
-    strips[:, HALF : HALF + WIDE] = taps(range(coarse - RIM, coarse + EXT), count_y).T
+    high = list(range(coarse, coarse + EXT)) + list(range(coarse - RIM, coarse))
+    strips[:, HALF : HALF + WIDE] = taps(high, count_y).T
 
     def ends(w):
         return np.concatenate([w[:SIDE], w[count_y - SIDE :]], 0)
@@ -181,11 +182,22 @@
             at = slice(level * 48, (level + 1) * 48)
             x_high[at], x_low[at] = split(message_sums(three[odd], two[odd], u_ref[level], v_ref[level]))
     sums = column_sums(x_high[...], x_low[...], weights)
+    row = lax.broadcasted_iota(jnp.int32, e_ref.shape, 0)
+    wide = (row < 16) & (lax.rem(row, 8) < WIDE)
     for place, ref in ((0, e_ref), (8, o_ref)):
-        strips = [pltpu.roll(message_of(sums, level, place), WIDE * level, 1) for level in range(levels)]
-        ref[...] = added(strips)
+        parts = [message_of(sums, level, place) for level in range(levels)]
+        ref[...] = jnp.where(wide, packed(parts, WIDE), packed([short_only(p) for p in parts], EXT))
     for copy in consts[3:]:
         copy.wait()
+
+
+def short_only(strips):
+    lane = lax.broadcasted_iota(jnp.int32, strips.shape, 1)
+    return jnp.where(lax.rem(lane, HALF) < EXT, strips, 0.0)
+
+
+def packed(parts, cells):
+    return added([pltpu.roll(part, cells * level, 1) for level, part in enumerate(parts)])
 
 
 def added(terms):
@@ -239,11 +251,15 @@
         )
         at = slice(level * rows, (level + 1) * rows)
         x_high[at], x_low[at] = own_rows_of(left[...], u, v)
-    strips = jnp.zeros((rows, lanes), F32)
+    wide = rows // 5 * 2
+    strips, short = jnp.zeros((wide, lanes), F32), jnp.zeros((rows - wide, lanes), F32)
     for level in range(levels):
         at = slice(level * rows, (level + 1) * rows)
-        strips = strips + pltpu.roll(column_sums(x_high[at], x_low[at], weights), WIDE * level, 1)
-    s_ref[...] = strips
+        sums = column_sums(x_high[at], x_low[at], weights)
+        strips = strips + pltpu.roll(sums[:wide], WIDE * level, 1)
+        short = short + pltpu.roll(short_only(sums[wide:]), EXT * level, 1)
+    s_ref[:wide] = strips
+    s_ref[wide:] = short
 
 
 def own_kernel(u_ref, v_ref, left, ends_high, ends_low, w_ends, w_rest, p_ref, x_high, x_low):
@@ -286,7 +302,7 @@
                 ref[back : back + 2] = ref[back : back + 2] + got_high[at : at + 2]
 
 
-def strip_kernel(s_ref, own_e, own_o, got_e, got_o, e_ref, o_ref, us, vs, uus, uvs, vvs):
+def strip_kernel(levels, s_ref, own_e, own_o, got_e, got_o, e_ref, o_ref, us, vs, uus, uvs, vvs):
     odd_x = lax.rem(lax.axis_index("gx"), 2)
     odd_y = lax.rem(lax.axis_index("gy"), 2)
     coarse = uus.shape[0]
@@ -298,19 +314,33 @@
     own_low, own_high = low_and_high(odd_x, own_e[...], own_o[...])
     got_low, got_high = low_and_high(odd_x, got_e[got_e.shape[0] - 1], got_o[...])
     add_rows((us, vs), (uus, uvs, vvs), own_low, own_high, got_low, got_high)
-    rim_rows = us.shape[0]
-    start = -(-rim_rows // 8) * 8
-    pairs = (
-        (0, us[...], vs[...]),
-        (start, uus[...], uvs[...]),
-        (start + coarse, vvs[0 : coarse // 2], vvs[coarse // 2 : coarse]),
-    )
-    for at, a, b in pairs:
-        lane = lax.broadcasted_iota(jnp.int32, a.shape, 1)
-        low = jnp.where(lane < HALF, a, pltpu.roll(b, HALF, 1))
-        high = jnp.where(lane < HALF, pltpu.roll(a, HALF, 1), b)
-        e_ref[at : at + a.shape[0]] = jnp.where(odd_y == 0, high, low)
-        o_ref[at : at + a.shape[0]] = jnp.where(odd_y == 0, low, high)
+    start = e_ref.shape[0] - coarse // 2
+    lanes = e_ref.shape[1]
+    wide, short = WIDE * levels, EXT * levels
+
+    def laid(fields, ends, from_lane):
+        lane = lax.broadcasted_iota(jnp.int32, fields[0].shape, 1)
+        total, begin = None, 0
+        for field, end in zip(fields, ends):
+            there = pltpu.roll(field, (lanes + begin - from_lane) % lanes, 1) if begin != from_lane else field
+            total = there if total is None else jnp.where(lane < begin, total, there)
+            begin = end
+        return total
+
+    h = coarse // 2
+    sides = []
+    for from_lane in (0, HALF):
+        both = laid((us[...], vs[...]), (wide, 2 * wide), from_lane)
+        lane = lax.broadcasted_iota(jnp.int32, (coarse, lanes), 1)
+        uu = pltpu.roll(uus[...], (lanes + 2 * wide - from_lane) % lanes, 1)
+        first = jnp.where(lane < 2 * wide, both[:coarse], uu)
+        quarters = (uvs[:h], uvs[h:], vvs[:h], vvs[h:])
+        second = laid(quarters, [short * n for n in range(1, 5)], from_lane)
+        sides.append((first, both[coarse:], second))
+    for low, high, at in zip(*sides, (0, coarse, start)):
+        here = slice(at, at + low.shape[0])
+        e_ref[here] = jnp.where(odd_y == 0, high, low)
+        o_ref[here] = jnp.where(odd_y == 0, low, high)
 
 
 def first_form(plus_two, plus_one, minus_one, minus_two):
@@ -331,11 +361,17 @@
     rim_rows = us.shape[0]
     own_low, own_high = low_and_high(odd_y, ye_own[...], yo_own[...])
     got_low, got_high = low_and_high(odd_y, ye_got[...], yo_got[...])
-    place = lax.rem(lax.rem(lax.broadcasted_iota(jnp.int32, own_low.shape, 1), HALF), WIDE)
-    back = pltpu.roll(own_low, lanes - RIM, 1)
-    ahead = pltpu.roll(own_high, RIM, 1)
-    low_side[...] = got_low + jnp.where(place < RIM, back, 0.0)
-    high_side[...] = got_high + jnp.where(place >= EXT, ahead, 0.0)
+    lane = lax.broadcasted_iota(jnp.int32, own_low.shape, 1)
+    row = lax.broadcasted_iota(jnp.int32, own_low.shape, 0)
+    wide, short = WIDE * levels, EXT * levels
+    start = own_low.shape[0] - coarse // 2
+    is_wide = (lane < 2 * wide) & (row < start)
+    place = lax.rem(lane, WIDE)
+    rim = pltpu.roll(got_low, lanes - EXT, 1) + pltpu.roll(own_low, lanes - RIM, 1)
+    ordered = jnp.where(place < RIM, rim, pltpu.roll(got_low, RIM, 1))
+    low_side[...] = jnp.where(is_wide, ordered, got_low)
+    ahead = pltpu.roll(own_high, EXT, 1)
+    high_side[...] = got_high + jnp.where(is_wide & (place >= EXT), ahead, 0.0)
 
     def out(level):
         return (
@@ -355,12 +391,11 @@
         got_low, got_high = low_and_high(odd_x, xe_got[level], xo_got[level])
         add_rows((us, vs), (uus, uvs, vvs), own_low, own_high, got_low, got_high)
 
-        shift = WIDE * level
-
-        def sides(at, count, second):
-            base = HALF if second else 0
-            low = pltpu.roll(low_side[at : at + count], lanes - RIM - base - shift, 1)
-            high = pltpu.roll(high_side[at : at + count], lanes - EXT - base - shift, 1)
+        def sides(at, count, base, cells):
+            rim = RIM if cells == WIDE else 0
+            first = base + cells * level
+            low = pltpu.roll(low_side[at : at + count], lax.rem(2 * lanes - rim - first, lanes), 1)
+            high = pltpu.roll(high_side[at : at + count], lanes - EXT - first, 1)
             return low, high
 
         def joined(field, low, high):
@@ -370,7 +405,7 @@
         means = []
         found = []
         for k, ref in enumerate((us, vs)):
-            low, high = sides(0, rim_rows, k == 1)
+            low, high = sides(0, rim_rows, k * wide, WIDE)
             f = joined(ref[...], low, high)
             ref[...] = f
             lane = lax.broadcasted_iota(jnp.int32, f.shape, 1)
@@ -394,15 +429,13 @@
             found.append((grad_x, grad_y, curve_x, cross, curve_y))
 
         u, v = means
-        start = -(-rim_rows // 8) * 8
-        low, high = sides(start, coarse, False)
+        low, high = sides(0, coarse, 2 * wide, EXT)
         st_ref[0, level] = joined(uus[...], low, high) - u * u
-        low, high = sides(start, coarse, True)
-        st_ref[1, level] = joined(uvs[...], low, high) - u * v
-        for h in range(2):
-            part = slice(coarse // 2 * h, coarse // 2 * (h + 1))
-            low, high = sides(start + coarse, coarse // 2, h == 1)
-            st_ref[2, level, part] = joined(vvs[part], low, high) - v[part] * v[part]
+        for k, (ref, other) in enumerate(((uvs, u), (vvs, v))):
+            for h in range(2):
+                part = slice(coarse // 2 * h, coarse // 2 * (h + 1))
+                low, high = sides(start, coarse // 2, (2 * k + h) * short, EXT)
+                st_ref[1 + k, level, part] = joined(ref[part], low, high) - other[part] * v[part]
 
         (ux, uy, uxx, uxy, uyy), (vx, vy, vxx, vxy, vyy) = found
         vorticity = vx - uy
@@ -448,14 +481,14 @@
 def in_order(east_flow, north_flow):
     levels, count_x, count_y = east_flow.shape
     coarse, lanes = count_x // STEP, count_y // STEP
-    assert lanes == 2 * HALF and WIDE * levels <= HALF and coarse % 16 == 0
+    assert lanes == 2 * HALF and (2 * WIDE + EXT) * levels <= lanes and coarse % 16 == 0
     assert count_x >= 2 * EDGE and count_y > 2 * SIDE
     three, two = (jnp.asarray(c) for c in message_rows(count_x))
     w_strips, w_ends, w_rest = (jnp.asarray(c) for c in column_weights(count_y))
     left = jnp.asarray(left_operand(taps(range(coarse), count_x)))
     rim_rows = coarse + 2 * RIM
     start = -(-rim_rows // 8) * 8
-    side = (start + coarse + coarse // 2, lanes)
+    side = (start + coarse // 2, lanes)
     own_count = 5 * coarse
     f32, bf16 = functools.partial(pltpu.VMEM, dtype=F32), functools.partial(pltpu.VMEM, dtype=BF16)
 
@@ -492,7 +525,7 @@
         *held(left, w_strips),
     )
     rows = [f32((rim_rows, lanes))] * 2 + [f32((coarse, lanes))] * 3
-    ye, yo = local_call(strip_kernel, [f32(side)] * 2, rows, *held(strips, se, so, xe_got, so_got))
+    ye, yo = local_call(functools.partial(strip_kernel, levels), [f32(side)] * 2, rows, *held(strips, se, so, xe_got, so_got))
     ye_got, yo_got = lax.ppermute(ye, "gy", even_y), lax.ppermute(yo, "gy", odd_y)
     (partial_sums,) = local_call(
         own_kernel,

time: 23.1 us -> 22.9 us (level)
  no operation moved by 1% of the time
where the time goes in v5:
time: 22.9 us; the launch traced here: 22.8 us
  Pallas kernels  9.79 us (43%)
  starting transfers between devices  8.26 us (36%)
  waiting for transfers between devices  3.47 us (15%)
  between operations  0.71 us (3%)
  local copies, waits for them, and re-layouts  0.53 us (2%)
    pallas_call x6, Pallas kernels, local_call(): pl.pallas_call(body, in_specs=specs, out_specs=[in_hbm if isinstance(o, j...  9.79 us
    ppermute x1, starting transfers between devices, in_order(): lax.ppermute(xo, 'gx', odd_x)  3.54 us
    ppermute x1, starting transfers between devices, in_order(): lax.ppermute(yo, 'gy', odd_y)  2.47 us
    ppermute x1, waiting for transfers between devices, in_order(): so_got = lax.ppermute(so, 'gx', odd_x)  2.35 us
    ppermute x1, starting transfers between devices, in_order(): lax.ppermute(ye, 'gy', even_y)  1.64 us
    ppermute x1, waiting for transfers between devices, in_order(): lax.ppermute(yo, 'gy', odd_y)  1.11 us
    ppermute x1, starting transfers between devices, in_order(): lax.ppermute(xe, 'gx', even_x)  0.56 us
    unnamed x4, local copies, waits for them, and re-layouts  0.53 us
  transfers between devices with their start and end apart: 5, of which 2 were waited for; matrix products, arithmetic and copies ran while one was open for 0% of the time, Pallas kernels for 17%

profile of v5, /device:TPU:0, one launch (start us, length us, event | category | flops | bytes accessed | tf_op | source)
XLA Modules:
  0.0 22.8 jit_solution(11294277320390865327)
XLA Ops:
  0.6 0.0 copy-start.1
  0.6 0.0 copy-start
  0.6 2.2 %shard_map.95 = (f32[24,128]{1,0:T(8,128)S(1)}, f32[24,128]{1,0:T(8,128)S(1)}, bf16[384,256]{1,0:T(8,128)(2,1)S(1)}, bf16[384,256]{1,0:T(8,128)(2,1)S(1)}, bf16[...) custom-call(f32[8,128,512]{2,1,0:T(8,128)} %u_ref.5, ...), custom_call_target="tpu_custom_call" | custom-call | tf_op jit(solution)/shard_map/pallas_call | solution.py:471
  2.8 0.0 copy-done.1
  2.8 0.5 %copy-done = f32[8,128,512]{2,1,0:T(8,128)S(1)} copy-done((f32[8,128,512]{2,1,0:T(8,128)S(1)}, f32[8,128,512]{2,1,0:T(8,128)}, u32[]{:S(2)}) %copy-start) | copy-done | bytes 2097176
  3.4 0.6 %shard_map.98 = (f32[9,24,128]{2,1,0:T(8,128)S(1)}, f32[8,24,128]{2,1,0:T(8,128)S(1)}) custom-call(f32[8,128,512]{2,1,0:T(8,128)S(1)} %copy-done, f32[8,128,512]{2,1,0:T(8,128)S(1)} %copy-done.1, bf16[2,64,256]{2,1,0:T(8,128)(2,1)S(1)} %get-tuple-element.25.three, bf16[2,32,128]{2,1,0:T(8,128)(2,1)S(1)} %get-tuple-element.26.two, ...), custom_call_target="tpu_custom_call" | custom-call | tf_op jit(solution)/shard_map/pallas_call | solution.py:471
  4.0 0.6 %collective-permute-start = (f32[9,24,128]{2,1,0:T(8,128)S(1)}, f32[9,24,128]{2,1,0:T(8,128)S(1)}, u32[]{:S(2)}, u32[]{:S(2)}) collective-permute-start(f32[9,24,128]{2,1,0:T(8,128)S(1)} %get-tuple-element.30.xe_own), channel_id=1, source_target_pairs={{0,4},{4,0},{8,12},{12,8},{16,20},{20,16},{24,28},{28,24},{1,5},{5... | collective-permute-start | bytes 331784 | tf_op jit(solution)/shard_map/ppermute | solution.py:519
  4.5 3.5 %collective-permute-start.1 = (f32[8,24,128]{2,1,0:T(8,128)S(1)}, f32[8,24,128]{2,1,0:T(8,128)S(1)}, u32[]{:S(2)}, u32[]{:S(2)}) collective-permute-start(f32[8,24,128]{2,1,0:T(8,128)S(1)} %get-tuple-element.31.xo_own), channel_id=1, source_target_pairs={{0,28},{4,8},{8,4},{12,16},{16,12},{20,24},{24,20},{28,0},{1,29},{... | collective-permute-start | bytes 294920 | tf_op jit(solution)/shard_map/ppermute | solution.py:519
  8.1 0.0 collective-permute-start.2
  8.1 1.6 %shard_map.96 = (f32[160,128]{1,0:T(8,128)S(1)}, bf16[1280,256]{1,0:T(8,128)(2,1)S(1)}, bf16[1280,256]{1,0:T(8,128)(2,1)S(1)}) custom-call(f32[8,128,512]{2,1,0:T(8,128)S(1)} %copy-done, f32[8,128,512]{2,1,0:T(8,128)S(1)} %copy-done.1, bf16[64,256]{1,0:T(8,128)(2,1)S(1)} %get-tuple-element.19.left, bf16[256,256]{1,0:T(8,128)(2,1)S(1)} %get-tuple-element.20.weights), custom_call_target="tpu_custom_call" | custom-call | tf_op jit(solution)/shard_map/pallas_call | solution.py:471
  9.7 2.3 %collective-permute-done.2.got_o = f32[24,128]{1,0:T(8,128)S(1)} collective-permute-done((f32[24,128]{1,0:T(8,128)S(1)}, f32[24,128]{1,0:T(8,128)S(1)}, u32[]{:S(2)}, u32[]{:S(2)}) %collective-permute-start.2) | collective-permute-done | bytes 12320 | tf_op jit(solution)/shard_map/ppermute | solution.py:510
  12.1 0.0 collective-permute-done.got_e.xe_got
  12.1 0.1 shard_map.99
  12.2 1.6 %collective-permute-start.3 = (f32[56,128]{1,0:T(8,128)S(1)}, f32[56,128]{1,0:T(8,128)S(1)}, u32[]{:S(2)}, u32[]{:S(2)}) collective-permute-start(f32[56,128]{1,0:T(8,128)S(1)} %get-tuple-element.34.ye_own), channel_id=1, source_target_pairs={{0,1},{1,0},{2,3},{3,2},{4,5},{5,4},{6,7},{7,6},{8,9},{9,8},{10,11... | collective-permute-start | bytes 86024 | tf_op jit(solution)/shard_map/ppermute | solution.py:529
  13.9 2.5 %collective-permute-start.4 = (f32[56,128]{1,0:T(8,128)S(1)}, f32[56,128]{1,0:T(8,128)S(1)}, u32[]{:S(2)}, u32[]{:S(2)}) collective-permute-start(f32[56,128]{1,0:T(8,128)S(1)} %get-tuple-element.35.yo_own), channel_id=1, source_target_pairs={{0,3},{1,2},{2,1},{3,0},{4,7},{5,6},{6,5},{7,4},{8,11},{9,10},{10,... | collective-permute-start | bytes 86024 | tf_op jit(solution)/shard_map/ppermute | solution.py:529
  16.3 2.1 %shard_map.97.p_ref = f32[1280,128]{1,0:T(8,128)S(1)} custom-call(f32[8,128,512]{2,1,0:T(8,128)S(1)} %copy-done, f32[8,128,512]{2,1,0:T(8,128)S(1)} %copy-done.1, bf16[64,256]{1,0:T(8,128)(2,1)S(1)} %get-tuple-element.19.left, bf16[1280,256]{1,0:T(8,128)(2,1)S(1)} %get-tuple-element.21.ends_high, bf16[1280,256]{1,0:T(8,128)(2,1)S(1)} %get-tuple-element.22.ends_low, ...), custom_call_target="tpu_custom_call" | custom-call | tf_op jit(solution)/shard_map/pallas_call | solution.py:471
  18.4 0.0 collective-permute-done.1.xo_got
  18.4 0.0 collective-permute-done.3.ye_got
  18.4 1.1 %collective-permute-done.4.yo_got = f32[56,128]{1,0:T(8,128)S(1)} collective-permute-done((f32[56,128]{1,0:T(8,128)S(1)}, f32[56,128]{1,0:T(8,128)S(1)}, u32[]{:S(2)}, u32[]{:S(2)}) %collective-permute-start.4) | collective-permute-done | bytes 28704 | tf_op jit(solution)/shard_map/ppermute | solution.py:529
  19.5 3.2 %shard_map.100 = (f32[3,8,32,128]{3,2,1,0:T(8,128)}, f32[48,8,32,128]{3,2,1,0:T(8,128)}) custom-call(f32[1280,128]{1,0:T(8,128)S(1)} %shard_map.97.p_ref, f32[9,24,128]{2,1,0:T(8,128)S(1)} %get-tuple-element.30.xe_own, f32[8,24,128]{2,1,0:T(8,128)S(1)} %get-tuple-element.31.xo_own, f32[9,24,128]{2,1,0:T(8,128)S(1)} %collective-permute-done.got_e.xe_got, ...), custom_call_target="tpu_custom_call" | custom-call | tf_op jit(solution)/shard_map/pallas_call | solution.py:471
Async XLA Ops:
  0.6 2.2 %copy-start.1 = (f32[8,128,512]{2,1,0:T(8,128)S(1)}, f32[8,128,512]{2,1,0:T(8,128)}, u32[]{:S(2)}) copy-start(f32[8,128,512]{2,1,0:T(8,128)} %v_ref.5) | copy-start | bytes 6291460
  0.6 2.7 %copy-start = (f32[8,128,512]{2,1,0:T(8,128)S(1)}, f32[8,128,512]{2,1,0:T(8,128)}, u32[]{:S(2)}) copy-start(f32[8,128,512]{2,1,0:T(8,128)} %u_ref.5) | copy-start | bytes 6291460
  4.0 8.1 %collective-permute-start = (f32[9,24,128]{2,1,0:T(8,128)S(1)}, f32[9,24,128]{2,1,0:T(8,128)S(1)}, u32[]{:S(2)}, u32[]{:S(2)}) collective-permute-start(f32[9,24,128]{2,1,0:T(8,128)S(1)} %get-tuple-element.30.xe_own), channel_id=1, source_target_pairs={{0,4},{4,0},{8,12},{12,8},{16,20},{20,16},{24,28},{28,24},{1,5},{5... | collective-permute-start | bytes 331784 | tf_op jit(solution)/shard_map/ppermute | solution.py:519
  4.5 13.9 %collective-permute-start.1 = (f32[8,24,128]{2,1,0:T(8,128)S(1)}, f32[8,24,128]{2,1,0:T(8,128)S(1)}, u32[]{:S(2)}, u32[]{:S(2)}) collective-permute-start(f32[8,24,128]{2,1,0:T(8,128)S(1)} %get-tuple-element.31.xo_own), channel_id=1, source_target_pairs={{0,28},{4,8},{8,4},{12,16},{16,12},{20,24},{24,20},{28,0},{1,29},{... | collective-permute-start | bytes 294920 | tf_op jit(solution)/shard_map/ppermute | solution.py:519
  8.1 4.0 %collective-permute-start.2 = (f32[24,128]{1,0:T(8,128)S(1)}, f32[24,128]{1,0:T(8,128)S(1)}, u32[]{:S(2)}, u32[]{:S(2)}) collective-permute-start(f32[24,128]{1,0:T(8,128)S(1)} %get-tuple-element.33.own_o), channel_id=1, source_target_pairs={{0,28},{4,8},{8,4},{12,16},{16,12},{20,24},{24,20},{28,0},{1,29},{... | collective-permute-start | bytes 36872 | tf_op jit(solution)/shard_map/ppermute | solution.py:510
  12.2 6.2 %collective-permute-start.3 = (f32[56,128]{1,0:T(8,128)S(1)}, f32[56,128]{1,0:T(8,128)S(1)}, u32[]{:S(2)}, u32[]{:S(2)}) collective-permute-start(f32[56,128]{1,0:T(8,128)S(1)} %get-tuple-element.34.ye_own), channel_id=1, source_target_pairs={{0,1},{1,0},{2,3},{3,2},{4,5},{5,4},{6,7},{7,6},{8,9},{9,8},{10,11... | collective-permute-start | bytes 86024 | tf_op jit(solution)/shard_map/ppermute | solution.py:529
  13.9 5.7 %collective-permute-start.4 = (f32[56,128]{1,0:T(8,128)S(1)}, f32[56,128]{1,0:T(8,128)S(1)}, u32[]{:S(2)}, u32[]{:S(2)}) collective-permute-start(f32[56,128]{1,0:T(8,128)S(1)} %get-tuple-element.35.yo_own), channel_id=1, source_target_pairs={{0,3},{1,2},{2,1},{3,0},{4,7},{5,6},{6,5},{7,4},{8,11},{9,10},{10,... | collective-permute-start | bytes 86024 | tf_op jit(solution)/shard_map/ppermute | solution.py:529

commit v6 on v5

--- a/solution.py
+++ b/solution.py
@@ -516,7 +516,8 @@
         *fine,
         *held(three, two, *message_ends, w_ends, w_rest, se),
     )
-    xe_got, xo_got = lax.ppermute(xe, "gx", even_x), lax.ppermute(xo, "gx", odd_x)
+    xo_got = lax.ppermute(xo, "gx", odd_x)
+    xe_got = lax.ppermute(xe, "gx", even_x)
     strips, *own_ends = local_call(
         ends_kernel,
         [f32((own_count, lanes))] + [bf16((own_count * levels, 2 * SIDE))] * 2,
@@ -526,7 +527,8 @@
     )
     rows = [f32((rim_rows, lanes))] * 2 + [f32((coarse, lanes))] * 3
     ye, yo = local_call(functools.partial(strip_kernel, levels), [f32(side)] * 2, rows, *held(strips, se, so, xe_got, so_got))
-    ye_got, yo_got = lax.ppermute(ye, "gy", even_y), lax.ppermute(yo, "gy", odd_y)
+    yo_got = lax.ppermute(yo, "gy", odd_y)
+    ye_got = lax.ppermute(ye, "gy", even_y)
     (partial_sums,) = local_call(
         own_kernel,
         [f32((own_count * levels, lanes))],

time: 22.9 us -> 22.9 us (level)
  no operation moved by 1% of the time
where the time goes in v6:
time: 22.9 us; the launch traced here: 22.8 us
  Pallas kernels  9.79 us (43%)
  starting transfers between devices  8.26 us (36%)
  waiting for transfers between devices  3.47 us (15%)
  between operations  0.71 us (3%)
  local copies, waits for them, and re-layouts  0.53 us (2%)
    pallas_call x6, Pallas kernels, local_call(): pl.pallas_call(body, in_specs=specs, out_specs=[in_hbm if isinstance(o, j...  9.79 us
    ppermute x1, starting transfers between devices, in_order(): xo_got = lax.ppermute(xo, 'gx', odd_x)  3.54 us
    ppermute x1, starting transfers between devices, in_order(): yo_got = lax.ppermute(yo, 'gy', odd_y)  2.47 us
    ppermute x1, waiting for transfers between devices, in_order(): so_got = lax.ppermute(so, 'gx', odd_x)  2.35 us
    ppermute x1, starting transfers between devices, in_order(): ye_got = lax.ppermute(ye, 'gy', even_y)  1.64 us
    ppermute x1, waiting for transfers between devices, in_order(): yo_got = lax.ppermute(yo, 'gy', odd_y)  1.11 us
    ppermute x1, starting transfers between devices, in_order(): xe_got = lax.ppermute(xe, 'gx', even_x)  0.56 us
    unnamed x4, local copies, waits for them, and re-layouts  0.53 us
  transfers between devices with their start and end apart: 5, of which 2 were waited for; matrix products, arithmetic and copies ran while one was open for 0% of the time, Pallas kernels for 17%

profile of v6, /device:TPU:0, one launch (start us, length us, event | category | flops | bytes accessed | tf_op | source)
XLA Modules:
  0.0 22.8 jit_solution(11294277320390865327)
XLA Ops:
  0.6 0.0 copy-start.1
  0.6 0.0 copy-start
  0.6 2.2 %shard_map.95 = (f32[24,128]{1,0:T(8,128)S(1)}, f32[24,128]{1,0:T(8,128)S(1)}, bf16[384,256]{1,0:T(8,128)(2,1)S(1)}, bf16[384,256]{1,0:T(8,128)(2,1)S(1)}, bf16[...) custom-call(f32[8,128,512]{2,1,0:T(8,128)} %u_ref.5, ...), custom_call_target="tpu_custom_call" | custom-call | tf_op jit(solution)/shard_map/pallas_call | solution.py:471
  2.8 0.0 copy-done.1
  2.8 0.5 %copy-done = f32[8,128,512]{2,1,0:T(8,128)S(1)} copy-done((f32[8,128,512]{2,1,0:T(8,128)S(1)}, f32[8,128,512]{2,1,0:T(8,128)}, u32[]{:S(2)}) %copy-start) | copy-done | bytes 2097176
  3.4 0.6 %shard_map.98 = (f32[9,24,128]{2,1,0:T(8,128)S(1)}, f32[8,24,128]{2,1,0:T(8,128)S(1)}) custom-call(f32[8,128,512]{2,1,0:T(8,128)S(1)} %copy-done, f32[8,128,512]{2,1,0:T(8,128)S(1)} %copy-done.1, bf16[2,64,256]{2,1,0:T(8,128)(2,1)S(1)} %get-tuple-element.25.three, bf16[2,32,128]{2,1,0:T(8,128)(2,1)S(1)} %get-tuple-element.26.two, ...), custom_call_target="tpu_custom_call" | custom-call | tf_op jit(solution)/shard_map/pallas_call | solution.py:471
  4.0 0.6 %collective-permute-start = (f32[9,24,128]{2,1,0:T(8,128)S(1)}, f32[9,24,128]{2,1,0:T(8,128)S(1)}, u32[]{:S(2)}, u32[]{:S(2)}) collective-permute-start(f32[9,24,128]{2,1,0:T(8,128)S(1)} %get-tuple-element.30.xe_own), channel_id=1, source_target_pairs={{0,4},{4,0},{8,12},{12,8},{16,20},{20,16},{24,28},{28,24},{1,5},{5... | collective-permute-start | bytes 331784 | tf_op jit(solution)/shard_map/ppermute | solution.py:520
  4.5 3.5 %collective-permute-start.1 = (f32[8,24,128]{2,1,0:T(8,128)S(1)}, f32[8,24,128]{2,1,0:T(8,128)S(1)}, u32[]{:S(2)}, u32[]{:S(2)}) collective-permute-start(f32[8,24,128]{2,1,0:T(8,128)S(1)} %get-tuple-element.31.xo_own), channel_id=1, source_target_pairs={{0,28},{4,8},{8,4},{12,16},{16,12},{20,24},{24,20},{28,0},{1,29},{... | collective-permute-start | bytes 294920 | tf_op jit(solution)/shard_map/ppermute | solution.py:519
  8.1 0.0 collective-permute-start.2
  8.1 1.6 %shard_map.96 = (f32[160,128]{1,0:T(8,128)S(1)}, bf16[1280,256]{1,0:T(8,128)(2,1)S(1)}, bf16[1280,256]{1,0:T(8,128)(2,1)S(1)}) custom-call(f32[8,128,512]{2,1,0:T(8,128)S(1)} %copy-done, f32[8,128,512]{2,1,0:T(8,128)S(1)} %copy-done.1, bf16[64,256]{1,0:T(8,128)(2,1)S(1)} %get-tuple-element.19.left, bf16[256,256]{1,0:T(8,128)(2,1)S(1)} %get-tuple-element.20.weights), custom_call_target="tpu_custom_call" | custom-call | tf_op jit(solution)/shard_map/pallas_call | solution.py:471
  9.7 2.3 %collective-permute-done.2.got_o = f32[24,128]{1,0:T(8,128)S(1)} collective-permute-done((f32[24,128]{1,0:T(8,128)S(1)}, f32[24,128]{1,0:T(8,128)S(1)}, u32[]{:S(2)}, u32[]{:S(2)}) %collective-permute-start.2) | collective-permute-done | bytes 12320 | tf_op jit(solution)/shard_map/ppermute | solution.py:510
  12.1 0.0 collective-permute-done.got_e.xe_got
  12.1 0.1 shard_map.99
  12.2 1.6 %collective-permute-start.3 = (f32[56,128]{1,0:T(8,128)S(1)}, f32[56,128]{1,0:T(8,128)S(1)}, u32[]{:S(2)}, u32[]{:S(2)}) collective-permute-start(f32[56,128]{1,0:T(8,128)S(1)} %get-tuple-element.34.ye_own), channel_id=1, source_target_pairs={{0,1},{1,0},{2,3},{3,2},{4,5},{5,4},{6,7},{7,6},{8,9},{9,8},{10,11... | collective-permute-start | bytes 86024 | tf_op jit(solution)/shard_map/ppermute | solution.py:531
  13.9 2.5 %collective-permute-start.4 = (f32[56,128]{1,0:T(8,128)S(1)}, f32[56,128]{1,0:T(8,128)S(1)}, u32[]{:S(2)}, u32[]{:S(2)}) collective-permute-start(f32[56,128]{1,0:T(8,128)S(1)} %get-tuple-element.35.yo_own), channel_id=1, source_target_pairs={{0,3},{1,2},{2,1},{3,0},{4,7},{5,6},{6,5},{7,4},{8,11},{9,10},{10,... | collective-permute-start | bytes 86024 | tf_op jit(solution)/shard_map/ppermute | solution.py:530
  16.3 2.1 %shard_map.97.p_ref = f32[1280,128]{1,0:T(8,128)S(1)} custom-call(f32[8,128,512]{2,1,0:T(8,128)S(1)} %copy-done, f32[8,128,512]{2,1,0:T(8,128)S(1)} %copy-done.1, bf16[64,256]{1,0:T(8,128)(2,1)S(1)} %get-tuple-element.19.left, bf16[1280,256]{1,0:T(8,128)(2,1)S(1)} %get-tuple-element.21.ends_high, bf16[1280,256]{1,0:T(8,128)(2,1)S(1)} %get-tuple-element.22.ends_low, ...), custom_call_target="tpu_custom_call" | custom-call | tf_op jit(solution)/shard_map/pallas_call | solution.py:471
  18.4 0.0 collective-permute-done.1.xo_got
  18.4 0.0 collective-permute-done.3.ye_got
  18.4 1.1 %collective-permute-done.4.yo_got = f32[56,128]{1,0:T(8,128)S(1)} collective-permute-done((f32[56,128]{1,0:T(8,128)S(1)}, f32[56,128]{1,0:T(8,128)S(1)}, u32[]{:S(2)}, u32[]{:S(2)}) %collective-permute-start.4) | collective-permute-done | bytes 28704 | tf_op jit(solution)/shard_map/ppermute | solution.py:530
  19.5 3.2 %shard_map.100 = (f32[3,8,32,128]{3,2,1,0:T(8,128)}, f32[48,8,32,128]{3,2,1,0:T(8,128)}) custom-call(f32[1280,128]{1,0:T(8,128)S(1)} %shard_map.97.p_ref, f32[9,24,128]{2,1,0:T(8,128)S(1)} %get-tuple-element.30.xe_own, f32[8,24,128]{2,1,0:T(8,128)S(1)} %get-tuple-element.31.xo_own, f32[9,24,128]{2,1,0:T(8,128)S(1)} %collective-permute-done.got_e.xe_got, ...), custom_call_target="tpu_custom_call" | custom-call | tf_op jit(solution)/shard_map/pallas_call | solution.py:471
Async XLA Ops:
  0.6 2.2 %copy-start.1 = (f32[8,128,512]{2,1,0:T(8,128)S(1)}, f32[8,128,512]{2,1,0:T(8,128)}, u32[]{:S(2)}) copy-start(f32[8,128,512]{2,1,0:T(8,128)} %v_ref.5) | copy-start | bytes 6291460
  0.6 2.7 %copy-start = (f32[8,128,512]{2,1,0:T(8,128)S(1)}, f32[8,128,512]{2,1,0:T(8,128)}, u32[]{:S(2)}) copy-start(f32[8,128,512]{2,1,0:T(8,128)} %u_ref.5) | copy-start | bytes 6291460
  4.0 8.1 %collective-permute-start = (f32[9,24,128]{2,1,0:T(8,128)S(1)}, f32[9,24,128]{2,1,0:T(8,128)S(1)}, u32[]{:S(2)}, u32[]{:S(2)}) collective-permute-start(f32[9,24,128]{2,1,0:T(8,128)S(1)} %get-tuple-element.30.xe_own), channel_id=1, source_target_pairs={{0,4},{4,0},{8,12},{12,8},{16,20},{20,16},{24,28},{28,24},{1,5},{5... | collective-permute-start | bytes 331784 | tf_op jit(solution)/shard_map/ppermute | solution.py:520
  4.5 13.9 %collective-permute-start.1 = (f32[8,24,128]{2,1,0:T(8,128)S(1)}, f32[8,24,128]{2,1,0:T(8,128)S(1)}, u32[]{:S(2)}, u32[]{:S(2)}) collective-permute-start(f32[8,24,128]{2,1,0:T(8,128)S(1)} %get-tuple-element.31.xo_own), channel_id=1, source_target_pairs={{0,28},{4,8},{8,4},{12,16},{16,12},{20,24},{24,20},{28,0},{1,29},{... | collective-permute-start | bytes 294920 | tf_op jit(solution)/shard_map/ppermute | solution.py:519
  8.1 4.0 %collective-permute-start.2 = (f32[24,128]{1,0:T(8,128)S(1)}, f32[24,128]{1,0:T(8,128)S(1)}, u32[]{:S(2)}, u32[]{:S(2)}) collective-permute-start(f32[24,128]{1,0:T(8,128)S(1)} %get-tuple-element.33.own_o), channel_id=1, source_target_pairs={{0,28},{4,8},{8,4},{12,16},{16,12},{20,24},{24,20},{28,0},{1,29},{... | collective-permute-start | bytes 36872 | tf_op jit(solution)/shard_map/ppermute | solution.py:510
  12.2 6.2 %collective-permute-start.3 = (f32[56,128]{1,0:T(8,128)S(1)}, f32[56,128]{1,0:T(8,128)S(1)}, u32[]{:S(2)}, u32[]{:S(2)}) collective-permute-start(f32[56,128]{1,0:T(8,128)S(1)} %get-tuple-element.34.ye_own), channel_id=1, source_target_pairs={{0,1},{1,0},{2,3},{3,2},{4,5},{5,4},{6,7},{7,6},{8,9},{9,8},{10,11... | collective-permute-start | bytes 86024 | tf_op jit(solution)/shard_map/ppermute | solution.py:531
  13.9 5.7 %collective-permute-start.4 = (f32[56,128]{1,0:T(8,128)S(1)}, f32[56,128]{1,0:T(8,128)S(1)}, u32[]{:S(2)}, u32[]{:S(2)}) collective-permute-start(f32[56,128]{1,0:T(8,128)S(1)} %get-tuple-element.35.yo_own), channel_id=1, source_target_pairs={{0,3},{1,2},{2,1},{3,0},{4,7},{5,6},{6,5},{7,4},{8,11},{9,10},{10,... | collective-permute-start | bytes 86024 | tf_op jit(solution)/shard_map/ppermute | solution.py:530

commit v7 on v6

--- a/solution.py
+++ b/solution.py
@@ -21,7 +21,7 @@
 MSG = 24
 F32, BF16 = jnp.float32, jnp.bfloat16
 VMEM_BYTES = 24 << 20
-MAIN_UNROLL, OWN_UNROLL, FINAL_UNROLL = 8, 8, 1
+MAIN_UNROLL, FINAL_UNROLL = 8, 1
 
 
 def taps(cells, count_in):
@@ -241,39 +241,63 @@
     return split(jnp.concatenate([row_sums(left, f) for f in products(u, v)], 0))
 
 
-def ends_kernel(u_ref, v_ref, left, weights, s_ref, x_high, x_low):
+def ends_kernel(u_ref, v_ref, left, weights, s_ref, x_high, x_low, y_high, y_low):
     levels, _, count_y = u_ref.shape
     rows, lanes = s_ref.shape
 
+    few = levels - x_high.shape[0] // rows
+    lane = lax.broadcasted_iota(jnp.int32, (u_ref.shape[1], SIDE), 1)
     for level in range(levels):
-        u, v = (
-            jnp.concatenate([r[level, :, :SIDE], r[level, :, count_y - SIDE :]], 1) for r in (u_ref, v_ref)
-        )
-        at = slice(level * rows, (level + 1) * rows)
-        x_high[at], x_low[at] = own_rows_of(left[...], u, v)
+        ends = [(r[level, :, :SIDE], r[level, :, count_y - SIDE :]) for r in (u_ref, v_ref)]
+        if level < few:
+            u, v = (jnp.where(lane < HALF, first, last) for first, last in ends)
+            at = slice(level * rows, (level + 1) * rows)
+            y_high[at], y_low[at] = own_rows_of(left[...], u, v)
+        else:
+            u, v = (jnp.concatenate(pair, 1) for pair in ends)
+            at = slice((level - few) * rows, (level - few + 1) * rows)
+            x_high[at], x_low[at] = own_rows_of(left[...], u, v)
+    packed_weights = jnp.concatenate([weights[:HALF], weights[2 * SIDE - HALF :]], 0)
     wide = rows // 5 * 2
     strips, short = jnp.zeros((wide, lanes), F32), jnp.zeros((rows - wide, lanes), F32)
     for level in range(levels):
-        at = slice(level * rows, (level + 1) * rows)
-        sums = column_sums(x_high[at], x_low[at], weights)
+        if level < few:
+            at = slice(level * rows, (level + 1) * rows)
+            sums = column_sums(y_high[at], y_low[at], packed_weights)
+        else:
+            at = slice((level - few) * rows, (level - few + 1) * rows)
+            sums = column_sums(x_high[at], x_low[at], weights)
         strips = strips + pltpu.roll(sums[:wide], WIDE * level, 1)
         short = short + pltpu.roll(short_only(sums[wide:]), EXT * level, 1)
     s_ref[:wide] = strips
     s_ref[wide:] = short
 
 
-def own_kernel(u_ref, v_ref, left, ends_high, ends_low, w_ends, w_rest, p_ref, x_high, x_low):
-    levels = u_ref.shape[0]
+def own_kernel(
+    u_ref, v_ref, left, ends_high, ends_low, w_ends, w_rest, p_ref, x_high, x_low, y_high, y_low
+):
+    levels, _, count_y = u_ref.shape
     rows = p_ref.shape[0] // levels
-
-    def rows_of(level):
-        at = pl.ds(pl.multiple_of(level * rows, 16), rows)
-        x_high[at], x_low[at] = own_rows_of(left[...], u_ref[level, :, middle(u_ref)], v_ref[level, :, middle(v_ref)])
-
-    each(levels, OWN_UNROLL, rows_of)
+    few = y_high.shape[0] // rows
+    for level in range(levels):
+        at = slice(level * rows, (level + 1) * rows)
+        if level < few:
+            high, low = own_rows_of(left[...], u_ref[level], v_ref[level])
+            for whole, rest, ends in ((high, x_high, y_high), (low, x_low, y_low)):
+                rest[at] = whole[:, SIDE : count_y - SIDE]
+                ends[at] = jnp.concatenate([whole[:, :SIDE], whole[:, count_y - SIDE :]], 1)
+        else:
+            x_high[at], x_low[at] = own_rows_of(
+                left[...], u_ref[level, :, middle(u_ref)], v_ref[level, :, middle(v_ref)]
+            )
     for level in range(0, levels, 2):
         at = slice(level * rows, (level + 2) * rows)
-        p_ref[at] = column_sums(ends_high[at], ends_low[at], w_ends) + column_sums(x_high[at], x_low[at], w_rest)
+        if level < few:
+            ends = column_sums(y_high[at], y_low[at], w_ends)
+        else:
+            kept = slice((level - few) * rows, (level - few + 2) * rows)
+            ends = column_sums(ends_high[kept], ends_low[kept], w_ends)
+        p_ref[at] = ends + column_sums(x_high[at], x_low[at], w_rest)
 
 
 def low_and_high(odd, e, o):
@@ -496,7 +520,7 @@
         return [(a, True) for a in arrays]
 
     (even_x, odd_x), (even_y, odd_y) = pairs_of("gx"), pairs_of("gy")
-    parts = 1
+    parts, few = 1, levels // 4 * 3
     consts = (three, two, w_strips, w_ends, w_rest, left)
     se, so, ends_high, ends_low, *kept = local_call(
         slab_kernel,
@@ -520,8 +544,8 @@
     xe_got = lax.ppermute(xe, "gx", even_x)
     strips, *own_ends = local_call(
         ends_kernel,
-        [f32((own_count, lanes))] + [bf16((own_count * levels, 2 * SIDE))] * 2,
-        [],
+        [f32((own_count, lanes))] + [bf16((own_count * (levels - few), 2 * SIDE))] * 2,
+        [bf16((own_count * few, SIDE))] * 2,
         *fine,
         *held(left, w_strips),
     )
@@ -532,7 +556,7 @@
     (partial_sums,) = local_call(
         own_kernel,
         [f32((own_count * levels, lanes))],
-        [bf16((own_count * levels, count_y - 2 * SIDE))] * 2,
+        [bf16((own_count * levels, count_y - 2 * SIDE))] * 2 + [bf16((own_count * few, 2 * SIDE))] * 2,
         *fine,
         *held(left, *own_ends, w_ends, w_rest),
     )

time: 22.9 us -> 22.9 us (level)
  Pallas kernels: 9.79 us -> 10.4 us
  waiting for transfers between devices: 3.47 us -> 2.9 us
    ppermute x1, waiting for transfers between devices: 1.11 us -> 0.1 us  [in_order(): yo_got = lax.ppermute(yo, 'gy', odd_y)]
    pallas_call x6, Pallas kernels: 9.79 us -> 10.4 us  [local_call(): pl.pallas_call(body, in_specs=specs, out_specs=[in_hbm if isinstance(o, j...]
    ppermute x1, waiting for transfers between devices: 2.35 us -> 2.79 us  [in_order(): so_got = lax.ppermute(so, 'gx', odd_x)]
  transfers between devices with their start and end apart: 5 -> 5, of which waited for: 2 -> 2; matrix products, arithmetic and copies ran while one was open for 0% -> 0% of each run, Pallas kernels for 17% -> 19%
where the time goes in v7:
time: 22.9 us; the launch traced here: 22.8 us
  Pallas kernels  10.4 us (45%)
  starting transfers between devices  8.26 us (36%)
  waiting for transfers between devices  2.9 us (13%)
  between operations  0.71 us (3%)
  local copies, waits for them, and re-layouts  0.53 us (2%)
    pallas_call x6, Pallas kernels, local_call(): pl.pallas_call(body, in_specs=specs, out_specs=[in_hbm if isinstance(o, j...  10.4 us
    ppermute x1, starting transfers between devices, in_order(): xo_got = lax.ppermute(xo, 'gx', odd_x)  3.54 us
    ppermute x1, waiting for transfers between devices, in_order(): so_got = lax.ppermute(so, 'gx', odd_x)  2.79 us
    ppermute x1, starting transfers between devices, in_order(): yo_got = lax.ppermute(yo, 'gy', odd_y)  2.47 us
    ppermute x1, starting transfers between devices, in_order(): ye_got = lax.ppermute(ye, 'gy', even_y)  1.65 us
    ppermute x1, starting transfers between devices, in_order(): xe_got = lax.ppermute(xe, 'gx', even_x)  0.56 us
    unnamed x4, local copies, waits for them, and re-layouts  0.53 us
  transfers between devices with their start and end apart: 5, of which 2 were waited for; matrix products, arithmetic and copies ran while one was open for 0% of the time, Pallas kernels for 19%

profile of v7, /device:TPU:0, one launch (start us, length us, event | category | flops | bytes accessed | tf_op | source)
XLA Modules:
  0.0 22.8 jit_solution(3192543563749936873)
XLA Ops:
  0.6 0.0 copy-start.1
  0.6 0.0 copy-start
  0.6 2.2 %shard_map.95 = (f32[24,128]{1,0:T(8,128)S(1)}, f32[24,128]{1,0:T(8,128)S(1)}, bf16[384,256]{1,0:T(8,128)(2,1)S(1)}, bf16[384,256]{1,0:T(8,128)(2,1)S(1)}, bf16[...) custom-call(f32[8,128,512]{2,1,0:T(8,128)} %u_ref.5, ...), custom_call_target="tpu_custom_call" | custom-call | tf_op jit(solution)/shard_map/pallas_call | solution.py:495
  2.8 0.0 copy-done.1
  2.8 0.5 %copy-done = f32[8,128,512]{2,1,0:T(8,128)S(1)} copy-done((f32[8,128,512]{2,1,0:T(8,128)S(1)}, f32[8,128,512]{2,1,0:T(8,128)}, u32[]{:S(2)}) %copy-start) | copy-done | bytes 2097176
  3.4 0.6 %shard_map.98 = (f32[9,24,128]{2,1,0:T(8,128)S(1)}, f32[8,24,128]{2,1,0:T(8,128)S(1)}) custom-call(f32[8,128,512]{2,1,0:T(8,128)S(1)} %copy-done, f32[8,128,512]{2,1,0:T(8,128)S(1)} %copy-done.1, bf16[2,64,256]{2,1,0:T(8,128)(2,1)S(1)} %get-tuple-element.25.three, bf16[2,32,128]{2,1,0:T(8,128)(2,1)S(1)} %get-tuple-element.26.two, ...), custom_call_target="tpu_custom_call" | custom-call | tf_op jit(solution)/shard_map/pallas_call | solution.py:495
  4.0 0.6 %collective-permute-start = (f32[9,24,128]{2,1,0:T(8,128)S(1)}, f32[9,24,128]{2,1,0:T(8,128)S(1)}, u32[]{:S(2)}, u32[]{:S(2)}) collective-permute-start(f32[9,24,128]{2,1,0:T(8,128)S(1)} %get-tuple-element.30.xe_own), channel_id=1, source_target_pairs={{0,4},{4,0},{8,12},{12,8},{16,20},{20,16},{24,28},{28,24},{1,5},{5... | collective-permute-start | bytes 331784 | tf_op jit(solution)/shard_map/ppermute | solution.py:544
  4.5 3.5 %collective-permute-start.1 = (f32[8,24,128]{2,1,0:T(8,128)S(1)}, f32[8,24,128]{2,1,0:T(8,128)S(1)}, u32[]{:S(2)}, u32[]{:S(2)}) collective-permute-start(f32[8,24,128]{2,1,0:T(8,128)S(1)} %get-tuple-element.31.xo_own), channel_id=1, source_target_pairs={{0,28},{4,8},{8,4},{12,16},{16,12},{20,24},{24,20},{28,0},{1,29},{... | collective-permute-start | bytes 294920 | tf_op jit(solution)/shard_map/ppermute | solution.py:543
  8.1 0.0 collective-permute-start.2
  8.1 1.2 %shard_map.96 = (f32[160,128]{1,0:T(8,128)S(1)}, bf16[320,256]{1,0:T(8,128)(2,1)S(1)}, bf16[320,256]{1,0:T(8,128)(2,1)S(1)}) custom-call(f32[8,128,512]{2,1,0:T(8,128)S(1)} %copy-done, f32[8,128,512]{2,1,0:T(8,128)S(1)} %copy-done.1, bf16[64,256]{1,0:T(8,128)(2,1)S(1)} %get-tuple-element.19.left, bf16[256,256]{1,0:T(8,128)(2,1)S(1)} %get-tuple-element.20.weights), custom_call_target="tpu_custom_call" | custom-call | tf_op jit(solution)/shard_map/pallas_call | solution.py:495
  9.3 2.8 %collective-permute-done.2.got_o = f32[24,128]{1,0:T(8,128)S(1)} collective-permute-done((f32[24,128]{1,0:T(8,128)S(1)}, f32[24,128]{1,0:T(8,128)S(1)}, u32[]{:S(2)}, u32[]{:S(2)}) %collective-permute-start.2) | collective-permute-done | bytes 12320 | tf_op jit(solution)/shard_map/ppermute | solution.py:534
  12.1 0.0 collective-permute-done.got_e.xe_got
  12.1 0.1 shard_map.99
  12.2 1.6 %collective-permute-start.3 = (f32[56,128]{1,0:T(8,128)S(1)}, f32[56,128]{1,0:T(8,128)S(1)}, u32[]{:S(2)}, u32[]{:S(2)}) collective-permute-start(f32[56,128]{1,0:T(8,128)S(1)} %get-tuple-element.34.ye_own), channel_id=1, source_target_pairs={{0,1},{1,0},{2,3},{3,2},{4,5},{5,4},{6,7},{7,6},{8,9},{9,8},{10,11... | collective-permute-start | bytes 86024 | tf_op jit(solution)/shard_map/ppermute | solution.py:555
  13.9 2.5 %collective-permute-start.4 = (f32[56,128]{1,0:T(8,128)S(1)}, f32[56,128]{1,0:T(8,128)S(1)}, u32[]{:S(2)}, u32[]{:S(2)}) collective-permute-start(f32[56,128]{1,0:T(8,128)S(1)} %get-tuple-element.35.yo_own), channel_id=1, source_target_pairs={{0,3},{1,2},{2,1},{3,0},{4,7},{5,6},{6,5},{7,4},{8,11},{9,10},{10,... | collective-permute-start | bytes 86024 | tf_op jit(solution)/shard_map/ppermute | solution.py:554
  16.3 3.1 %shard_map.97.p_ref = f32[1280,128]{1,0:T(8,128)S(1)} custom-call(f32[8,128,512]{2,1,0:T(8,128)S(1)} %copy-done, f32[8,128,512]{2,1,0:T(8,128)S(1)} %copy-done.1, bf16[64,256]{1,0:T(8,128)(2,1)S(1)} %get-tuple-element.19.left, bf16[320,256]{1,0:T(8,128)(2,1)S(1)} %get-tuple-element.21.ends_high, bf16[320,256]{1,0:T(8,128)(2,1)S(1)} %get-tuple-element.22.ends_low, ...), custom_call_target="tpu_custom_call" | custom-call | tf_op jit(solution)/shard_map/pallas_call | solution.py:495
  19.4 0.0 collective-permute-done.1.xo_got
  19.4 0.0 collective-permute-done.3.ye_got
  19.4 0.1 collective-permute-done.4.yo_got
  19.5 3.2 %shard_map.100 = (f32[3,8,32,128]{3,2,1,0:T(8,128)}, f32[48,8,32,128]{3,2,1,0:T(8,128)}) custom-call(f32[1280,128]{1,0:T(8,128)S(1)} %shard_map.97.p_ref, f32[9,24,128]{2,1,0:T(8,128)S(1)} %get-tuple-element.30.xe_own, f32[8,24,128]{2,1,0:T(8,128)S(1)} %get-tuple-element.31.xo_own, f32[9,24,128]{2,1,0:T(8,128)S(1)} %collective-permute-done.got_e.xe_got, ...), custom_call_target="tpu_custom_call" | custom-call | tf_op jit(solution)/shard_map/pallas_call | solution.py:495
Async XLA Ops:
  0.6 2.2 %copy-start.1 = (f32[8,128,512]{2,1,0:T(8,128)S(1)}, f32[8,128,512]{2,1,0:T(8,128)}, u32[]{:S(2)}) copy-start(f32[8,128,512]{2,1,0:T(8,128)} %v_ref.5) | copy-start | bytes 6291460
  0.6 2.7 %copy-start = (f32[8,128,512]{2,1,0:T(8,128)S(1)}, f32[8,128,512]{2,1,0:T(8,128)}, u32[]{:S(2)}) copy-start(f32[8,128,512]{2,1,0:T(8,128)} %u_ref.5) | copy-start | bytes 6291460
  4.0 8.1 %collective-permute-start = (f32[9,24,128]{2,1,0:T(8,128)S(1)}, f32[9,24,128]{2,1,0:T(8,128)S(1)}, u32[]{:S(2)}, u32[]{:S(2)}) collective-permute-start(f32[9,24,128]{2,1,0:T(8,128)S(1)} %get-tuple-element.30.xe_own), channel_id=1, source_target_pairs={{0,4},{4,0},{8,12},{12,8},{16,20},{20,16},{24,28},{28,24},{1,5},{5... | collective-permute-start | bytes 331784 | tf_op jit(solution)/shard_map/ppermute | solution.py:544
  4.5 14.9 %collective-permute-start.1 = (f32[8,24,128]{2,1,0:T(8,128)S(1)}, f32[8,24,128]{2,1,0:T(8,128)S(1)}, u32[]{:S(2)}, u32[]{:S(2)}) collective-permute-start(f32[8,24,128]{2,1,0:T(8,128)S(1)} %get-tuple-element.31.xo_own), channel_id=1, source_target_pairs={{0,28},{4,8},{8,4},{12,16},{16,12},{20,24},{24,20},{28,0},{1,29},{... | collective-permute-start | bytes 294920 | tf_op jit(solution)/shard_map/ppermute | solution.py:543
  8.1 4.0 %collective-permute-start.2 = (f32[24,128]{1,0:T(8,128)S(1)}, f32[24,128]{1,0:T(8,128)S(1)}, u32[]{:S(2)}, u32[]{:S(2)}) collective-permute-start(f32[24,128]{1,0:T(8,128)S(1)} %get-tuple-element.33.own_o), channel_id=1, source_target_pairs={{0,28},{4,8},{8,4},{12,16},{16,12},{20,24},{24,20},{28,0},{1,29},{... | collective-permute-start | bytes 36872 | tf_op jit(solution)/shard_map/ppermute | solution.py:534
  12.2 7.2 %collective-permute-start.3 = (f32[56,128]{1,0:T(8,128)S(1)}, f32[56,128]{1,0:T(8,128)S(1)}, u32[]{:S(2)}, u32[]{:S(2)}) collective-permute-start(f32[56,128]{1,0:T(8,128)S(1)} %get-tuple-element.34.ye_own), channel_id=1, source_target_pairs={{0,1},{1,0},{2,3},{3,2},{4,5},{5,4},{6,7},{7,6},{8,9},{9,8},{10,11... | collective-permute-start | bytes 86024 | tf_op jit(solution)/shard_map/ppermute | solution.py:555
  13.9 5.7 %collective-permute-start.4 = (f32[56,128]{1,0:T(8,128)S(1)}, f32[56,128]{1,0:T(8,128)S(1)}, u32[]{:S(2)}, u32[]{:S(2)}) collective-permute-start(f32[56,128]{1,0:T(8,128)S(1)} %get-tuple-element.35.yo_own), channel_id=1, source_target_pairs={{0,3},{1,2},{2,1},{3,0},{4,7},{5,6},{6,5},{7,4},{8,11},{9,10},{10,... | collective-permute-start | bytes 86024 | tf_op jit(solution)/shard_map/ppermute | solution.py:554

commit v8 on v6

--- a/solution.py
+++ b/solution.py
@@ -21,7 +21,7 @@
 MSG = 24
 F32, BF16 = jnp.float32, jnp.bfloat16
 VMEM_BYTES = 24 << 20
-MAIN_UNROLL, OWN_UNROLL, FINAL_UNROLL = 8, 8, 1
+MAIN_UNROLL, FINAL_UNROLL = 8, 1
 
 
 def taps(cells, count_in):
@@ -216,7 +216,7 @@
 
 
 def main_kernel(
-    u_ref, v_ref, three, two, ends_high, ends_low, w_ends, w_rest, slab_ref, e_ref, o_ref, x_high, x_low
+    u_ref, v_ref, three, two, ends_high, ends_low, w_ends, w_rest, e_ref, o_ref, x_high, x_low
 ):
     odd = lax.rem(lax.axis_index("gx"), 2)
     levels, count_x = u_ref.shape[:2]
@@ -234,7 +234,6 @@
     for place, ref in ((0, e_ref), (8, o_ref)):
         for level in range(levels):
             ref[level] = message_of(sums, level, place)
-    e_ref[levels] = slab_ref[...]
 
 
 def own_rows_of(left, u, v):
@@ -242,38 +241,37 @@
 
 
 def ends_kernel(u_ref, v_ref, left, weights, s_ref, x_high, x_low):
-    levels, _, count_y = u_ref.shape
+    levels, count_x, count_y = u_ref.shape
     rows, lanes = s_ref.shape
-
+    lane = lax.broadcasted_iota(jnp.int32, (count_x, SIDE), 1)
     for level in range(levels):
         u, v = (
-            jnp.concatenate([r[level, :, :SIDE], r[level, :, count_y - SIDE :]], 1) for r in (u_ref, v_ref)
+            jnp.where(lane < HALF, r[level, :, :SIDE], r[level, :, count_y - SIDE :]) for r in (u_ref, v_ref)
         )
         at = slice(level * rows, (level + 1) * rows)
         x_high[at], x_low[at] = own_rows_of(left[...], u, v)
+    read = jnp.concatenate([weights[:HALF], weights[2 * SIDE - HALF :]], 0)
     wide = rows // 5 * 2
     strips, short = jnp.zeros((wide, lanes), F32), jnp.zeros((rows - wide, lanes), F32)
     for level in range(levels):
         at = slice(level * rows, (level + 1) * rows)
-        sums = column_sums(x_high[at], x_low[at], weights)
+        sums = column_sums(x_high[at], x_low[at], read)
         strips = strips + pltpu.roll(sums[:wide], WIDE * level, 1)
         short = short + pltpu.roll(short_only(sums[wide:]), EXT * level, 1)
     s_ref[:wide] = strips
     s_ref[wide:] = short
 
 
-def own_kernel(u_ref, v_ref, left, ends_high, ends_low, w_ends, w_rest, p_ref, x_high, x_low):
+def own_kernel(u_ref, v_ref, left, w_ends, w_rest, p_ref, x_high, x_low):
     levels = u_ref.shape[0]
     rows = p_ref.shape[0] // levels
-
-    def rows_of(level):
-        at = pl.ds(pl.multiple_of(level * rows, 16), rows)
-        x_high[at], x_low[at] = own_rows_of(left[...], u_ref[level, :, middle(u_ref)], v_ref[level, :, middle(v_ref)])
-
-    each(levels, OWN_UNROLL, rows_of)
+    for level in range(levels):
+        at = slice(level * rows, (level + 1) * rows)
+        x_high[at], x_low[at] = own_rows_of(left[...], u_ref[level], v_ref[level])
+    weights = jnp.concatenate([w_ends[:SIDE], w_rest[...], w_ends[SIDE:]], 0)
     for level in range(0, levels, 2):
         at = slice(level * rows, (level + 2) * rows)
-        p_ref[at] = column_sums(ends_high[at], ends_low[at], w_ends) + column_sums(x_high[at], x_low[at], w_rest)
+        p_ref[at] = column_sums(x_high[at], x_low[at], weights)
 
 
 def low_and_high(odd, e, o):
@@ -312,7 +310,7 @@
     uvs[...] = s_ref[3 * coarse : 4 * coarse]
     vvs[...] = s_ref[4 * coarse : 5 * coarse]
     own_low, own_high = low_and_high(odd_x, own_e[...], own_o[...])
-    got_low, got_high = low_and_high(odd_x, got_e[got_e.shape[0] - 1], got_o[...])
+    got_low, got_high = low_and_high(odd_x, got_e[...], got_o[...])
     add_rows((us, vs), (uus, uvs, vvs), own_low, own_high, got_low, got_high)
     start = e_ref.shape[0] - coarse // 2
     lanes = e_ref.shape[1]
@@ -508,33 +506,30 @@
     message_ends = (ends_high, ends_low)
     three, two, w_strips, w_ends, w_rest, left = kept
     so_got = lax.ppermute(so, "gx", odd_x)
+    se_got = lax.ppermute(se, "gx", even_x)
     fine = held(east_flow, north_flow)
     xe, xo = local_call(
         main_kernel,
-        [f32((levels + 1, MSG, lanes)), f32((levels, MSG, lanes))],
+        [f32((levels, MSG, lanes))] * 2,
         [bf16((48 * levels, count_y - 2 * SIDE))] * 2,
         *fine,
-        *held(three, two, *message_ends, w_ends, w_rest, se),
+        *held(three, two, *message_ends, w_ends, w_rest),
     )
     xo_got = lax.ppermute(xo, "gx", odd_x)
     xe_got = lax.ppermute(xe, "gx", even_x)
-    strips, *own_ends = local_call(
-        ends_kernel,
-        [f32((own_count, lanes))] + [bf16((own_count * levels, 2 * SIDE))] * 2,
-        [],
-        *fine,
-        *held(left, w_strips),
+    (strips,) = local_call(
+        ends_kernel, [f32((own_count, lanes))], [bf16((own_count * levels, SIDE))] * 2, *fine, *held(left, w_strips)
     )
     rows = [f32((rim_rows, lanes))] * 2 + [f32((coarse, lanes))] * 3
-    ye, yo = local_call(functools.partial(strip_kernel, levels), [f32(side)] * 2, rows, *held(strips, se, so, xe_got, so_got))
+    ye, yo = local_call(functools.partial(strip_kernel, levels), [f32(side)] * 2, rows, *held(strips, se, so, se_got, so_got))
     yo_got = lax.ppermute(yo, "gy", odd_y)
     ye_got = lax.ppermute(ye, "gy", even_y)
     (partial_sums,) = local_call(
         own_kernel,
         [f32((own_count * levels, lanes))],
-        [bf16((own_count * levels, count_y - 2 * SIDE))] * 2,
+        [bf16((own_count * levels, count_y))] * 2,
         *fine,
-        *held(left, *own_ends, w_ends, w_rest),
+        *held(left, w_ends, w_rest),
     )
     outs = [jax.ShapeDtypeStruct((n, levels, coarse, lanes), F32) for n in (3, 48)]
     return local_call(

time: 22.9 us -> 23.2 us (1.013)
  waiting for transfers between devices: 3.47 us -> 2.31 us
  Pallas kernels: 9.79 us -> 10.5 us
  starting transfers between devices: 8.26 us -> 8.87 us
    ppermute x1, waiting for transfers between devices: 1.11 us -> 0.01 us  [in_order(): yo_got = lax.ppermute(yo, 'gy', odd_y)]
    pallas_call x6, Pallas kernels: 9.79 us -> 10.5 us  [local_call(): pl.pallas_call(body, in_specs=specs, out_specs=[in_hbm if isinstance(o, j...]
    ppermute x1, starting transfers between devices: 0.04 us -> 0.65 us  [in_order(): so_got = lax.ppermute(so, 'gx', odd_x)]
  transfers between devices with their start and end apart: 5 -> 6, of which waited for: 2 -> 1; matrix products, arithmetic and copies ran while one was open for 0% -> 0% of each run, Pallas kernels for 17% -> 20%
where the time goes in v8:
time: 23.2 us; the launch traced here: 23 us
  Pallas kernels  10.5 us (45%)
  starting transfers between devices  8.87 us (38%)
  waiting for transfers between devices  2.31 us (10%)
  between operations  0.73 us (3%)
  local copies, waits for them, and re-layouts  0.53 us (2%)
    pallas_call x6, Pallas kernels, local_call(): pl.pallas_call(body, in_specs=specs, out_specs=[in_hbm if isinstance(o, j...  10.5 us
    ppermute x1, starting transfers between devices, in_order(): xo_got = lax.ppermute(xo, 'gx', odd_x)  3.55 us
    ppermute x1, starting transfers between devices, in_order(): yo_got = lax.ppermute(yo, 'gy', odd_y)  2.47 us
    ppermute x1, waiting for transfers between devices, in_order(): so_got = lax.ppermute(so, 'gx', odd_x)  2.3 us
    ppermute x1, starting transfers between devices, in_order(): ye_got = lax.ppermute(ye, 'gy', even_y)  1.64 us
    ppermute x1, starting transfers between devices, in_order(): so_got = lax.ppermute(so, 'gx', odd_x)  0.65 us
    ppermute x1, starting transfers between devices, in_order(): xe_got = lax.ppermute(xe, 'gx', even_x)  0.56 us
    unnamed x4, local copies, waits for them, and re-layouts  0.53 us
  transfers between devices with their start and end apart: 6, of which 1 were waited for; matrix products, arithmetic and copies ran while one was open for 0% of the time, Pallas kernels for 20%

profile of v8, /device:TPU:0, one launch (start us, length us, event | category | flops | bytes accessed | tf_op | source)
XLA Modules:
  0.0 23.0 jit_solution(4875532276614831105)
XLA Ops:
  0.6 0.0 copy-start.1
  0.6 0.0 copy-start
  0.6 2.2 %shard_map.95 = (f32[24,128]{1,0:T(8,128)S(1)}, f32[24,128]{1,0:T(8,128)S(1)}, bf16[384,256]{1,0:T(8,128)(2,1)S(1)}, bf16[384,256]{1,0:T(8,128)(2,1)S(1)}, bf16[...) custom-call(f32[8,128,512]{2,1,0:T(8,128)} %u_ref.5, ...), custom_call_target="tpu_custom_call" | custom-call | tf_op jit(solution)/shard_map/pallas_call | solution.py:469
  2.8 0.0 copy-done.1
  2.8 0.5 %copy-done = f32[8,128,512]{2,1,0:T(8,128)S(1)} copy-done((f32[8,128,512]{2,1,0:T(8,128)S(1)}, f32[8,128,512]{2,1,0:T(8,128)}, u32[]{:S(2)}) %copy-start) | copy-done | bytes 2097176
  3.4 0.6 %shard_map.97 = (f32[8,24,128]{2,1,0:T(8,128)S(1)}, f32[8,24,128]{2,1,0:T(8,128)S(1)}) custom-call(f32[8,128,512]{2,1,0:T(8,128)S(1)} %copy-done, f32[8,128,512]{2,1,0:T(8,128)S(1)} %copy-done.1, bf16[2,64,256]{2,1,0:T(8,128)(2,1)S(1)} %get-tuple-element.19.three, bf16[2,32,128]{2,1,0:T(8,128)(2,1)S(1)} %get-tuple-element.20.two, ...), custom_call_target="tpu_custom_call" | custom-call | tf_op jit(solution)/shard_map/pallas_call | solution.py:469
  4.0 0.6 %collective-permute-start = (f32[8,24,128]{2,1,0:T(8,128)S(1)}, f32[8,24,128]{2,1,0:T(8,128)S(1)}, u32[]{:S(2)}, u32[]{:S(2)}) collective-permute-start(f32[8,24,128]{2,1,0:T(8,128)S(1)} %get-tuple-element.23.xe_own), channel_id=1, source_target_pairs={{0,4},{4,0},{8,12},{12,8},{16,20},{20,16},{24,28},{28,24},{1,5},{5... | collective-permute-start | bytes 294920 | tf_op jit(solution)/shard_map/ppermute | solution.py:519
  4.5 3.5 %collective-permute-start.1 = (f32[8,24,128]{2,1,0:T(8,128)S(1)}, f32[8,24,128]{2,1,0:T(8,128)S(1)}, u32[]{:S(2)}, u32[]{:S(2)}) collective-permute-start(f32[8,24,128]{2,1,0:T(8,128)S(1)} %get-tuple-element.24.xo_own), channel_id=1, source_target_pairs={{0,28},{4,8},{8,4},{12,16},{16,12},{20,24},{24,20},{28,0},{1,29},{... | collective-permute-start | bytes 294920 | tf_op jit(solution)/shard_map/ppermute | solution.py:518
  8.1 0.0 collective-permute-start.2
  8.1 0.6 %collective-permute-start.3 = (f32[24,128]{1,0:T(8,128)S(1)}, f32[24,128]{1,0:T(8,128)S(1)}, u32[]{:S(2)}, u32[]{:S(2)}) collective-permute-start(f32[24,128]{1,0:T(8,128)S(1)} %get-tuple-element.27.own_o), channel_id=1, source_target_pairs={{0,28},{4,8},{8,4},{12,16},{16,12},{20,24},{24,20},{28,0},{1,29},{... | collective-permute-start | bytes 36872 | tf_op jit(solution)/shard_map/ppermute | solution.py:508
  8.7 1.1 %shard_map.98.s_ref = f32[160,128]{1,0:T(8,128)S(1)} custom-call(f32[8,128,512]{2,1,0:T(8,128)S(1)} %copy-done, f32[8,128,512]{2,1,0:T(8,128)S(1)} %copy-done.1, bf16[64,256]{1,0:T(8,128)(2,1)S(1)} %get-tuple-element.16.left, bf16[256,256]{1,0:T(8,128)(2,1)S(1)} %get-tuple-element.25.weights), custom_call_target="tpu_custom_call" | custom-call | tf_op jit(solution)/shard_map/pallas_call | solution.py:469
  9.8 0.0 collective-permute-done.2.got_e
  9.8 2.3 %collective-permute-done.3.got_o = f32[24,128]{1,0:T(8,128)S(1)} collective-permute-done((f32[24,128]{1,0:T(8,128)S(1)}, f32[24,128]{1,0:T(8,128)S(1)}, u32[]{:S(2)}, u32[]{:S(2)}) %collective-permute-start.3) | collective-permute-done | bytes 12320 | tf_op jit(solution)/shard_map/ppermute | solution.py:508
  12.1 0.1 shard_map.99
  12.2 1.6 %collective-permute-start.4 = (f32[56,128]{1,0:T(8,128)S(1)}, f32[56,128]{1,0:T(8,128)S(1)}, u32[]{:S(2)}, u32[]{:S(2)}) collective-permute-start(f32[56,128]{1,0:T(8,128)S(1)} %get-tuple-element.28.ye_own), channel_id=1, source_target_pairs={{0,1},{1,0},{2,3},{3,2},{4,5},{5,4},{6,7},{7,6},{8,9},{9,8},{10,11... | collective-permute-start | bytes 86024 | tf_op jit(solution)/shard_map/ppermute | solution.py:526
  13.9 2.5 %collective-permute-start.5 = (f32[56,128]{1,0:T(8,128)S(1)}, f32[56,128]{1,0:T(8,128)S(1)}, u32[]{:S(2)}, u32[]{:S(2)}) collective-permute-start(f32[56,128]{1,0:T(8,128)S(1)} %get-tuple-element.29.yo_own), channel_id=1, source_target_pairs={{0,3},{1,2},{2,1},{3,0},{4,7},{5,6},{6,5},{7,4},{8,11},{9,10},{10,... | collective-permute-start | bytes 86024 | tf_op jit(solution)/shard_map/ppermute | solution.py:525
  16.3 3.4 %shard_map.96.p_ref = f32[1280,128]{1,0:T(8,128)S(1)} custom-call(f32[8,128,512]{2,1,0:T(8,128)S(1)} %copy-done, f32[8,128,512]{2,1,0:T(8,128)S(1)} %copy-done.1, bf16[64,256]{1,0:T(8,128)(2,1)S(1)} %get-tuple-element.16.left, bf16[256,256]{1,0:T(8,128)(2,1)S(1)} %get-tuple-element.17.w_ends, bf16[256,256]{1,0:T(8,128)(2,1)S(1)} %get-tuple-element.18.w_rest), custom_call_target="tpu_custom_call" | custom-call | tf_op jit(solution)/shard_map/pallas_call | solution.py:469
  19.7 0.0 collective-permute-done.4.ye_got
  19.7 0.0 collective-permute-done.5.yo_got
  19.7 0.0 collective-permute-done.xe_got
  19.7 0.0 collective-permute-done.1.xo_got
  19.8 3.2 %shard_map.100 = (f32[3,8,32,128]{3,2,1,0:T(8,128)}, f32[48,8,32,128]{3,2,1,0:T(8,128)}) custom-call(f32[1280,128]{1,0:T(8,128)S(1)} %shard_map.96.p_ref, f32[8,24,128]{2,1,0:T(8,128)S(1)} %get-tuple-element.23.xe_own, f32[8,24,128]{2,1,0:T(8,128)S(1)} %get-tuple-element.24.xo_own, f32[8,24,128]{2,1,0:T(8,128)S(1)} %collective-permute-done.xe_got, ...), custom_call_target="tpu_custom_call" | custom-call | tf_op jit(solution)/shard_map/pallas_call | solution.py:469
Async XLA Ops:
  0.6 2.2 %copy-start.1 = (f32[8,128,512]{2,1,0:T(8,128)S(1)}, f32[8,128,512]{2,1,0:T(8,128)}, u32[]{:S(2)}) copy-start(f32[8,128,512]{2,1,0:T(8,128)} %v_ref.5) | copy-start | bytes 6291460
  0.6 2.7 %copy-start = (f32[8,128,512]{2,1,0:T(8,128)S(1)}, f32[8,128,512]{2,1,0:T(8,128)}, u32[]{:S(2)}) copy-start(f32[8,128,512]{2,1,0:T(8,128)} %u_ref.5) | copy-start | bytes 6291460
  4.0 15.8 %collective-permute-start = (f32[8,24,128]{2,1,0:T(8,128)S(1)}, f32[8,24,128]{2,1,0:T(8,128)S(1)}, u32[]{:S(2)}, u32[]{:S(2)}) collective-permute-start(f32[8,24,128]{2,1,0:T(8,128)S(1)} %get-tuple-element.23.xe_own), channel_id=1, source_target_pairs={{0,4},{4,0},{8,12},{12,8},{16,20},{20,16},{24,28},{28,24},{1,5},{5... | collective-permute-start | bytes 294920 | tf_op jit(solution)/shard_map/ppermute | solution.py:519
  4.5 15.2 %collective-permute-start.1 = (f32[8,24,128]{2,1,0:T(8,128)S(1)}, f32[8,24,128]{2,1,0:T(8,128)S(1)}, u32[]{:S(2)}, u32[]{:S(2)}) collective-permute-start(f32[8,24,128]{2,1,0:T(8,128)S(1)} %get-tuple-element.24.xo_own), channel_id=1, source_target_pairs={{0,28},{4,8},{8,4},{12,16},{16,12},{20,24},{24,20},{28,0},{1,29},{... | collective-permute-start | bytes 294920 | tf_op jit(solution)/shard_map/ppermute | solution.py:518
  8.1 1.7 %collective-permute-start.2 = (f32[24,128]{1,0:T(8,128)S(1)}, f32[24,128]{1,0:T(8,128)S(1)}, u32[]{:S(2)}, u32[]{:S(2)}) collective-permute-start(f32[24,128]{1,0:T(8,128)S(1)} %get-tuple-element.26.own_e), channel_id=1, source_target_pairs={{0,4},{4,0},{8,12},{12,8},{16,20},{20,16},{24,28},{28,24},{1,5},{5... | collective-permute-start | bytes 36872 | tf_op jit(solution)/shard_map/ppermute | solution.py:509
  8.1 4.0 %collective-permute-start.3 = (f32[24,128]{1,0:T(8,128)S(1)}, f32[24,128]{1,0:T(8,128)S(1)}, u32[]{:S(2)}, u32[]{:S(2)}) collective-permute-start(f32[24,128]{1,0:T(8,128)S(1)} %get-tuple-element.27.own_o), channel_id=1, source_target_pairs={{0,28},{4,8},{8,4},{12,16},{16,12},{20,24},{24,20},{28,0},{1,29},{... | collective-permute-start | bytes 36872 | tf_op jit(solution)/shard_map/ppermute | solution.py:508
  12.2 7.5 %collective-permute-start.4 = (f32[56,128]{1,0:T(8,128)S(1)}, f32[56,128]{1,0:T(8,128)S(1)}, u32[]{:S(2)}, u32[]{:S(2)}) collective-permute-start(f32[56,128]{1,0:T(8,128)S(1)} %get-tuple-element.28.ye_own), channel_id=1, source_target_pairs={{0,1},{1,0},{2,3},{3,2},{4,5},{5,4},{6,7},{7,6},{8,9},{9,8},{10,11... | collective-permute-start | bytes 86024 | tf_op jit(solution)/shard_map/ppermute | solution.py:526
  13.9 5.9 %collective-permute-start.5 = (f32[56,128]{1,0:T(8,128)S(1)}, f32[56,128]{1,0:T(8,128)S(1)}, u32[]{:S(2)}, u32[]{:S(2)}) collective-permute-start(f32[56,128]{1,0:T(8,128)S(1)} %get-tuple-element.29.yo_own), channel_id=1, source_target_pairs={{0,3},{1,2},{2,1},{3,0},{4,7},{5,6},{6,5},{7,4},{8,11},{9,10},{10,... | collective-permute-start | bytes 86024 | tf_op jit(solution)/shard_map/ppermute | solution.py:525

commit v9 on v8

--- a/solution.py
+++ b/solution.py
@@ -269,8 +269,9 @@
         at = slice(level * rows, (level + 1) * rows)
         x_high[at], x_low[at] = own_rows_of(left[...], u_ref[level], v_ref[level])
     weights = jnp.concatenate([w_ends[:SIDE], w_rest[...], w_ends[SIDE:]], 0)
-    for level in range(0, levels, 2):
-        at = slice(level * rows, (level + 2) * rows)
+    batch = levels // 2
+    for level in range(0, levels, batch):
+        at = slice(level * rows, (level + batch) * rows)
         p_ref[at] = column_sums(x_high[at], x_low[at], weights)
 
 
@@ -480,6 +481,7 @@
     levels, count_x, count_y = east_flow.shape
     coarse, lanes = count_x // STEP, count_y // STEP
     assert lanes == 2 * HALF and (2 * WIDE + EXT) * levels <= lanes and coarse % 16 == 0
+    assert levels % 2 == 0
     assert count_x >= 2 * EDGE and count_y > 2 * SIDE
     three, two = (jnp.asarray(c) for c in message_rows(count_x))
     w_strips, w_ends, w_rest = (jnp.asarray(c) for c in column_weights(count_y))

time: 23.2 us -> 23.2 us (level)
  no operation moved by 1% of the time
where the time goes in v9:
time: 23.2 us; the launch traced here: 23 us
  Pallas kernels  10.5 us (45%)
  starting transfers between devices  8.87 us (38%)
  waiting for transfers between devices  2.31 us (10%)
  between operations  0.73 us (3%)
  local copies, waits for them, and re-layouts  0.53 us (2%)
    pallas_call x6, Pallas kernels, local_call(): pl.pallas_call(body, in_specs=specs, out_specs=[in_hbm if isinstance(o, j...  10.5 us
    ppermute x1, starting transfers between devices, in_order(): xo_got = lax.ppermute(xo, 'gx', odd_x)  3.55 us
    ppermute x1, starting transfers between devices, in_order(): yo_got = lax.ppermute(yo, 'gy', odd_y)  2.47 us
    ppermute x1, waiting for transfers between devices, in_order(): so_got = lax.ppermute(so, 'gx', odd_x)  2.3 us
    ppermute x1, starting transfers between devices, in_order(): ye_got = lax.ppermute(ye, 'gy', even_y)  1.64 us
    ppermute x1, starting transfers between devices, in_order(): so_got = lax.ppermute(so, 'gx', odd_x)  0.65 us
    ppermute x1, starting transfers between devices, in_order(): xe_got = lax.ppermute(xe, 'gx', even_x)  0.56 us
    unnamed x4, local copies, waits for them, and re-layouts  0.53 us
  transfers between devices with their start and end apart: 6, of which 1 were waited for; matrix products, arithmetic and copies ran while one was open for 0% of the time, Pallas kernels for 20%

profile of v9, /device:TPU:0, one launch (start us, length us, event | category | flops | bytes accessed | tf_op | source)
XLA Modules:
  0.0 23.0 jit_solution(7067058778129398109)
XLA Ops:
  0.6 0.0 copy-start.1
  0.6 0.0 copy-start
  0.6 2.2 %shard_map.95 = (f32[24,128]{1,0:T(8,128)S(1)}, f32[24,128]{1,0:T(8,128)S(1)}, bf16[384,256]{1,0:T(8,128)(2,1)S(1)}, bf16[384,256]{1,0:T(8,128)(2,1)S(1)}, bf16[...) custom-call(f32[8,128,512]{2,1,0:T(8,128)} %u_ref.5, ...), custom_call_target="tpu_custom_call" | custom-call | tf_op jit(solution)/shard_map/pallas_call | solution.py:470
  2.8 0.0 copy-done.1
  2.8 0.5 %copy-done = f32[8,128,512]{2,1,0:T(8,128)S(1)} copy-done((f32[8,128,512]{2,1,0:T(8,128)S(1)}, f32[8,128,512]{2,1,0:T(8,128)}, u32[]{:S(2)}) %copy-start) | copy-done | bytes 2097176
  3.4 0.6 %shard_map.97 = (f32[8,24,128]{2,1,0:T(8,128)S(1)}, f32[8,24,128]{2,1,0:T(8,128)S(1)}) custom-call(f32[8,128,512]{2,1,0:T(8,128)S(1)} %copy-done, f32[8,128,512]{2,1,0:T(8,128)S(1)} %copy-done.1, bf16[2,64,256]{2,1,0:T(8,128)(2,1)S(1)} %get-tuple-element.19.three, bf16[2,32,128]{2,1,0:T(8,128)(2,1)S(1)} %get-tuple-element.20.two, ...), custom_call_target="tpu_custom_call" | custom-call | tf_op jit(solution)/shard_map/pallas_call | solution.py:470
  4.0 0.6 %collective-permute-start = (f32[8,24,128]{2,1,0:T(8,128)S(1)}, f32[8,24,128]{2,1,0:T(8,128)S(1)}, u32[]{:S(2)}, u32[]{:S(2)}) collective-permute-start(f32[8,24,128]{2,1,0:T(8,128)S(1)} %get-tuple-element.23.xe_own), channel_id=1, source_target_pairs={{0,4},{4,0},{8,12},{12,8},{16,20},{20,16},{24,28},{28,24},{1,5},{5... | collective-permute-start | bytes 294920 | tf_op jit(solution)/shard_map/ppermute | solution.py:521
  4.5 3.5 %collective-permute-start.1 = (f32[8,24,128]{2,1,0:T(8,128)S(1)}, f32[8,24,128]{2,1,0:T(8,128)S(1)}, u32[]{:S(2)}, u32[]{:S(2)}) collective-permute-start(f32[8,24,128]{2,1,0:T(8,128)S(1)} %get-tuple-element.24.xo_own), channel_id=1, source_target_pairs={{0,28},{4,8},{8,4},{12,16},{16,12},{20,24},{24,20},{28,0},{1,29},{... | collective-permute-start | bytes 294920 | tf_op jit(solution)/shard_map/ppermute | solution.py:520
  8.1 0.0 collective-permute-start.2
  8.1 0.6 %collective-permute-start.3 = (f32[24,128]{1,0:T(8,128)S(1)}, f32[24,128]{1,0:T(8,128)S(1)}, u32[]{:S(2)}, u32[]{:S(2)}) collective-permute-start(f32[24,128]{1,0:T(8,128)S(1)} %get-tuple-element.27.own_o), channel_id=1, source_target_pairs={{0,28},{4,8},{8,4},{12,16},{16,12},{20,24},{24,20},{28,0},{1,29},{... | collective-permute-start | bytes 36872 | tf_op jit(solution)/shard_map/ppermute | solution.py:510
  8.7 1.1 %shard_map.98.s_ref = f32[160,128]{1,0:T(8,128)S(1)} custom-call(f32[8,128,512]{2,1,0:T(8,128)S(1)} %copy-done, f32[8,128,512]{2,1,0:T(8,128)S(1)} %copy-done.1, bf16[64,256]{1,0:T(8,128)(2,1)S(1)} %get-tuple-element.16.left, bf16[256,256]{1,0:T(8,128)(2,1)S(1)} %get-tuple-element.25.weights), custom_call_target="tpu_custom_call" | custom-call | tf_op jit(solution)/shard_map/pallas_call | solution.py:470
  9.8 0.0 collective-permute-done.2.got_e
  9.8 2.3 %collective-permute-done.3.got_o = f32[24,128]{1,0:T(8,128)S(1)} collective-permute-done((f32[24,128]{1,0:T(8,128)S(1)}, f32[24,128]{1,0:T(8,128)S(1)}, u32[]{:S(2)}, u32[]{:S(2)}) %collective-permute-start.3) | collective-permute-done | bytes 12320 | tf_op jit(solution)/shard_map/ppermute | solution.py:510
  12.1 0.1 shard_map.99
  12.2 1.6 %collective-permute-start.4 = (f32[56,128]{1,0:T(8,128)S(1)}, f32[56,128]{1,0:T(8,128)S(1)}, u32[]{:S(2)}, u32[]{:S(2)}) collective-permute-start(f32[56,128]{1,0:T(8,128)S(1)} %get-tuple-element.28.ye_own), channel_id=1, source_target_pairs={{0,1},{1,0},{2,3},{3,2},{4,5},{5,4},{6,7},{7,6},{8,9},{9,8},{10,11... | collective-permute-start | bytes 86024 | tf_op jit(solution)/shard_map/ppermute | solution.py:528
  13.9 2.5 %collective-permute-start.5 = (f32[56,128]{1,0:T(8,128)S(1)}, f32[56,128]{1,0:T(8,128)S(1)}, u32[]{:S(2)}, u32[]{:S(2)}) collective-permute-start(f32[56,128]{1,0:T(8,128)S(1)} %get-tuple-element.29.yo_own), channel_id=1, source_target_pairs={{0,3},{1,2},{2,1},{3,0},{4,7},{5,6},{6,5},{7,4},{8,11},{9,10},{10,... | collective-permute-start | bytes 86024 | tf_op jit(solution)/shard_map/ppermute | solution.py:527
  16.3 3.4 %shard_map.96.p_ref = f32[1280,128]{1,0:T(8,128)S(1)} custom-call(f32[8,128,512]{2,1,0:T(8,128)S(1)} %copy-done, f32[8,128,512]{2,1,0:T(8,128)S(1)} %copy-done.1, bf16[64,256]{1,0:T(8,128)(2,1)S(1)} %get-tuple-element.16.left, bf16[256,256]{1,0:T(8,128)(2,1)S(1)} %get-tuple-element.17.w_ends, bf16[256,256]{1,0:T(8,128)(2,1)S(1)} %get-tuple-element.18.w_rest), custom_call_target="tpu_custom_call" | custom-call | tf_op jit(solution)/shard_map/pallas_call | solution.py:470
  19.7 0.0 collective-permute-done.4.ye_got
  19.7 0.0 collective-permute-done.5.yo_got
  19.7 0.0 collective-permute-done.xe_got
  19.7 0.0 collective-permute-done.1.xo_got
  19.8 3.2 %shard_map.100 = (f32[3,8,32,128]{3,2,1,0:T(8,128)}, f32[48,8,32,128]{3,2,1,0:T(8,128)}) custom-call(f32[1280,128]{1,0:T(8,128)S(1)} %shard_map.96.p_ref, f32[8,24,128]{2,1,0:T(8,128)S(1)} %get-tuple-element.23.xe_own, f32[8,24,128]{2,1,0:T(8,128)S(1)} %get-tuple-element.24.xo_own, f32[8,24,128]{2,1,0:T(8,128)S(1)} %collective-permute-done.xe_got, ...), custom_call_target="tpu_custom_call" | custom-call | tf_op jit(solution)/shard_map/pallas_call | solution.py:470
Async XLA Ops:
  0.6 2.2 %copy-start.1 = (f32[8,128,512]{2,1,0:T(8,128)S(1)}, f32[8,128,512]{2,1,0:T(8,128)}, u32[]{:S(2)}) copy-start(f32[8,128,512]{2,1,0:T(8,128)} %v_ref.5) | copy-start | bytes 6291460
  0.6 2.7 %copy-start = (f32[8,128,512]{2,1,0:T(8,128)S(1)}, f32[8,128,512]{2,1,0:T(8,128)}, u32[]{:S(2)}) copy-start(f32[8,128,512]{2,1,0:T(8,128)} %u_ref.5) | copy-start | bytes 6291460
  4.0 15.8 %collective-permute-start = (f32[8,24,128]{2,1,0:T(8,128)S(1)}, f32[8,24,128]{2,1,0:T(8,128)S(1)}, u32[]{:S(2)}, u32[]{:S(2)}) collective-permute-start(f32[8,24,128]{2,1,0:T(8,128)S(1)} %get-tuple-element.23.xe_own), channel_id=1, source_target_pairs={{0,4},{4,0},{8,12},{12,8},{16,20},{20,16},{24,28},{28,24},{1,5},{5... | collective-permute-start | bytes 294920 | tf_op jit(solution)/shard_map/ppermute | solution.py:521
  4.5 15.2 %collective-permute-start.1 = (f32[8,24,128]{2,1,0:T(8,128)S(1)}, f32[8,24,128]{2,1,0:T(8,128)S(1)}, u32[]{:S(2)}, u32[]{:S(2)}) collective-permute-start(f32[8,24,128]{2,1,0:T(8,128)S(1)} %get-tuple-element.24.xo_own), channel_id=1, source_target_pairs={{0,28},{4,8},{8,4},{12,16},{16,12},{20,24},{24,20},{28,0},{1,29},{... | collective-permute-start | bytes 294920 | tf_op jit(solution)/shard_map/ppermute | solution.py:520
  8.1 1.7 %collective-permute-start.2 = (f32[24,128]{1,0:T(8,128)S(1)}, f32[24,128]{1,0:T(8,128)S(1)}, u32[]{:S(2)}, u32[]{:S(2)}) collective-permute-start(f32[24,128]{1,0:T(8,128)S(1)} %get-tuple-element.26.own_e), channel_id=1, source_target_pairs={{0,4},{4,0},{8,12},{12,8},{16,20},{20,16},{24,28},{28,24},{1,5},{5... | collective-permute-start | bytes 36872 | tf_op jit(solution)/shard_map/ppermute | solution.py:511
  8.1 4.0 %collective-permute-start.3 = (f32[24,128]{1,0:T(8,128)S(1)}, f32[24,128]{1,0:T(8,128)S(1)}, u32[]{:S(2)}, u32[]{:S(2)}) collective-permute-start(f32[24,128]{1,0:T(8,128)S(1)} %get-tuple-element.27.own_o), channel_id=1, source_target_pairs={{0,28},{4,8},{8,4},{12,16},{16,12},{20,24},{24,20},{28,0},{1,29},{... | collective-permute-start | bytes 36872 | tf_op jit(solution)/shard_map/ppermute | solution.py:510
  12.2 7.5 %collective-permute-start.4 = (f32[56,128]{1,0:T(8,128)S(1)}, f32[56,128]{1,0:T(8,128)S(1)}, u32[]{:S(2)}, u32[]{:S(2)}) collective-permute-start(f32[56,128]{1,0:T(8,128)S(1)} %get-tuple-element.28.ye_own), channel_id=1, source_target_pairs={{0,1},{1,0},{2,3},{3,2},{4,5},{5,4},{6,7},{7,6},{8,9},{9,8},{10,11... | collective-permute-start | bytes 86024 | tf_op jit(solution)/shard_map/ppermute | solution.py:528
  13.9 5.9 %collective-permute-start.5 = (f32[56,128]{1,0:T(8,128)S(1)}, f32[56,128]{1,0:T(8,128)S(1)}, u32[]{:S(2)}, u32[]{:S(2)}) collective-permute-start(f32[56,128]{1,0:T(8,128)S(1)} %get-tuple-element.29.yo_own), channel_id=1, source_target_pairs={{0,3},{1,2},{2,1},{3,0},{4,7},{5,6},{6,5},{7,4},{8,11},{9,10},{10,... | collective-permute-start | bytes 86024 | tf_op jit(solution)/shard_map/ppermute | solution.py:527
